TPU v7x, 32 devices: a whole 2x2x4 slice. The times are simulated.
32 devices in a mesh: dp: 8 (over z, x), tensor: 4 (over y, core).
Axes of the slice: x: 2, y: 2, z: 4, core: 2. Of those that a mesh axis runs over, the one named last changes fastest.
Arguments:
- tokens: bfloat16 [25088, 768], P(('dp', 'tensor')), may hold values from -6 to 6
- cotangent: bfloat16 [25088, 768], P(('dp', 'tensor')), may hold values from -6 to 6
- block_patches: int32 [32], P('dp'), may hold values from 196 to 784, as said below
- qkv_weight: bfloat16 [3, 768, 768], P(None, 'dp', 'tensor'), may hold values from -0.21875 to 0.21875
- out_weight: bfloat16 [768, 768], P('tensor', 'dp'), may hold values from -0.875 to 0.875
- up_weight: bfloat16 [768, 3072], P('dp', 'tensor'), may hold values from -0.21875 to 0.21875
- down_weight: bfloat16 [3072, 768], P('tensor', 'dp'), may hold values from -0.109375 to 0.109375
- vectors: float32 [9216], replicated, may hold values from -0.7 to 1.7, as said below
- momentum: float32 [1], replicated, may hold values from 0.4 to 0.7
- target_qkv: float32 [3, 768, 768], P(None, 'dp', 'tensor'), may hold values from -0.21875 to 0.21875
- target_out: float32 [768, 768], P('tensor', 'dp'), may hold values from -0.875 to 0.875
- target_up: float32 [768, 3072], P('dp', 'tensor'), may hold values from -0.21875 to 0.21875
- target_down: float32 [3072, 768], P('tensor', 'dp'), may hold values from -0.109375 to 0.109375
- target_vectors: float32 [9216], replicated, may hold values from -0.7 to 1.7, as said below
Outputs:
- output: bfloat16 [25088, 768], P(('dp', 'tensor'))
- grad_tokens: bfloat16 [25088, 768], P(('dp', 'tensor'))
- grad_qkv: float32 [3, 768, 768], P(None, 'dp', 'tensor')
- grad_out: float32 [768, 768], P('tensor', 'dp')
- grad_up: float32 [768, 3072], P('dp', 'tensor')
- grad_down: float32 [3072, 768], P('tensor', 'dp')
- grad_vectors: float32 [9216], replicated
- next_qkv: float32 [3, 768, 768], P(None, 'dp', 'tensor')
- next_out: float32 [768, 768], P('tensor', 'dp')
- next_up: float32 [768, 3072], P('dp', 'tensor')
- next_down: float32 [3072, 768], P('tensor', 'dp')
- next_vectors: float32 [9216], replicated
Inputs may be any that keep to these rules, and one draw needn't show every extreme that they name: `block_patches`: each block of 784 rows holds either one image of 784 patches (entry 784) or four images of 196 patches, one after another (entry 196); both kinds occur in every draw. `vectors`: the gains (the first and third pieces of 768) lie between 0.3 and 1.7. `target_vectors`: laid out as vectors, with gains between 0.3 and 1.7.
All inputs are finite; a program needn't handle non-finite values.
Results may differ from a plain program's by a relative error of at most 0.012.
Values may be sent and summed in bfloat16 or wider, within the bound.
A program may use at most 192 MiB of HBM per device.

v0:
```python
import jax
import jax.numpy as jnp
from jax import lax
from jax.sharding import PartitionSpec as P

D = 768
HD = 64
FF = 3072
PB = 784


def unpack(vectors):
    return (
        vectors[0:D],
        vectors[D : 2 * D],
        vectors[2 * D : 3 * D],
        vectors[3 * D : 4 * D],
        vectors[4 * D : 5 * D],
        vectors[5 * D : 6 * D],
        vectors[6 * D : 7 * D],
        vectors[7 * D : 7 * D + FF],
        vectors[7 * D + FF : 8 * D + FF],
    )


def layer_norm_parts(values, gain, bias):
    middle = jnp.mean(values, axis=-1, keepdims=True)
    centred = values - middle
    inverse = lax.rsqrt(jnp.mean(centred * centred, axis=-1, keepdims=True) + 1e-06)
    scaled = centred * inverse
    return (scaled * gain + bias, scaled, inverse)


def norm_backward(grad_normed, scaled, inverse, gain):
    weighted = grad_normed * gain
    return inverse * (
        weighted
        - jnp.mean(weighted, axis=-1, keepdims=True)
        - scaled * jnp.mean(weighted * scaled, axis=-1, keepdims=True)
    )


def gelu_exact(values):
    return jax.nn.gelu(values, approximate=False)


def softmax_rows(query, key, value):
    factor = query.shape[-1] ** (-0.5)
    scores = jnp.einsum("qhd,khd->hqk", query, key, preferred_element_type=jnp.float32) * factor
    highest = jnp.max(scores, axis=-1, keepdims=True)
    raised = jnp.exp(scores - highest)
    total = jnp.sum(raised, axis=-1, keepdims=True)
    softened = (raised / total).astype(jnp.bfloat16)
    result = jnp.einsum("hqk,khd->qhd", softened, value, preferred_element_type=jnp.float32)
    return (result.astype(jnp.bfloat16), (highest + jnp.log(total))[..., 0])


def softmax_grads(query, key, value, grad_result, log_total):
    factor = query.shape[-1] ** (-0.5)
    scores = jnp.einsum("qhd,khd->hqk", query, key, preferred_element_type=jnp.float32) * factor
    softened = jnp.exp(scores - log_total[..., None])
    grad_value = jnp.einsum(
        "hqk,qhd->khd",
        softened.astype(jnp.bfloat16),
        grad_result,
        preferred_element_type=jnp.float32,
    )
    grad_soft = jnp.einsum("qhd,khd->hqk", grad_result, value, preferred_element_type=jnp.float32)
    grad_scores = (
        softened * (grad_soft - jnp.sum(softened * grad_soft, axis=-1, keepdims=True))
    ).astype(jnp.bfloat16)
    grad_query = (
        jnp.einsum("hqk,khd->qhd", grad_scores, key, preferred_element_type=jnp.float32) * factor
    )
    grad_key = (
        jnp.einsum("hqk,qhd->khd", grad_scores, query, preferred_element_type=jnp.float32) * factor
    )
    return (
        grad_query.astype(jnp.bfloat16),
        grad_key.astype(jnp.bfloat16),
        grad_value.astype(jnp.bfloat16),
    )


def forward_block(items):
    query, key, value, patches = items
    length = query.shape[0]

    def forward_whole(parts):
        return softmax_rows(*parts)

    def forward_split(parts):
        pieces = tuple((array.reshape((4, length // 4) + array.shape[1:]) for array in parts))
        result, log_total = jax.vmap(softmax_rows)(*pieces)
        return (
            result.reshape(query.shape),
            jnp.transpose(log_total, (1, 0, 2)).reshape(query.shape[1], length),
        )

    return lax.cond(patches == length, forward_whole, forward_split, (query, key, value))


def backward_block(items):
    query, key, value, grad_result, log_total, patches = items
    length = query.shape[0]

    def backward_whole(parts):
        return softmax_grads(*parts)

    def backward_split(parts):
        pieces = tuple((array.reshape((4, length // 4) + array.shape[1:]) for array in parts[:4]))
        totals = jnp.transpose(parts[4].reshape(query.shape[1], 4, length // 4), (1, 0, 2))
        results = jax.vmap(softmax_grads)(*pieces, totals)
        return tuple((array.reshape(query.shape) for array in results))

    return lax.cond(
        patches == length,
        backward_whole,
        backward_split,
        (query, key, value, grad_result, log_total),
    )


def as_blocks(array, heads):
    return array.reshape(array.shape[0] // PB, PB, heads, array.shape[1] // heads)


def gather_weights(shards):
    gathered = (
        lax.all_gather(shards[0], "dp", axis=1, tiled=True),
        lax.all_gather(shards[1], "dp", axis=1, tiled=True),
        lax.all_gather(shards[2], "dp", axis=0, tiled=True),
        lax.all_gather(shards[3], "dp", axis=1, tiled=True),
    )
    return gathered


def forward_pass(tokens, block_patches, weights, vectors):
    qkv_full, out_full, up_full, down_full = weights
    gain1, bias1, gain2, bias2, bias_query, bias_value, bias_out, bias_up, bias_down = unpack(
        vectors
    )
    place = lax.axis_index("tensor")
    head_width = qkv_full.shape[2]
    unit_width = up_full.shape[1]
    heads = head_width // HD
    inputs = tokens.astype(jnp.float32)
    normed1, scaled1, inverse1 = layer_norm_parts(inputs, gain1, bias1)
    normed1_all = normed1.astype(jnp.bfloat16)
    normed1_all = lax.all_gather(normed1_all, "tensor", axis=0, tiled=True)
    mixed = jnp.einsum("td,cde->cte", normed1_all, qkv_full, preferred_element_type=jnp.float32)
    query = (
        mixed[0] + lax.dynamic_slice_in_dim(bias_query, place * head_width, head_width)
    ).astype(jnp.bfloat16)
    key = mixed[1].astype(jnp.bfloat16)
    value = (
        mixed[2] + lax.dynamic_slice_in_dim(bias_value, place * head_width, head_width)
    ).astype(jnp.bfloat16)
    group_rows = mixed.shape[1]
    attended, log_totals = lax.map(
        forward_block,
        (as_blocks(query, heads), as_blocks(key, heads), as_blocks(value, heads), block_patches),
    )
    attended = attended.reshape(group_rows, head_width)
    branch = lax.psum_scatter(
        jnp.dot(attended, out_full, preferred_element_type=jnp.float32),
        "tensor",
        scatter_dimension=0,
        tiled=True,
    )
    residual = inputs + branch + bias_out
    normed2, scaled2, inverse2 = layer_norm_parts(residual, gain2, bias2)
    normed2_all = normed2.astype(jnp.bfloat16)
    normed2_all = lax.all_gather(normed2_all, "tensor", axis=0, tiled=True)
    pre_active = jnp.dot(
        normed2_all, up_full, preferred_element_type=jnp.float32
    ) + lax.dynamic_slice_in_dim(bias_up, place * unit_width, unit_width)
    active = gelu_exact(pre_active).astype(jnp.bfloat16)
    second = lax.psum_scatter(
        jnp.dot(active, down_full, preferred_element_type=jnp.float32).astype(jnp.bfloat16),
        "tensor",
        scatter_dimension=0,
        tiled=True,
    ).astype(jnp.float32)
    result = residual + second + bias_down
    return (
        scaled1,
        inverse1,
        normed1_all,
        query,
        key,
        value,
        log_totals,
        attended,
        scaled2,
        inverse2,
        normed2_all,
        pre_active,
        active,
        result,
    )


def backward_pass(cotangent, block_patches, weights, vectors, state):
    qkv_full, out_full, up_full, down_full = weights
    gain1, bias1, gain2, bias2, bias_query, bias_value, bias_out, bias_up, bias_down = unpack(
        vectors
    )
    (
        scaled1,
        inverse1,
        normed1_all,
        query,
        key,
        value,
        log_totals,
        attended,
        scaled2,
        inverse2,
        normed2_all,
        pre_active,
        active,
        result,
    ) = state
    place = lax.axis_index("tensor")
    head_width = qkv_full.shape[2]
    unit_width = up_full.shape[1]
    heads = head_width // HD
    group_rows = query.shape[0]
    grad_result = cotangent.astype(jnp.float32)
    grad_result_all = lax.all_gather(cotangent, "tensor", axis=0, tiled=True)
    grad_down = jnp.einsum("tf,td->fd", active, grad_result_all, preferred_element_type=jnp.float32)
    grad_active = jnp.einsum(
        "td,fd->tf", grad_result_all, down_full, preferred_element_type=jnp.float32
    )
    _, gelu_pull = jax.vjp(gelu_exact, pre_active)
    grad_pre = gelu_pull(grad_active)[0].astype(jnp.bfloat16)
    grad_up = jnp.einsum("td,tf->df", normed2_all, grad_pre, preferred_element_type=jnp.float32)
    grad_normed2 = lax.psum_scatter(
        jnp.einsum("tf,df->td", grad_pre, up_full, preferred_element_type=jnp.float32),
        "tensor",
        scatter_dimension=0,
        tiled=True,
    )
    grad_residual = grad_result + norm_backward(grad_normed2, scaled2, inverse2, gain2)
    grad_branch_all = grad_residual.astype(jnp.bfloat16)
    grad_branch_all = lax.all_gather(grad_branch_all, "tensor", axis=0, tiled=True)
    grad_out = jnp.einsum(
        "te,td->ed", attended, grad_branch_all, preferred_element_type=jnp.float32
    )
    grad_attended = jnp.einsum(
        "td,ed->te", grad_branch_all, out_full, preferred_element_type=jnp.float32
    ).astype(jnp.bfloat16)
    grad_query, grad_key, grad_value = lax.map(
        backward_block,
        (
            as_blocks(query, heads),
            as_blocks(key, heads),
            as_blocks(value, heads),
            as_blocks(grad_attended, heads),
            log_totals,
            block_patches,
        ),
    )
    grad_mixed = jnp.stack(
        [
            grad_query.reshape(group_rows, head_width),
            grad_key.reshape(group_rows, head_width),
            grad_value.reshape(group_rows, head_width),
        ]
    )
    grad_qkv = jnp.einsum(
        "td,cte->cde", normed1_all, grad_mixed, preferred_element_type=jnp.float32
    )
    grad_normed1 = lax.psum_scatter(
        jnp.einsum("cte,cde->td", grad_mixed, qkv_full, preferred_element_type=jnp.float32),
        "tensor",
        scatter_dimension=0,
        tiled=True,
    )
    grad_tokens = (grad_residual + norm_backward(grad_normed1, scaled1, inverse1, gain1)).astype(
        jnp.bfloat16
    )
    empty_width = jnp.zeros((D,), jnp.float32)
    column_sums = jnp.sum(grad_mixed.astype(jnp.float32), axis=1)
    query_sums = lax.dynamic_update_slice_in_dim(empty_width, column_sums[0], place * head_width, 0)
    value_sums = lax.dynamic_update_slice_in_dim(empty_width, column_sums[2], place * head_width, 0)
    unit_sums = lax.dynamic_update_slice_in_dim(
        jnp.zeros((FF,), jnp.float32),
        jnp.sum(grad_pre.astype(jnp.float32), axis=0),
        place * unit_width,
        0,
    )
    gradient_vector = jnp.concatenate(
        [
            jnp.sum(grad_normed1 * scaled1, axis=0),
            jnp.sum(grad_normed1, axis=0),
            jnp.sum(grad_normed2 * scaled2, axis=0),
            jnp.sum(grad_normed2, axis=0),
            query_sums,
            value_sums,
            jnp.sum(grad_residual, axis=0),
            unit_sums,
            jnp.sum(grad_result, axis=0),
        ]
    )
    gradient_vector = lax.psum(gradient_vector, ("dp", "tensor"))
    matrices = (grad_qkv, grad_out, grad_up, grad_down)
    matrices = (
        lax.psum_scatter(matrices[0], "dp", scatter_dimension=1, tiled=True),
        lax.psum_scatter(matrices[1], "dp", scatter_dimension=1, tiled=True),
        lax.psum_scatter(matrices[2], "dp", scatter_dimension=0, tiled=True),
        lax.psum_scatter(matrices[3], "dp", scatter_dimension=1, tiled=True),
    )
    return (grad_tokens, matrices, gradient_vector)


def body(
    tokens,
    cotangent,
    block_patches,
    qkv_weight,
    out_weight,
    up_weight,
    down_weight,
    vectors,
    momentum,
    target_qkv,
    target_out,
    target_up,
    target_down,
    target_vectors,
):
    shards = (qkv_weight, out_weight, up_weight, down_weight)
    weights = gather_weights(shards)
    state = forward_pass(tokens, block_patches, weights, vectors)
    result = state[-1]
    fenced = lax.optimization_barrier((shards, result))
    weights = gather_weights(fenced[0])
    fenced_again = lax.optimization_barrier((tokens, weights, result))
    state = forward_pass(fenced_again[0], block_patches, fenced_again[1], vectors)
    grad_tokens, matrices, gradient_vector = backward_pass(
        cotangent, block_patches, weights, vectors, state
    )
    rate = momentum[0]

    def average(target, online):
        return rate * target + (1.0 - rate) * online.astype(jnp.float32)

    return (
        result.astype(jnp.bfloat16),
        grad_tokens,
        matrices[0],
        matrices[1],
        matrices[2],
        matrices[3],
        gradient_vector,
        average(target_qkv, qkv_weight),
        average(target_out, out_weight),
        average(target_up, up_weight),
        average(target_down, down_weight),
        average(target_vectors, vectors),
    )


def solution(mesh):
    placed = (
        P(("dp", "tensor"), None),
        P(("dp", "tensor"), None),
        P("dp"),
        P(None, "dp", "tensor"),
        P("tensor", "dp"),
        P("dp", "tensor"),
        P("tensor", "dp"),
        P(),
        P(),
        P(None, "dp", "tensor"),
        P("tensor", "dp"),
        P("dp", "tensor"),
        P("tensor", "dp"),
        P(),
    )
    return jax.shard_map(
        body,
        mesh=mesh,
        in_specs=placed,
        out_specs=(
            P(("dp", "tensor"), None),
            P(("dp", "tensor"), None),
            P(None, "dp", "tensor"),
            P("tensor", "dp"),
            P("dp", "tensor"),
            P("tensor", "dp"),
            P(),
            P(None, "dp", "tensor"),
            P("tensor", "dp"),
            P("dp", "tensor"),
            P("tensor", "dp"),
            P(),
        ),
        check_vma=False,
    )
```

profile of v0, /device:TPU:0, one launch (start us, length us, event | category | flops | bytes accessed | tf_op | source)
XLA Modules:
  0.0 1344.8 jit_solution(16622954526668428863)
XLA Ops:
  15.2 38.8 %all_gather.43 = bf16[3,768,192]{2,0,1:T(4,128)(2,1)S(1)} all-gather(bf16[3,96,192]{2,0,1:T(4,128)(2,1)S(1)} %copy.187), channel_id=1, replica_groups=mesh['dp'=8,'tensor'=4] {'dp'}, dimensions={1}, use_global_device_ids=true | all-gather | bytes 995328 | tf_op jit(solution)/shard_map/all_gather | solution.py:130
  56.1 33.1 %all_gather.44 = bf16[192,768]{0,1:T(8,128)(2,1)} all-gather(bf16[192,96]{0,1:T(8,128)(2,1)S(1)} %copy.193), channel_id=1, replica_groups=mesh['dp'=8,'tensor'=4] {'dp'}, dimensions={1}, use_global_device_ids=true | all-gather | bytes 331776 | tf_op jit(solution)/shard_map/all_gather | solution.py:131
  118.7 52.0 %while.36 = (s32[]{:T(128)}, bf16[4,784,3,64]{1,3,2,0:T(8,128)(2,1)}, s32[4]{0:T(128)S(1)}, bf16[4,784,3,64]{1,3,2,0:T(8,128)(2,1)}, bf16[4,784,3,64]{1,3,2,0:T(...) while((s32[]{:T(128)}, bf16[4,784,3,64]{1,3,2,0:T(8,128)(2,1)}, s32[4]{0:T(128)S(1)}, ...), condition=%wide.region_9.10_spmd, body=%wide.region_2.9_spmd.sunk | while | flops 481426944 | bytes 18426404 | solution.py:160
  122.1 10.3 conditional.6
  148.1 10.3 conditional.6
  174.2 13.5 %reshape.230 = bf16[3136,192]{0,1:T(8,128)(2,1)S(1)} reshape(bf16[4,784,3,64]{1,0,3,2:T(4,128)(2,1)} %copy.192) | data formatting | bytes 2408448 | tf_op jit(solution)/shard_map/reshape | solution.py:164
  194.2 79.0 %reduce-scatter.14.cloned.1.call-done = f32[784,768]{1,0:T(8,128)} async-done(((f32[3136,768]{1,0:T(8,128)}), f32[784,768]{1,0:T(8,128)}) %reduce-scatter.14.cloned.1.call-update) | async-done | bytes 2408464 | tf_op jit(solution)/shard_map/reduce_scatter | solution.py:165
  279.7 38.4 %all-gather.13.cloned.1.call-done = bf16[3136,768]{1,0:T(8,128)(2,1)} async-done(((bf16[784,768]{1,0:T(8,128)(2,1)}), bf16[3136,768]{1,0:T(8,128)(2,1)}) %all-gather.13.cloned.1.call-update) | async-done | bytes 4816912 | tf_op jit(solution)/shard_map/all_gather | solution.py:174
  318.1 30.8 %convolution_convert_fusion.3 = bf16[3136,768]{1,0:T(8,128)(2,1)} fusion(bf16[768,768]{0,1:T(8,128)(2,1)} %all-gather.17.cloned.1.call-done, bf16[3136,768]{1,0:T(8,128)(2,1)} %all-gather.13.cloned.1.call-done, bf16[768,768]{1,0:T(8,128)(2,1)} %all-gather.15.cloned.1.call-done, f32[768]{0:T(1024)S(1)} %dynamic_slice.59), kind=kOutput, calls=%fused_computation.139 | convolution fusion | flops 7560118272 | bytes 11996160 | tf_op jit(solution)/shard_map/dot_general | solution.py:180
  348.9 48.4 %reduce-scatter.16.cloned.1.call-done = bf16[784,768]{1,0:T(8,128)(2,1)} async-done(((bf16[3136,768]{1,0:T(8,128)(2,1)}), bf16[784,768]{1,0:T(8,128)(2,1)}) %reduce-scatter.16.cloned.1.call-update) | async-done | bytes 1204240 | tf_op jit(solution)/shard_map/reduce_scatter | solution.py:179
  401.9 34.1 %all_gather.49 = bf16[192,768]{0,1:T(8,128)(2,1)} all-gather(bf16[192,96]{0,1:T(8,128)(2,1)S(1)} %copy.194), channel_id=1, replica_groups=mesh['dp'=8,'tensor'=4] {'dp'}, dimensions={1}, use_global_device_ids=true | all-gather | bytes 331776 | tf_op jit(solution)/shard_map/all_gather | solution.py:131
  435.9 34.5 %all_gather.48 = bf16[3,768,192]{2,1,0:T(8,128)(2,1)S(1)} all-gather(bf16[3,96,192]{2,1,0:T(8,128)(2,1)S(1)} %copy-done.23), channel_id=1, replica_groups=mesh['dp'=8,'tensor'=4] {'dp'}, dimensions={1}, use_global_device_ids=true | all-gather | bytes 995328 | tf_op jit(solution)/shard_map/all_gather | solution.py:130
  470.5 22.4 %all-gather.21.cloned.1.call-done = bf16[768,768]{0,1:T(8,128)(2,1)} async-done(((bf16[768,96]{0,1:T(8,128)(2,1)}), bf16[768,768]{0,1:T(8,128)(2,1)}) %all-gather.21.cloned.1.call-update) | async-done | bytes 1179664 | tf_op jit(solution)/shard_map/all_gather | solution.py:133
  495.6 36.2 %all-gather.23.cloned.1.call-done = bf16[3136,768]{1,0:T(8,128)(2,1)} async-done(((bf16[784,768]{1,0:T(8,128)(2,1)}), bf16[3136,768]{1,0:T(8,128)(2,1)}) %all-gather.23.cloned.1.call-update) | async-done | bytes 4816912 | tf_op jit(solution)/shard_map/all_gather | solution.py:150
  563.4 41.2 %while.37 = (s32[]{:T(128)}, bf16[4,784,3,64]{1,3,2,0:T(8,128)(2,1)}, f32[4,3,784]{2,1,0:T(4,128)}, s32[4]{0:T(128)S(1)}, bf16[4,784,3,64]{1,3,2,0:T(8,128)(2,1)...) while((s32[]{:T(128)}, ...), condition=%wide.region_23.24_spmd, body=%wide.region_16.23_spmd.sunk | while | flops 488799680 | bytes 25882488 | solution.py:160
  616.4 79.9 %reduce-scatter.18.cloned.1.call-done = f32[784,768]{1,0:T(8,128)} async-done(((f32[3136,768]{1,0:T(8,128)}), f32[784,768]{1,0:T(8,128)}) %reduce-scatter.18.cloned.1.call-update) | async-done | bytes 2408464 | tf_op jit(solution)/shard_map/reduce_scatter | solution.py:165
  702.0 37.3 %all-gather.25.cloned.1.call-done = bf16[3136,768]{1,0:T(8,128)(2,1)} async-done(((bf16[784,768]{1,0:T(8,128)(2,1)}), bf16[3136,768]{1,0:T(8,128)(2,1)}) %all-gather.25.cloned.1.call-update) | async-done | bytes 4816912 | tf_op jit(solution)/shard_map/all_gather | solution.py:174
  739.3 26.1 %fusion.61 = (f32[3136,768]{1,0:T(8,128)}, f32[3136,768]{1,0:T(8,128)}) fusion(f32[768]{0:T(1024)S(1)} %dynamic_slice.59, bf16[3136,768]{1,0:T(8,128)(2,1)} %all-gather.25.cloned.1.call-done, bf16[768,768]{1,0:T(8,128)(2,1)S(1)} %copy-done.61), kind=kOutput, calls=%fused_computation.96 | convolution fusion | flops 3851108352 | bytes 25267200 | tf_op jit(solution)/shard_map/dot_general | solution.py:175
  765.4 13.3 all-gather.27.cloned.1.call-done
  778.7 14.4 %convert_reduce_fusion = (f32[768]{0:T(1024)}, bf16[3136,768]{1,0:T(8,128)(2,1)S(1)}) fusion(f32[3136,768]{1,0:T(8,128)} %get-tuple-element.474, bf16[3136,768]{1,0:T(8,128)(2,1)} %all-gather.27.cloned.1.call-done, bf16[768,768]{0,1:T(8,128)(2,1)S(1)} %copy-done.62, f32[3136,768]{1,0:T(8,128)} %get-tuple-element.475, f32[768]{0:T(1024)S(1)} %dynamic_slice.59), kind=kOutput, calls=%fused_computation.106 | convolution fusion | flops 3740318976 | bytes 30087168 | tf_op jit(solution)/shard_map/td,fd->tf/dot_general | solution.py:233
  801.8 79.8 %reduce-scatter.20.cloned.1.call-done = f32[784,768]{1,0:T(8,128)} async-done(((f32[3136,768]{1,0:T(8,128)}), f32[784,768]{1,0:T(8,128)}) %reduce-scatter.20.cloned.1.call-update) | async-done | bytes 2408464 | tf_op jit(solution)/shard_map/reduce_scatter | solution.py:239
  891.0 37.9 %all-gather.29.cloned.1.call-done = bf16[3136,768]{1,0:T(8,128)(2,1)} async-done(((bf16[784,768]{1,0:T(8,128)(2,1)}), bf16[3136,768]{1,0:T(8,128)(2,1)}) %all-gather.29.cloned.1.call-update) | async-done | bytes 4816912 | tf_op jit(solution)/shard_map/all_gather | solution.py:247
  944.6 68.5 %while.38 = (s32[]{:T(128)}, bf16[4,784,3,64]{1,3,2,0:T(8,128)(2,1)}, bf16[4,784,3,64]{1,3,2,0:T(8,128)(2,1)}, bf16[4,784,3,64]{1,3,2,0:T(8,128)(2,1)}, s32[4]{0...) while((s32[]{:T(128)}, ...), condition=%wide.region_35.36_spmd, body=%wide.region_30.35_spmd.sunk | while | flops 1203017472 | bytes 62739500 | solution.py:254
  965.3 11.3 conditional.8
  999.3 11.3 conditional.8
  1041.6 10.2 convolution_bitcast_fusion
  1061.7 13.8 %fusion.81 = f32[768,768]{0,1:T(8,128)} fusion(bf16[3136,768]{1,0:T(8,128)(2,1)} %all-gather.27.cloned.1.call-done, f32[3136,768]{1,0:T(8,128)} %get-tuple-element.474, f32[3136,768]{1,0:T(8,128)} %get-tuple-element.475, f32[768]{0:T(1024)S(1)} %copy-done.58), kind=kOutput, calls=%fused_computation.141 | convolution fusion | flops 3709009920 | bytes 26446848 | tf_op jit(solution)/shard_map/tf,td->fd/dot_general | solution.py:232
  1084.9 24.3 %reduce-scatter.28.cloned.1.call-done = f32[96,576]{1,0:T(8,128)} async-done(((f32[768,576]{1,0:T(8,128)}), f32[96,576]{1,0:T(8,128)}) %reduce-scatter.28.cloned.1.call-update) | async-done | bytes 221200
  1111.2 79.5 %reduce-scatter.22.cloned.1.call-done = f32[784,768]{1,0:T(8,128)} async-done(((f32[3136,768]{1,0:T(8,128)}), f32[784,768]{1,0:T(8,128)}) %reduce-scatter.22.cloned.1.call-update) | async-done | bytes 2408464 | tf_op jit(solution)/shard_map/reduce_scatter | solution.py:275
  1193.6 41.6 %psum.7 = f32[9216]{0:T(1024)} all-reduce(f32[9216]{0:T(1024)S(1)} %constant_dynamic-update-slice_fusion.10), channel_id=1, replica_groups=mesh['dp'=8,'tensor'=4] {'dp','tensor'}, use_global_device_ids=true, to_apply=%region_51.52 | all-reduce | flops 9216 | bytes 73728 | tf_op jit(solution)/shard_map/psum | solution.py:307
  1239.0 25.6 %reduce-scatter.24.cloned.1.call-done = f32[96,768]{1,0:T(8,128)} async-done(((f32[768,768]{1,0:T(8,128)}), f32[96,768]{1,0:T(8,128)}) %reduce-scatter.24.cloned.1.call-update) | async-done | bytes 294928 | tf_op jit(solution)/shard_map/reduce_scatter | solution.py:312
  1264.6 72.6 %reduce-scatter.26.cloned.1.call-done = f32[768,96]{0,1:T(8,128)} async-done(((f32[768,768]{0,1:T(8,128)}), f32[768,96]{0,1:T(8,128)}) %reduce-scatter.26.cloned.1.call-update) | async-done | bytes 294928 | tf_op jit(solution)/shard_map/reduce_scatter | solution.py:313
  (468 shorter events, 407.3 us)
Async XLA Ops:
  8.0 81.1 %all-gather.11.cloned.1.call-start = ((), (), s32[]{:S(2)}) async-start(), calls=%async_computation.9 | async-start | bytes 6021120 | tf_op jit(solution)/shard_map/all_gather | solution.py:150
  13.0 263.4 %copy-start.38 = (f32[768]{0:T(1024)}, f32[768]{0:T(1024)S(1)}, u32[]{:S(2)}) copy-start(f32[768]{0:T(1024)S(1)} %get-tuple-element.466) | copy-start | bytes 9220
  13.0 263.4 %copy-start.46 = (f32[768]{0:T(1024)}, f32[768]{0:T(1024)S(1)}, u32[]{:S(2)}) copy-start(f32[768]{0:T(1024)S(1)} %get-tuple-element.465) | copy-start | bytes 9220
  14.6 258.7 %reduce-scatter.14.cloned.1.call-start = ((), (), s32[]{:S(2)}) async-start(), calls=%async_computation.10 | async-start | bytes 12042240 | tf_op jit(solution)/shard_map/reduce_scatter | solution.py:165
  14.8 97.7 %copy-start.50 = (f32[3,64]{1,0:T(4,128)}, f32[3,64]{1,0:T(4,128)S(1)}, u32[]{:S(2)}) copy-start(f32[3,64]{1,0:T(4,128)S(1)} %add.235) | copy-start | bytes 2308
  14.9 97.6 %copy-start.48 = (f32[3,64]{1,0:T(4,128)}, f32[3,64]{1,0:T(4,128)S(1)}, u32[]{:S(2)}) copy-start(f32[3,64]{1,0:T(4,128)S(1)} %add.232) | copy-start | bytes 2308
  193.0 85.9 %all-gather.15.cloned.1.call-start = ((), (), s32[]{:S(2)}) async-start(), calls=%async_computation.12 | async-start | bytes 1327104 | tf_op jit(solution)/shard_map/all_gather | solution.py:132
  193.6 86.1 %all-gather.17.cloned.1.call-start = ((), (), s32[]{:S(2)}) async-start(), calls=%async_computation.13 | async-start | bytes 1327104 | tf_op jit(solution)/shard_map/all_gather | solution.py:133
  194.2 123.9 %all-gather.13.cloned.1.call-start = ((), (), s32[]{:S(2)}) async-start(), calls=%async_computation.11 | async-start | bytes 6021120 | tf_op jit(solution)/shard_map/all_gather | solution.py:174
  278.1 119.2 %reduce-scatter.16.cloned.1.call-start = ((), (), s32[]{:S(2)}) async-start(), calls=%async_computation.14 | async-start | bytes 6021120 | tf_op jit(solution)/shard_map/reduce_scatter | solution.py:179
  278.9 499.8 %copy-start.57 = (f32[768]{0:T(1024)}, f32[768]{0:T(1024)S(1)}, u32[]{:S(2)}) copy-start(f32[768]{0:T(1024)S(1)} %dynamic_slice.59) | copy-start | bytes 9220
  348.8 121.6 %all-gather.19.cloned.1.call-start = ((), (), s32[]{:S(2)}) async-start(), calls=%async_computation.15 | async-start | bytes 1327104 | tf_op jit(solution)/shard_map/all_gather | solution.py:132
  401.0 92.0 %all-gather.21.cloned.1.call-start = ((), (), s32[]{:S(2)}) async-start(), calls=%async_computation.16 | async-start | bytes 1327104 | tf_op jit(solution)/shard_map/all_gather | solution.py:133
  401.7 130.1 %all-gather.23.cloned.1.call-start = ((), (), s32[]{:S(2)}) async-start(), calls=%async_computation.17 | async-start | bytes 6021120 | tf_op jit(solution)/shard_map/all_gather | solution.py:150
  495.3 201.0 %reduce-scatter.18.cloned.1.call-start = ((), (), s32[]{:S(2)}) async-start(), calls=%async_computation.18 | async-start | bytes 12042240 | tf_op jit(solution)/shard_map/reduce_scatter | solution.py:165
  616.1 123.1 %all-gather.25.cloned.1.call-start = ((), (), s32[]{:S(2)}) async-start(), calls=%async_computation.19 | async-start | bytes 6021120 | tf_op jit(solution)/shard_map/all_gather | solution.py:174
  701.3 77.4 %all-gather.27.cloned.1.call-start = ((), (), s32[]{:S(2)}) async-start(), calls=%async_computation.20 | async-start | bytes 6021120 | tf_op jit(solution)/shard_map/all_gather | solution.py:231
  701.9 179.7 %reduce-scatter.20.cloned.1.call-start = ((), (), s32[]{:S(2)}) async-start(), calls=%async_computation.21 | async-start | bytes 12042240 | tf_op jit(solution)/shard_map/reduce_scatter | solution.py:239
  801.8 127.1 %all-gather.29.cloned.1.call-start = ((), (), s32[]{:S(2)}) async-start(), calls=%async_computation.22 | async-start | bytes 6021120 | tf_op jit(solution)/shard_map/all_gather | solution.py:247
  890.9 192.4 %reduce-scatter.30.cloned.1.call-start = ((), (), s32[]{:S(2)}) async-start(), calls=%async_computation.27 | async-start | bytes 884736
  934.2 175.1 %reduce-scatter.28.cloned.1.call-start = ((), (), s32[]{:S(2)}) async-start(), calls=%async_computation.26 | async-start | bytes 2211840
  1041.3 149.3 %reduce-scatter.22.cloned.1.call-start = ((), (), s32[]{:S(2)}) async-start(), calls=%async_computation.23 | async-start | bytes 12042240 | tf_op jit(solution)/shard_map/reduce_scatter | solution.py:275
  1051.8 212.8 %reduce-scatter.24.cloned.1.call-start = ((), (), s32[]{:S(2)}) async-start(), calls=%async_computation.24 | async-start | bytes 2654208 | tf_op jit(solution)/shard_map/reduce_scatter | solution.py:312
  1061.4 275.8 %reduce-scatter.26.cloned.1.call-start = ((), (), s32[]{:S(2)}) async-start(), calls=%async_computation.25 | async-start | bytes 2654208 | tf_op jit(solution)/shard_map/reduce_scatter | solution.py:313
  1079.3 111.4 %copy-start.1 = (bf16[784,768]{1,0:T(8,128)(2,1)S(1)}, bf16[784,768]{1,0:T(8,128)(2,1)}, u32[]{:S(2)}) copy-start(bf16[784,768]{1,0:T(8,128)(2,1)} %param.26) | copy-start | bytes 3612676
  1079.3 111.4 %copy-start.35 = (f32[768]{0:T(1024)S(1)}, f32[768]{0:T(1024)}, u32[]{:S(2)}) copy-start(f32[768]{0:T(1024)} %copy-done.33) | copy-start | bytes 9220
  1079.3 111.4 %copy-start.37 = (f32[784]{0:T(1024)S(1)}, f32[784]{0:T(1024)}, u32[]{:S(2)}) copy-start(f32[784]{0:T(1024)} %copy-done.36) | copy-start | bytes 9412
  1079.3 111.4 %copy-start.42 = (f32[784]{0:T(1024)S(1)}, f32[784]{0:T(1024)}, u32[]{:S(2)}) copy-start(f32[784]{0:T(1024)} %copy-done.41) | copy-start | bytes 9412
  1082.8 110.7 %copy-start.56 = (f32[768]{0:T(1024)S(1)}, f32[768]{0:T(1024)}, u32[]{:S(2)}) copy-start(f32[768]{0:T(1024)} %get-tuple-element.381) | copy-start | bytes 9220
  1082.8 110.7 %copy-start.55 = (f32[768]{0:T(1024)S(1)}, f32[768]{0:T(1024)}, u32[]{:S(2)}) copy-start(f32[768]{0:T(1024)} %get-tuple-element.387) | copy-start | bytes 9220
  1082.8 110.7 %copy-start.53 = (f32[768]{0:T(1024)S(1)}, f32[768]{0:T(1024)}, u32[]{:S(2)}) copy-start(f32[768]{0:T(1024)} %get-tuple-element.435) | copy-start | bytes 9220
  1082.8 110.8 %copy-start.52 = (f32[768]{0:T(1024)S(1)}, f32[768]{0:T(1024)}, u32[]{:S(2)}) copy-start(f32[768]{0:T(1024)} %get-tuple-element.463) | copy-start | bytes 9220
  (55 other events, 1023.5 us)
Sparse Core Ops, SparseCore 0:
  14.7 40.7 all-gather.10
  193.1 80.0 reduce-scatter.13
  616.2 79.9 reduce-scatter.17
  801.9 79.6 reduce-scatter.19
Sparse Core Ops, SparseCore 1:
  195.7 41.9 all-gather.14
  239.7 39.9 all-gather.16
  281.7 36.3 all-gather.12
  348.9 48.3 reduce-scatter.15
  401.0 46.5 all-gather.18
  450.0 42.8 all-gather.20
  495.4 36.3 all-gather.22
  701.4 37.8 all-gather.24
  740.8 37.8 all-gather.26
  891.0 37.8 all-gather.28
  934.3 62.5 reduce-scatter.29
  1041.4 67.8 reduce-scatter.27
  1111.9 78.7 reduce-scatter.21
  1195.1 69.4 reduce-scatter.23
  1269.1 68.1 reduce-scatter.25
where the time goes:
time: 1350 us; the launch traced here: 1340 us
  waiting for transfers between devices  678 us (50%)
  matrix products  199 us (15%)
  local copies, waits for them, and re-layouts  191 us (14%)
  blocking collectives  182 us (13%)
  other arithmetic  66.2 us (5%)
  between operations  17.4 us (1%)
    reduce_scatter x2, waiting for transfers between devices, forward_pass(): lax.psum_scatter(jnp.dot(attended, out_full, preferred_element_type=jnp.f...  159 us
    reduce_scatter x1, waiting for transfers between devices, backward_pass(): lax.psum_scatter(jnp.einsum('tf,df->td', grad_pre, up_full, preferred_ele...  79.8 us
    reduce_scatter x1, waiting for transfers between devices, backward_pass(): lax.psum_scatter(jnp.einsum('cte,cde->td', grad_mixed, qkv_full, preferre...  79.5 us
    all_gather x2, waiting for transfers between devices, forward_pass(): normed2_all = lax.all_gather(normed2_all, 'tensor', axis=0, tiled=True)  75.7 us
    all_gather x2, blocking collectives, gather_weights(): lax.all_gather(shards[0], 'dp', axis=1, tiled=True)  73.4 us
    reduce_scatter x1, waiting for transfers between devices, backward_pass(): lax.psum_scatter(matrices[3], 'dp', scatter_dimension=1, tiled=True)  72.6 us
    all_gather x2, blocking collectives, gather_weights(): lax.all_gather(shards[1], 'dp', axis=1, tiled=True)  67.2 us
    reduce_scatter x1, waiting for transfers between devices, forward_pass(): lax.psum_scatter(jnp.dot(active, down_full, preferred_element_type=jnp.fl...  48.4 us
  transfers between devices with their start and end apart: 19, of which 15 were waited for; matrix products, arithmetic and copies ran while one was open for 14% of the time, Pallas kernels for 0%

commit v1 on v0

v1 whole, which is shorter than its diff:
```python
import jax
import jax.numpy as jnp
from jax import lax
from jax.sharding import PartitionSpec as P

HD = 64
BOTH = ("dp", "tensor")
F32 = jnp.float32
BF16 = jnp.bfloat16


def unpack(vectors, d, ff):
    cuts = [d * i for i in range(8)] + [7 * d + ff, 8 * d + ff]
    return tuple(vectors[a:b] for a, b in zip(cuts[:-1], cuts[1:]))


def norm_parts(values):
    centred = values - jnp.mean(values, axis=-1, keepdims=True)
    inverse = lax.rsqrt(jnp.mean(centred * centred, axis=-1, keepdims=True) + 1e-06)
    return centred * inverse, inverse


def norm_backward(grad_normed, scaled, inverse, gain):
    weighted = grad_normed * gain
    return inverse * (
        weighted
        - jnp.mean(weighted, axis=-1, keepdims=True)
        - scaled * jnp.mean(weighted * scaled, axis=-1, keepdims=True)
    )


def gelu_parts(v):
    cdf = 0.5 * (1.0 + lax.erf(v * (0.5**0.5)))
    return v * cdf, cdf + v * jnp.exp(-0.5 * v * v) * ((2.0 * jnp.pi) ** -0.5)


def dot(a, b, dims):
    return lax.dot_general(a, b, (dims, ((), ())), preferred_element_type=F32)


def pack_shards(qkv, out, up, down):
    first = jnp.concatenate([qkv[0], qkv[1], qkv[2], out.T], axis=1)
    return jnp.stack([first, up, down.T])


def gather_blocks(shards, dp, tensor):
    every = lax.all_gather(shards, BOTH, axis=0)
    b, r, c = shards.shape
    every = every.reshape(dp, tensor, b, r, c).transpose(2, 1, 0, 3, 4)
    return every.reshape(b, tensor, dp * r, c)


def scatter_blocks(blocks, dp, tensor):
    b, t, rows, c = blocks.shape
    r = rows // dp
    pieces = blocks.reshape(b, tensor, dp, r, c).transpose(2, 1, 0, 3, 4)
    pieces = pieces.reshape(dp * tensor, b, r, c)
    return lax.psum_scatter(pieces, BOTH, scatter_dimension=0, tiled=True)[0]


def local_layer(tokens, cotangent, patches, blocks, vectors):
    rows, d = tokens.shape
    tensor, c = blocks.shape[1], blocks.shape[3]
    w = c // 4
    ff = tensor * c
    heads = d // HD
    gain1, bias1, gain2, bias2, bias_q, bias_v, bias_out, bias_up, bias_down = unpack(
        vectors, d, ff
    )
    first, up, downt = blocks[0], blocks[1], blocks[2]
    factor = HD**-0.5

    x = tokens.astype(F32)
    scaled1, inverse1 = norm_parts(x)
    normed1 = (scaled1 * gain1 + bias1).astype(BF16)
    mixed = jnp.einsum("rd,tdc->rtc", normed1, first[:, :, : 3 * w], preferred_element_type=F32)
    query = (mixed[:, :, :w].reshape(rows, d) + bias_q).astype(BF16).reshape(rows, heads, HD)
    key = mixed[:, :, w : 2 * w].reshape(rows, d).astype(BF16).reshape(rows, heads, HD)
    value = (mixed[:, :, 2 * w :].reshape(rows, d) + bias_v).astype(BF16).reshape(rows, heads, HD)
    images = jnp.arange(rows, dtype=jnp.int32) // patches
    allowed = images[:, None] == images[None, :]
    scores = jnp.einsum("qhd,khd->hqk", query, key, preferred_element_type=F32) * factor
    scores = jnp.where(allowed[None], scores, -1e30)
    raised = jnp.exp(scores - jnp.max(scores, axis=-1, keepdims=True))
    soft = raised / jnp.sum(raised, axis=-1, keepdims=True)
    soft_low = soft.astype(BF16)
    attended = jnp.einsum("hqk,khd->qhd", soft_low, value, preferred_element_type=F32).astype(BF16)
    flat = attended.reshape(rows, tensor, w)
    outt = first[:, :, 3 * w :]
    residual = x + jnp.einsum("rte,tde->rd", flat, outt, preferred_element_type=F32) + bias_out
    scaled2, inverse2 = norm_parts(residual)
    normed2 = (scaled2 * gain2 + bias2).astype(BF16)
    pre = jnp.einsum("rd,tdf->rtf", normed2, up, preferred_element_type=F32) + bias_up.reshape(
        tensor, c
    )
    active, slope = gelu_parts(pre)
    active = active.astype(BF16)
    second = jnp.einsum("rtf,tdf->rd", active, downt, preferred_element_type=F32)
    output = (residual + second + bias_down).astype(BF16)

    grad_active = jnp.einsum("rd,tdf->rtf", cotangent, downt, preferred_element_type=F32)
    grad_pre = (grad_active * slope).astype(BF16)
    g_down = jnp.einsum("rd,rtf->tdf", cotangent, active, preferred_element_type=F32)
    g_up = jnp.einsum("rd,rtf->tdf", normed2, grad_pre, preferred_element_type=F32)
    grad_normed2 = jnp.einsum("rtf,tdf->rd", grad_pre, up, preferred_element_type=F32)
    grad_result = cotangent.astype(F32)
    grad_residual = grad_result + norm_backward(grad_normed2, scaled2, inverse2, gain2)
    grad_branch = grad_residual.astype(BF16)
    g_outt = jnp.einsum("rd,rte->tde", grad_branch, flat, preferred_element_type=F32)
    grad_att = jnp.einsum("rd,tde->rte", grad_branch, outt, preferred_element_type=F32)
    grad_att = grad_att.astype(BF16).reshape(rows, heads, HD)
    grad_value = jnp.einsum("hqk,qhd->khd", soft_low, grad_att, preferred_element_type=F32)
    grad_soft = jnp.einsum("qhd,khd->hqk", grad_att, value, preferred_element_type=F32)
    grad_scores = (
        soft * (grad_soft - jnp.sum(soft * grad_soft, axis=-1, keepdims=True))
    ).astype(BF16)
    grad_query = (
        jnp.einsum("hqk,khd->qhd", grad_scores, key, preferred_element_type=F32) * factor
    )
    grad_key = jnp.einsum("hqk,qhd->khd", grad_scores, query, preferred_element_type=F32) * factor
    three = [
        g.astype(BF16).reshape(rows, tensor, w) for g in (grad_query, grad_key, grad_value)
    ]
    grad_mixed = jnp.concatenate(three, axis=2)
    g_qkv = jnp.einsum("rd,rtc->tdc", normed1, grad_mixed, preferred_element_type=F32)
    grad_normed1 = jnp.einsum(
        "rtc,tdc->rd", grad_mixed, first[:, :, : 3 * w], preferred_element_type=F32
    )
    grad_tokens = (grad_residual + norm_backward(grad_normed1, scaled1, inverse1, gain1)).astype(
        BF16
    )
    grads = jnp.stack(
        [
            jnp.concatenate([g_qkv, g_outt], axis=2).astype(BF16),
            g_up.astype(BF16),
            g_down.astype(BF16),
        ]
    )

    def total(values):
        return jnp.sum(values.astype(F32), axis=0).reshape(-1)

    sums = jnp.concatenate(
        [
            total(grad_normed1 * scaled1),
            total(grad_normed1),
            total(grad_normed2 * scaled2),
            total(grad_normed2),
            total(three[0]),
            total(three[2]),
            total(grad_residual),
            total(grad_pre),
            total(grad_result),
        ]
    )
    return output, grad_tokens, grads, sums


def make_body(dp, tensor):
    def body(
        tokens,
        cotangent,
        block_patches,
        qkv,
        out,
        up,
        down,
        vectors,
        momentum,
        target_qkv,
        target_out,
        target_up,
        target_down,
        target_vectors,
    ):
        patches = block_patches[lax.axis_index("tensor")]
        blocks = gather_blocks(pack_shards(qkv, out, up, down), dp, tensor)
        output, grad_tokens, grads, sums = local_layer(
            tokens, cotangent, patches, blocks, vectors
        )
        grads = scatter_blocks(grads, dp, tensor).astype(F32)
        sums = lax.psum(sums, BOTH)
        w = qkv.shape[2]
        rate = momentum[0]

        def average(target, online):
            return rate * target + (1.0 - rate) * online.astype(F32)

        return (
            output,
            grad_tokens,
            jnp.stack([grads[0][:, i * w : (i + 1) * w] for i in range(3)]),
            grads[0][:, 3 * w :].T,
            grads[1],
            grads[2].T,
            sums,
            average(target_qkv, qkv),
            average(target_out, out),
            average(target_up, up),
            average(target_down, down),
            average(target_vectors, vectors),
        )

    return body


def solution(mesh):
    rows, matrices = P(BOTH, None), (
        P(None, "dp", "tensor"),
        P("tensor", "dp"),
        P("dp", "tensor"),
        P("tensor", "dp"),
    )
    return jax.shard_map(
        make_body(mesh.shape["dp"], mesh.shape["tensor"]),
        mesh=mesh,
        in_specs=(rows, rows, P("dp")) + matrices + (P(), P()) + matrices + (P(),),
        out_specs=(rows, rows) + matrices + (P(),) + matrices + (P(),),
        check_vma=False,
    )
```

time: 1350 us -> 552 us (0.41)
  waiting for transfers between devices: 678 us -> 191 us
  blocking collectives: 182 us -> 39.2 us
  local copies, waits for them, and re-layouts: 191 us -> 64.2 us
  matrix products: 199 us -> 174 us
    reduce_scatter x7 -> x1, waiting for transfers between devices: 465 us -> 90.7 us  [scatter_blocks(): return lax.psum_scatter(pieces, BOTH, scatter_dimension=0, tiled=True)[0]]
    all_gather x4 -> x0, blocking collectives: 141 us -> none  [the longest x2 73.4 us: gather_weights(): lax.all_gather(shards[0], 'dp', axis=1, tiled=True)]
    all_gather x10 -> x1, waiting for transfers between devices: 186 us -> 100 us  [gather_blocks(): every = lax.all_gather(shards, BOTH, axis=0)]
    squeeze x32 -> x1, local copies, waits for them, and re-layouts: 47.3 us -> 0.86 us  [pack_shards(): first = jnp.concatenate([qkv[0], qkv[1], qkv[2], out.T], axis=1)]
    another operation x29 -> x0, local copies, waits for them, and re-layouts: 37.7 us -> none
    unnamed x21 -> x2, waiting for transfers between devices: 26.8 us -> 0.03 us
    dot_general x46 -> x16, matrix products: 176 us -> 154 us  [the longest x1 25.2 us: local_layer(): jnp.einsum('qhd,khd->hqk', grad_att, value, preferred_element_type=F32)]
    slice x7 -> x12, local copies, waits for them, and re-layouts: 9.54 us -> 31.2 us  [the longest x4 11.4 us: local_layer(): first, up, downt = (blocks[0], blocks[1], blocks[2])]
  transfers between devices with their start and end apart: 19 -> 2, of which waited for: 15 -> 2; matrix products, arithmetic and copies ran while one was open for 14% -> 7% of each run, Pallas kernels for 0% -> 0%
where the time goes in v1:
time: 552 us; the launch traced here: 542 us
  waiting for transfers between devices  191 us (35%)
  matrix products  174 us (32%)
  local copies, waits for them, and re-layouts  64.2 us (12%)
  other arithmetic  56.6 us (10%)
  blocking collectives  39.2 us (7%)
  between operations  16.5 us (3%)
    all_gather x1, waiting for transfers between devices, gather_blocks(): every = lax.all_gather(shards, BOTH, axis=0)  100 us
    reduce_scatter x1, waiting for transfers between devices, scatter_blocks(): return lax.psum_scatter(pieces, BOTH, scatter_dimension=0, tiled=True)[0]  90.7 us
    psum x1, blocking collectives, body(): sums = lax.psum(sums, BOTH)  39.2 us
    convert_element_type x1, other arithmetic, local_layer(): grad_scores = (soft * (grad_soft - jnp.sum(soft * grad_soft, axis=-1, kee...  27.9 us
    dot_general x1, matrix products, local_layer(): jnp.einsum('qhd,khd->hqk', grad_att, value, preferred_element_type=F32)  25.2 us
    sub x1, matrix products, local_layer(): raised = jnp.exp(scores - jnp.max(scores, axis=-1, keepdims=True))  19 us
    dot_general x1, matrix products, local_layer(): jnp.einsum('hqk,qhd->khd', soft_low, grad_att, preferred_element_type=F32)  15.6 us
    dot_general x1, matrix products, local_layer(): jnp.einsum('hqk,khd->qhd', soft_low, value, preferred_element_type=F32)  14.8 us
  transfers between devices with their start and end apart: 2, of which 2 were waited for; matrix products, arithmetic and copies ran while one was open for 7% of the time, Pallas kernels for 0%

profile of v1, /device:TPU:0, one launch (start us, length us, event | category | flops | bytes accessed | tf_op | source)
XLA Modules:
  0.0 541.5 jit_solution(5149204099893250085)
XLA Ops:
  17.3 100.2 %all-gather.3.cloned.1.call-done = bf16[96,96,768]{2,1,0:T(8,128)(2,1)} async-done(((bf16[3,96,768]{2,1,0:T(8,128)(2,1)}), bf16[96,96,768]{2,1,0:T(8,128)(2,1)}) %all-gather.3.cloned.1.call-update) | async-done | bytes 14155792 | tf_op jit(solution)/shard_map/all_gather | solution.py:47
  117.5 5.9 %fusion.70 = (bf16[1,4,8,96,768]{4,3,0,1,2:T(8,128)(2,1)S(1)}, bf16[1,4,8,96,768]{4,3,0,1,2:T(8,128)(2,1)S(1)}, bf16[1,4,8,96,768]{4,3,0,1,2:T(8,128)(2,1)S(1)}) fusion(bf16[3,4,8,96,768]{4,3,0,1,2:T(8,128)(2,1)} %bitcast.155), kind=kLoop, calls=%fused_computation.137 | loop fusion | bytes 28311552 | tf_op jit(solution)/shard_map/slice | solution.py:70
  126.1 5.8 %fusion.17 = f32[784,4,576]{2,0,1:T(8,128)} fusion(bf16[4,768,768]{2,1,0:T(8,128)(2,1)S(1)} %bitcast.158, bf16[784,768]{1,0:T(8,128)(2,1)S(1)} %copy-done.2, f32[768]{0:T(1024)S(1)} %get-tuple-element.92, f32[768]{0:T(1024)S(1)} %get-tuple-element.93, f32[784]{0:T(1024)S(1)} %add_rsqrt_fusion.1, f32[784]{0:T(1024)S(1)} %broadcast_multiply_fusion.5), kind=kOutput, calls=%fused_computation.31 | convolution fusion | flops 2778144768 | bytes 12378112 | tf_op jit(solution)/shard_map/rd,tdc->rtc/dot_general | solution.py:76
  131.9 3.0 slice.172
  134.8 6.1 %fusion.71 = (f32[784,4,192]{2,0,1:T(8,128)}, f32[784,4,192]{2,0,1:T(8,128)}) fusion(f32[784,4,576]{2,0,1:T(8,128)} %fusion.17), kind=kLoop, calls=%fused_computation.138 | loop fusion | bytes 9633792 | tf_op jit(solution)/shard_map/slice | solution.py:77
  143.4 2.6 copy.85
  150.1 4.6 copy.80
  154.7 19.0 %fusion.73 = (f32[12,784]{1,0:T(8,128)S(1)}, f32[12,784,784]{1,2,0:T(8,128)}) fusion(pred[784,784]{0,1:T(8,128)(4,1)S(1)} %broadcast_compare_fusion, bf16[784,12,64]{0,2,1:T(8,128)(2,1)} %bitcast.161, f32[784,12,64]{0,2,1:T(8,128)S(1)} %bitcast.152, f32[12,64]{1,0:T(8,128)S(1)} %add.137), kind=kOutput, calls=%fused_computation.140 | convolution fusion | flops 974820096 | bytes 33771520 | tf_op jit(solution)/shard_map/sub | solution.py:84
  173.7 14.8 %fusion.42 = bf16[12,64,784]{2,1,0:T(8,128)(2,1)S(1)} fusion(f32[784,12,64]{0,2,1:T(8,128)} %bitcast.175, f32[12,64]{1,0:T(8,128)S(1)} %add.133, f32[12,784,784]{1,2,0:T(8,128)} %get-tuple-element.95, f32[12,784]{1,0:T(8,128)S(1)} %get-tuple-element.94), kind=kOutput, calls=%fused_computation.77 | convolution fusion | flops 960669696 | bytes 33156864 | tf_op jit(solution)/shard_map/hqk,khd->qhd/dot_general | solution.py:87
  188.5 4.3 fusion.74
  193.3 6.2 %multiply_convert_fusion.1 = (bf16[784,4,768]{2,0,1:T(8,128)(2,1)}, f32[784,4,768]{2,0,1:T(8,128)S(1)}) fusion(f32[4,768]{1,0:T(4,128)S(1)} %slice.130, bf16[4,768,768]{2,1,0:T(8,128)(2,1)S(1)} %bitcast.173, f32[784,768]{1,0:T(8,128)S(1)} %get-tuple-element.97, f32[768]{0:T(1024)S(1)} %get-tuple-element.87, f32[768]{0:T(1024)S(1)} %get-tuple-element.88, ...), kind=kOutput, calls=%fused_computation.19 | convolution fusion | flops 3716837376 | bytes 21602432 | tf_op jit(solution)/shard_map/rd,tdf->rtf/dot_general | solution.py:93
  199.6 9.4 %convert_reduce_fusion = (f32[4,768]{1,0:T(4,128)}, bf16[784,4,768]{2,0,1:T(8,128)(2,1)S(1)}) fusion(f32[784,4,768]{2,0,1:T(8,128)S(1)} %get-tuple-element.99, f32[4,768]{1,0:T(4,128)S(1)} %slice.130, bf16[4,768,768]{2,1,0:T(8,128)(2,1)S(1)} %bitcast.170, bf16[784,768]{1,0:T(8,128)(2,1)S(1)} %copy-done.16), kind=kOutput, calls=%fused_computation.18 | convolution fusion | flops 3730682880 | bytes 20398080 | tf_op jit(solution)/shard_map/rd,tdf->rtf/dot_general | solution.py:101
  209.0 6.3 %fusion.37 = (f32[768]{0:T(1024)}, f32[784]{0:T(1024)S(1)}, f32[784]{0:T(1024)S(1)}, f32[768]{0:T(1024)}, f32[784,768,1]{1,0,2:T(8,128)}) fusion(f32[784,768]{1,0:T(8,128)S(1)} %get-tuple-element.97, f32[784]{0:T(1024)S(1)} %add_rsqrt_fusion, f32[784]{0:T(1024)S(1)} %broadcast_multiply_fusion.4, f32[768]{0:T(1024)S(1)} %get-tuple-element.88, ...), kind=kOutput, calls=%fused_computation.67 | convolution fusion | flops 3704792064 | bytes 14374144 | tf_op jit(solution)/shard_map/rtf,tdf->rd/dot_general | solution.py:105
  215.3 7.4 %convolution_convert_fusion.1 = bf16[4,768,768]{1,2,0:T(8,128)(2,1)} fusion(bf16[784,4,768]{2,0,1:T(8,128)(2,1)S(1)} %get-tuple-element.109, f32[784,768]{1,0:T(8,128)S(1)} %get-tuple-element.97, f32[768]{0:T(1024)S(1)} %get-tuple-element.87, f32[768]{0:T(1024)S(1)} %get-tuple-element.88, f32[784]{0:T(1024)S(1)} %add_rsqrt_fusion, ...), kind=kOutput, calls=%fused_computation.39 | convolution fusion | flops 3704745984 | bytes 11956352 | tf_op jit(solution)/shard_map/rd,rtf->tdf/dot_general | solution.py:104
  222.7 2.6 copy.103
  225.3 3.3 fusion.69
  233.8 15.6 %convert_reduce_fusion.3 = (f32[12,64]{1,0:T(8,128)}, bf16[12,64,784]{2,1,0:T(8,128)(2,1)}) fusion(bf16[784,12,64]{0,2,1:T(8,128)(2,1)} %bitcast.179, f32[12,784,784]{1,2,0:T(8,128)} %get-tuple-element.95, f32[12,784]{1,0:T(8,128)S(1)} %get-tuple-element.94), kind=kOutput, calls=%fused_computation.46 | convolution fusion | flops 960668928 | bytes 31952640 | tf_op jit(solution)/shard_map/hqk,qhd->khd/dot_general | solution.py:112
  249.4 25.2 %multiply_reduce_fusion = (f32[12,784]{1,0:T(8,128)S(1)}, f32[12,784,784]{1,2,0:T(8,128)}) fusion(f32[12,784,784]{1,2,0:T(8,128)} %get-tuple-element.95, f32[12,784]{1,0:T(8,128)S(1)} %get-tuple-element.94, bf16[784,12,64]{0,2,1:T(8,128)(2,1)} %bitcast.180, f32[784,12,64]{0,2,1:T(8,128)S(1)} %bitcast.176, f32[12,64]{1,0:T(8,128)S(1)} %add.133), kind=kOutput, calls=%fused_computation.2 | convolution fusion | flops 967434048 | bytes 62697984 | tf_op jit(solution)/shard_map/qhd,khd->hqk/dot_general | solution.py:113
  274.6 27.9 %multiply_convert_fusion = bf16[12,784,784]{1,2,0:T(8,128)(2,1)} fusion(f32[12,784,784]{1,2,0:T(8,128)} %get-tuple-element.102, f32[12,784]{1,0:T(8,128)S(1)} %get-tuple-element.101, f32[12,784,784]{1,2,0:T(8,128)} %get-tuple-element.95, f32[12,784]{1,0:T(8,128)S(1)} %get-tuple-element.94), kind=kLoop, calls=%fused_computation.1 | loop fusion | flops 29503488 | bytes 73833984 | tf_op jit(solution)/shard_map/convert_element_type | solution.py:116
  302.5 10.1 %multiply_convert_fusion.2 = bf16[12,64,784]{2,1,0:T(8,128)(2,1)} fusion(bf16[12,784,784]{1,2,0:T(8,128)(2,1)} %multiply_convert_fusion, f32[784,12,64]{0,2,1:T(8,128)S(1)} %bitcast.153, f32[12,64]{1,0:T(8,128)S(1)} %copy-done.26), kind=kOutput, calls=%fused_computation.48 | convolution fusion | flops 946520064 | bytes 18367488 | tf_op jit(solution)/shard_map/hqk,qhd->khd/dot_general | solution.py:120
  312.7 10.8 %convert_reduce_fusion.4 = (f32[12,64]{1,0:T(8,128)}, bf16[12,64,784]{2,1,0:T(8,128)(2,1)}) fusion(bf16[784,12,64]{0,2,1:T(8,128)(2,1)S(1)} %bitcast.162, bf16[12,784,784]{1,2,0:T(8,128)(2,1)} %multiply_convert_fusion), kind=kOutput, calls=%fused_computation.47 | convolution fusion | flops 946519296 | bytes 17163264 | tf_op jit(solution)/shard_map/hqk,khd->qhd/dot_general | solution.py:118
  323.5 9.2 %convolution_convert_fusion = bf16[4,768,768]{1,2,0:T(8,128)(2,1)} fusion(bf16[784,4,768]{2,0,1:T(8,128)(2,1)} %get-tuple-element.98, bf16[784,768]{1,0:T(8,128)(2,1)S(1)} %copy-done.17), kind=kOutput, calls=%fused_computation.38 | convolution fusion | flops 3701735424 | bytes 10739712 | tf_op jit(solution)/shard_map/rd,rtf->tdf/dot_general | solution.py:103
  338.6 2.7 copy.90
  341.4 8.5 %convert_bitcast_fusion = bf16[4,768,576]{1,2,0:T(8,128)(2,1)} fusion(bf16[784,4,192]{2,0,1:T(8,128)(2,1)S(1)} %copy-done.14, bf16[784,4,192]{2,0,1:T(8,128)(2,1)} %copy.91, bf16[784,4,192]{2,0,1:T(8,128)(2,1)} %copy.90, bf16[784,768]{1,0:T(8,128)(2,1)S(1)} %copy-done.4, f32[768]{0:T(1024)S(1)} %copy-done.40, f32[768]{0:T(1024)S(1)} %copy-done.32, ...), kind=kOutput, calls=%fused_computation.30 | convolution fusion | flops 2790752256 | bytes 8368256 | tf_op jit(solution)/shard_map/rd,rtc->tdc/dot_general | solution.py:125
  350.0 6.1 %copy.93 = bf16[4,768,576]{2,1,0:T(8,128)(2,1)} copy(bf16[4,768,576]{1,2,0:T(8,128)(2,1)} %convert_bitcast_fusion) | data formatting | bytes 7077888 | tf_op jit(solution)/shard_map/rd,rtc->tdc/transpose | solution.py:125
  356.0 7.7 %maximum_bitcast_fusion = bf16[8,4,3,96,768]{4,3,0,1,2:T(8,128)(2,1)S(1)} fusion(bf16[1,4,8,96,768]{4,3,2,1,0:T(8,128)(2,1)} %bitcast.166, bf16[1,4,8,96,768]{4,3,2,1,0:T(8,128)(2,1)} %bitcast.165, bf16[1,4,8,96,192]{4,3,2,1,0:T(8,128)(2,1)S(1)} %bitcast.164, bf16[1,4,8,96,576]{4,3,2,1,0:T(8,128)(2,1)} %bitcast.154), kind=kLoop, calls=%fused_computation.11 | loop fusion | flops 56623104 | bytes 28311552 | tf_op jit(solution)/shard_map/transpose | solution.py:56
  363.7 6.0 %copy.95 = bf16[8,4,3,96,768]{4,3,2,1,0:T(8,128)(2,1)} copy(bf16[8,4,3,96,768]{4,3,0,1,2:T(8,128)(2,1)S(1)} %maximum_bitcast_fusion) | data formatting | bytes 28311552 | tf_op jit(solution)/shard_map/transpose | solution.py:56
  379.3 8.7 %fusion.34 = (f32[768]{0:T(1024)S(1)}, f32[784]{0:T(1024)S(1)}, f32[784]{0:T(1024)S(1)}, f32[768]{0:T(1024)S(1)}, f32[784,768,1]{1,0,2:T(8,128)}) fusion(bf16[784,768]{1,0:T(8,128)(2,1)S(1)} %copy-done.4, f32[784]{0:T(1024)} %copy-done.33, f32[784]{0:T(1024)S(1)} %copy-done.28, f32[768]{0:T(1024)S(1)} %copy-done.32, bf16[4,768,768]{2,1,0:T(8,128)(2,1)} %bitcast.160, ...), kind=kOutput, calls=%fused_computation.59 | convolution fusion | flops 2791388160 | bytes 11983040 | tf_op jit(solution)/shard_map/rtc,tdc->rd/dot_general | solution.py:126
  388.1 39.2 %psum.7 = f32[9216]{0:T(1024)} all-reduce(f32[9216]{0:T(1024)S(1)} %constant_dynamic-update-slice_fusion), channel_id=1, replica_groups=mesh['dp'=8,'tensor'=4] {'dp','tensor'}, use_global_device_ids=true, to_apply=%region_21.22 | all-reduce | flops 9216 | bytes 73728 | tf_op jit(solution)/shard_map/psum | solution.py:182
  427.4 3.8 fusion.33
  431.2 8.8 %fusion.39 = bf16[784,768]{1,0:T(8,128)(2,1)} fusion(f32[784,768]{1,0:T(8,128)S(1)} %copy-done.9, bf16[784,4,768]{2,0,1:T(8,128)(2,1)} %get-tuple-element.98, bf16[4,768,768]{2,1,0:T(8,128)(2,1)} %bitcast.167, f32[768]{0:T(1024)S(1)} %copy-done.38), kind=kOutput, calls=%fused_computation.70 | convolution fusion | flops 3701182464 | bytes 13151232 | tf_op jit(solution)/shard_map/rtf,tdf->rd/dot_general | solution.py:98
  440.0 90.7 %reduce-scatter.2.cloned.1.call-done = bf16[1,3,96,768]{3,2,1,0:T(8,128)(2,1)} async-done(((bf16[32,3,96,768]{3,2,1,0:T(8,128)(2,1)}), bf16[1,3,96,768]{3,2,1,0:T(8,128)(2,1)}) %reduce-scatter.2.cloned.1.call-update) | async-done | bytes 442384 | tf_op jit(solution)/shard_map/reduce_scatter | solution.py:58
  (160 shorter events, 42.6 us)
Async XLA Ops:
  7.2 8.8 %copy-start.2 = (bf16[784,768]{1,0:T(8,128)(2,1)S(1)}, bf16[784,768]{1,0:T(8,128)(2,1)}, u32[]{:S(2)}) copy-start(bf16[784,768]{1,0:T(8,128)(2,1)} %param.14) | copy-start | bytes 3612676
  7.2 110.3 %all-gather.3.cloned.1.call-start = ((), (), s32[]{:S(2)}) async-start(), calls=%async_computation.2 | async-start | bytes 14598144 | tf_op jit(solution)/shard_map/all_gather | solution.py:47
  11.0 519.7 %reduce-scatter.2.cloned.1.call-start = ((), (), s32[]{:S(2)}) async-start(), calls=%async_computation.1 | async-start | bytes 14598144 | tf_op jit(solution)/shard_map/reduce_scatter | solution.py:58
  15.1 111.0 %copy-start.31 = (f32[768]{0:T(1024)}, f32[768]{0:T(1024)S(1)}, u32[]{:S(2)}) copy-start(f32[768]{0:T(1024)S(1)} %get-tuple-element.93) | copy-start | bytes 9220
  15.1 111.0 %copy-start.39 = (f32[768]{0:T(1024)}, f32[768]{0:T(1024)S(1)}, u32[]{:S(2)}) copy-start(f32[768]{0:T(1024)S(1)} %get-tuple-element.92) | copy-start | bytes 9220
  15.2 139.5 %copy-start.25 = (f32[12,64]{1,0:T(8,128)}, f32[12,64]{1,0:T(8,128)S(1)}, u32[]{:S(2)}) copy-start(f32[12,64]{1,0:T(8,128)S(1)} %add.137) | copy-start | bytes 9220
  16.3 109.8 %copy-start.27 = (f32[784]{0:T(1024)}, f32[784]{0:T(1024)S(1)}, u32[]{:S(2)}) copy-start(f32[784]{0:T(1024)S(1)} %broadcast_multiply_fusion.5) | copy-start | bytes 9412
  16.8 109.2 %copy-start.33 = (f32[784]{0:T(1024)}, f32[784]{0:T(1024)S(1)}, u32[]{:S(2)}) copy-start(f32[784]{0:T(1024)S(1)} %add_rsqrt_fusion.1) | copy-start | bytes 9412
  123.7 8.1 %copy-start.10 = (bf16[1,4,8,96,768]{4,3,2,1,0:T(8,128)(2,1)}, bf16[1,4,8,96,768]{4,3,2,1,0:T(8,128)(2,1)S(1)}, u32[]{:S(2)}) copy-start(bf16[1,4,8,96,768]{4,3,2,1,0:T(8,128)(2,1)S(1)} %copy.78) | copy-start | bytes 14155780
  173.6 14.8 %copy-start.3 = (bf16[784,768]{1,0:T(8,128)(2,1)S(1)}, bf16[784,768]{1,0:T(8,128)(2,1)}, u32[]{:S(2)}) copy-start(bf16[784,768]{1,0:T(8,128)(2,1)} %param.14) | copy-start | bytes 3612676
  188.5 4.8 slice-start.2
  188.5 11.1 %slice-start = ((s8[4718592]{0:T(1024)(128)(4,1)}), s8[4194304]{0:T(1024)(128)(4,1)S(1)}, s32[]{:S(2)}) async-start(s8[4718592]{0:T(1024)(128)(4,1)} %bitcast.168), calls=%async_computation.3 | async-start | bytes 8388608
  192.8 22.5 %copy-start.7 = (f32[784,768]{1,0:T(8,128)}, f32[784,768]{1,0:T(8,128)S(1)}, u32[]{:S(2)}) copy-start(f32[784,768]{1,0:T(8,128)S(1)} %get-tuple-element.97) | copy-start | bytes 7225348
  193.3 6.3 %slice-start.1 = ((s8[4718592]{0:T(1024)(128)(4,1)}), s8[524288]{0:T(1024)(128)(4,1)S(1)}, s32[]{:S(2)}) async-start(s8[4718592]{0:T(1024)(128)(4,1)} %bitcast.168), calls=%async_computation.4 | async-start | bytes 1048576
  193.3 6.2 %copy-start.16 = (bf16[784,768]{1,0:T(8,128)(2,1)S(1)}, bf16[784,768]{1,0:T(8,128)(2,1)}, u32[]{:S(2)}) copy-start(bf16[784,768]{1,0:T(8,128)(2,1)} %param.15) | copy-start | bytes 3612676
  233.8 15.6 %copy-start.13 = (f32[784,4,192]{0,2,1:T(8,128)S(1)}, f32[784,4,192]{0,2,1:T(8,128)}, u32[]{:S(2)}) copy-start(f32[784,4,192]{0,2,1:T(8,128)} %copy.80) | copy-start | bytes 7225348
  274.6 27.9 %copy-start.1 = (f32[784,4,192]{0,2,1:T(8,128)S(1)}, f32[784,4,192]{0,2,1:T(8,128)}, u32[]{:S(2)}) copy-start(f32[784,4,192]{0,2,1:T(8,128)} %copy-done) | copy-start | bytes 7225348
  274.6 27.9 %copy-start.26 = (f32[12,64]{1,0:T(8,128)S(1)}, f32[12,64]{1,0:T(8,128)}, u32[]{:S(2)}) copy-start(f32[12,64]{1,0:T(8,128)} %copy-done.25) | copy-start | bytes 9220
  302.5 10.1 %copy-start.11 = (bf16[784,4,192]{0,2,1:T(8,128)(2,1)S(1)}, bf16[784,4,192]{0,2,1:T(8,128)(2,1)}, u32[]{:S(2)}) copy-start(bf16[784,4,192]{0,2,1:T(8,128)(2,1)} %copy.82) | copy-start | bytes 3612676
  312.7 10.8 %copy-start.17 = (bf16[784,768]{1,0:T(8,128)(2,1)S(1)}, bf16[784,768]{1,0:T(8,128)(2,1)}, u32[]{:S(2)}) copy-start(bf16[784,768]{1,0:T(8,128)(2,1)} %param.15) | copy-start | bytes 3612676
  323.5 9.2 %copy-start.18 = (bf16[4,768,192]{1,2,0:T(8,128)(2,1)S(1)}, bf16[4,768,192]{1,2,0:T(8,128)(2,1)}, u32[]{:S(2)}) copy-start(bf16[4,768,192]{1,2,0:T(8,128)(2,1)} %fusion.48) | copy-start | bytes 3538948
  350.0 6.1 %copy-start.12 = (bf16[4,768,192]{2,1,0:T(8,128)(2,1)S(1)}, bf16[4,768,192]{2,1,0:T(8,128)(2,1)}, u32[]{:S(2)}) copy-start(bf16[4,768,192]{2,1,0:T(8,128)(2,1)} %copy.101) | copy-start | bytes 3538948
  369.7 5.0 copy-start.21
  369.7 9.6 %copy-start.15 = (bf16[784,4,192]{2,0,1:T(8,128)(2,1)S(1)}, bf16[784,4,192]{2,0,1:T(8,128)(2,1)}, u32[]{:S(2)}) copy-start(bf16[784,4,192]{2,0,1:T(8,128)(2,1)} %copy.92) | copy-start | bytes 3612676
  370.5 5.9 %copy-start.24 = (f32[9216]{0:T(1024)S(1)}, f32[9216]{0:T(1024)}, u32[]{:S(2)}) copy-start(f32[9216]{0:T(1024)} %param.21) | copy-start | bytes 110596
  370.5 5.8 %copy-start.29 = (f32[9216]{0:T(1024)S(1)}, f32[9216]{0:T(1024)}, u32[]{:S(2)}) copy-start(f32[9216]{0:T(1024)} %param.27) | copy-start | bytes 110596
  379.3 8.7 %copy-start.30 = (f32[9216]{0:T(1024)S(1)}, f32[9216]{0:T(1024)}, u32[]{:S(2)}) copy-start(f32[9216]{0:T(1024)} %custom-call) | copy-start | bytes 110596
  379.3 8.8 %copy-start.42 = (f32[768]{0:T(1024)S(1)}, f32[768]{0:T(1024)}, u32[]{:S(2)}) copy-start(f32[768]{0:T(1024)} %get-tuple-element.60) | copy-start | bytes 9220
  379.3 8.8 %copy-start.41 = (f32[768]{0:T(1024)S(1)}, f32[768]{0:T(1024)}, u32[]{:S(2)}) copy-start(f32[768]{0:T(1024)} %get-tuple-element.66) | copy-start | bytes 9220
  379.3 8.8 %copy-start.37 = (f32[768]{0:T(1024)S(1)}, f32[768]{0:T(1024)}, u32[]{:S(2)}) copy-start(f32[768]{0:T(1024)} %get-tuple-element.68) | copy-start | bytes 9220
  379.3 8.8 %copy-start.36 = (f32[768]{0:T(1024)S(1)}, f32[768]{0:T(1024)}, u32[]{:S(2)}) copy-start(f32[768]{0:T(1024)} %get-tuple-element.75) | copy-start | bytes 9220
  379.3 48.1 %copy-start.35 = (f32[784]{0:T(1024)S(1)}, f32[784]{0:T(1024)}, u32[]{:S(2)}) copy-start(f32[784]{0:T(1024)} %copy-done.33) | copy-start | bytes 9412
  (19 other events, 69.6 us)
Sparse Core Ops, SparseCore 0:
  11.5 105.9 all-gather.2
  369.8 160.8 reduce-scatter.1

commit v2 on v1

--- a/solution.py
+++ b/solution.py
@@ -1,12 +1,289 @@
 import jax
 import jax.numpy as jnp
 from jax import lax
+from jax.experimental import pallas as pl
+from jax.experimental.pallas import tpu as pltpu
 from jax.sharding import PartitionSpec as P
 
 HD = 64
 BOTH = ("dp", "tensor")
 F32 = jnp.float32
 BF16 = jnp.bfloat16
+MESH = pl.DeviceIdType.MESH
+NCH = 9
+HALF = 48
+
+
+class Place:
+    def __init__(self):
+        d, t = lax.axis_index("dp"), lax.axis_index("tensor")
+        self.x, self.z = lax.rem(d, 2), lax.div(d, 2)
+        self.c, self.y = lax.rem(t, 2), lax.div(t, 2)
+        self.core = (d, t + 1 - 2 * self.c)
+        self.ynb = (d, lax.rem(t + 2, 4))
+        self.xnb = (d + 1 - 2 * self.x, t)
+        self.zup = (lax.rem(d + 2, 8), t)
+        self.zdn = (lax.rem(d + 6, 8), t)
+
+    def zrel(self, s):
+        return lax.rem(self.z + 4 - s, 4)
+
+    def barrier(self):
+        bar = pltpu.get_barrier_semaphore()
+        near = (self.core, self.ynb, self.xnb, self.zup, self.zdn)
+        for dev in near:
+            pl.semaphore_signal(bar, inc=1, device_id=dev, device_id_type=MESH)
+        pl.semaphore_wait(bar, len(near))
+
+
+class Gather:
+    def __init__(self, p, own, w, ss, rs):
+        self.p, self.own, self.w, self.ss, self.rs = p, own, w, ss, rs
+
+    def copy(self, src, dst, n, k, dev):
+        return pltpu.make_async_remote_copy(
+            src, dst, send_sem=self.ss.at[n, k], recv_sem=self.rs.at[n, k], device_id=dev, device_id_type=MESH
+        )
+
+    def part(self, n, k):
+        p, w = self.p, self.w
+        x, y, c, z = p.x, p.y, p.c, p.z
+        lo, hi = pl.ds(0, HALF), pl.ds(HALF, HALF)
+        if k < 3:
+            src = self.own.at[n] if k == 0 else w.at[n, y, c, p.zrel(k), x]
+            return src, w.at[n, y, c, p.zrel(k), x], w.at[n, y, c, p.zrel(k + 1), x], p.zup
+        line = lambda yy, cc, xx: w.at[n, yy, cc, :, xx]
+        if k == 3:
+            return line(y, c, x), line(y, c, x), line(y, c, 1 - x), p.xnb
+        if k == 4:
+            return line(y, c, x), line(y, c, x), line(1 - y, c, x), p.ynb
+        if k == 5:
+            return line(y, c, x), line(y, c, x), line(y, 1 - c, x), p.core
+        if k == 6:
+            s = w.at[n, y, c, :, 1 - x, lo]
+            return s, s, w.at[n, 1 - y, c, :, 1 - x, lo], p.ynb
+        if k == 7:
+            return line(y, c, 1 - x), line(y, c, 1 - x), line(y, 1 - c, 1 - x), p.core
+        if k == 8:
+            s = w.at[n, 1 - y, c, :, x, hi]
+            return s, s, w.at[n, 1 - y, c, :, 1 - x, hi], p.xnb
+        if k == 9:
+            return line(1 - y, c, x), line(1 - y, c, x), line(1 - y, 1 - c, x), p.core
+        return line(1 - y, c, 1 - x), line(1 - y, c, 1 - x), line(1 - y, 1 - c, 1 - x), p.core
+
+    def start(self, n, k):
+        src, dst, _, dev = self.part(n, k)
+        self.copy(src, dst, n, k, dev).start()
+
+    def arrive(self, n, k):
+        _, _, mine, dev = self.part(n, k)
+        self.copy(mine, mine, n, k, dev).wait_recv()
+
+    def sent(self, n, k):
+        src, dst, _, dev = self.part(n, k)
+        self.copy(src, dst, n, k, dev).wait_send()
+
+    def stage(self, n, s):
+        if s == 0:
+            self.start(n, 0)
+        elif s < 3:
+            self.arrive(n, s - 1)
+            self.start(n, s)
+        elif s == 3:
+            self.arrive(n, 2)
+            for k in (3, 4, 5):
+                self.start(n, k)
+        elif s == 4:
+            self.arrive(n, 3)
+            self.start(n, 6)
+            self.start(n, 7)
+            self.arrive(n, 4)
+            self.start(n, 8)
+            self.start(n, 9)
+        elif s == 5:
+            self.arrive(n, 6)
+            self.arrive(n, 8)
+            self.start(n, 10)
+        else:
+            for k in (5, 7, 9, 10):
+                self.arrive(n, k)
+
+    STAGES = 7
+    COPIES = 11
+
+    def finish(self, n):
+        for k in range(self.COPIES):
+            self.sent(n, k)
+
+
+class Scatter:
+    STAGES = 7
+    COPIES = 8
+
+    def __init__(self, p, g, out, rc, rd, rl, rz, ss, rs):
+        self.p, self.g, self.out, self.rc, self.rd, self.rl, self.rz = p, g, out, rc, rd, rl, rz
+        self.ss, self.rs = ss, rs
+
+    def part(self, n, k):
+        p, g = self.p, self.g
+        x, y, c = p.x, p.y, p.c
+        lo, hi = pl.ds(0, HALF), pl.ds(HALF, HALF)
+        if k == 0:
+            return g.at[n, :, 1 - c], self.rc.at[n], p.core
+        if k == 1:
+            return g.at[n, 1 - y, c, :, 1 - x, lo], self.rd.at[n, 0], p.ynb
+        if k == 2:
+            return g.at[n, 1 - y, c, :, 1 - x, hi], self.rd.at[n, 1], p.xnb
+        if k == 3:
+            return g.at[n, y, c, :, 1 - x], self.rl.at[n, 0], p.xnb
+        if k == 4:
+            return g.at[n, 1 - y, c, :, x], self.rl.at[n, 1], p.ynb
+        return g.at[n, y, c, p.zrel(k - 4), x], self.rz.at[n, k - 5], p.zup
+
+    def copy(self, n, k):
+        src, dst, dev = self.part(n, k)
+        return pltpu.make_async_remote_copy(
+            src, dst, send_sem=self.ss.at[n, k], recv_sem=self.rs.at[n, k], device_id=dev, device_id_type=MESH
+        )
+
+    def start(self, n, k):
+        self.copy(n, k).start()
+
+    def arrive(self, n, k):
+        self.copy(n, k).wait_recv()
+
+    def finish(self, n):
+        for k in range(self.COPIES):
+            self.copy(n, k).wait_send()
+
+    def add(self, ref, *others):
+        total = ref[...].astype(F32)
+        for o in others:
+            total += o[...].astype(F32)
+        ref[...] = total.astype(BF16)
+
+    def stage(self, n, s):
+        p, g = self.p, self.g
+        x, y, c = p.x, p.y, p.c
+        lo, hi = pl.ds(0, HALF), pl.ds(HALF, HALF)
+        if s == 0:
+            self.start(n, 0)
+        elif s == 1:
+            self.arrive(n, 0)
+            self.add(g.at[n, 1 - y, c, :, 1 - x], self.rc.at[n, 1 - y, :, 1 - x])
+            self.start(n, 1)
+            self.start(n, 2)
+            self.add(g.at[n, y, c], self.rc.at[n, y])
+            self.add(g.at[n, 1 - y, c, :, x], self.rc.at[n, 1 - y, :, x])
+        elif s == 2:
+            self.arrive(n, 1)
+            self.add(g.at[n, y, c, :, 1 - x, lo], self.rd.at[n, 0])
+            self.start(n, 3)
+            self.arrive(n, 2)
+            self.add(g.at[n, 1 - y, c, :, x, hi], self.rd.at[n, 1])
+            self.start(n, 4)
+        elif s == 3:
+            self.arrive(n, 3)
+            self.arrive(n, 4)
+            self.add(g.at[n, y, c, :, x], self.rl.at[n, 0], self.rl.at[n, 1])
+            self.start(n, 5)
+        elif s < 6:
+            self.arrive(n, s + 1)
+            self.add(g.at[n, y, c, p.zrel(s - 2), x], self.rz.at[n, s - 4])
+            self.start(n, s + 2)
+        else:
+            self.arrive(n, 7)
+            self.out[n] = g[n, y, c, p.z, x].astype(F32) + self.rz[n, 2].astype(F32)
+
+
+WSHAPE = (NCH, 2, 2, 4, 2, 96, 256)
+
+
+def scatter_scratch():
+    return [
+        pltpu.VMEM((NCH, 2, 4, 2, 96, 256), BF16),
+        pltpu.VMEM((NCH, 2, 4, HALF, 256), BF16),
+        pltpu.VMEM((NCH, 2, 4, 96, 256), BF16),
+        pltpu.VMEM((NCH, 3, 96, 256), BF16),
+        pltpu.SemaphoreType.DMA((NCH, Scatter.COPIES)),
+        pltpu.SemaphoreType.DMA((NCH, Scatter.COPIES)),
+    ]
+
+
+def wave(engine, count, depth):
+    for tick in range(count + engine.STAGES - 1):
+        for s in reversed(range(engine.STAGES)):
+            n = tick - s
+            if 0 <= n < count:
+                engine.stage(n, s)
+
+
+def gather_kernel(own, w, ss, rs):
+    p = Place()
+    p.barrier()
+    gather = Gather(p, own, w, ss, rs)
+    for n in range(NCH):
+        w[n, p.y, p.c, p.z, p.x] = own[n]
+    wave(gather, NCH, 1)
+    for n in range(NCH):
+        gather.finish(n)
+
+
+def scatter_kernel(g_in, out, g, rc, rd, rl, rz, ss, rs, ls):
+    p = Place()
+    local = pltpu.make_async_copy(g_in, g, ls)
+    local.start()
+    p.barrier()
+    local.wait()
+    engine = Scatter(p, g, out, rc, rd, rl, rz, ss, rs)
+    wave(engine, NCH, 1)
+    for n in range(NCH):
+        engine.finish(n)
+
+
+def gather_call(own):
+    return pl.pallas_call(
+        gather_kernel,
+        out_shape=jax.ShapeDtypeStruct(WSHAPE, BF16),
+        in_specs=[pl.BlockSpec(memory_space=pltpu.VMEM)],
+        out_specs=pl.BlockSpec(memory_space=pltpu.VMEM),
+        scratch_shapes=[pltpu.SemaphoreType.DMA((NCH, Gather.COPIES)), pltpu.SemaphoreType.DMA((NCH, Gather.COPIES))],
+        compiler_params=pltpu.CompilerParams(collective_id=0, has_side_effects=True, vmem_limit_bytes=60 << 20),
+    )(own)
+
+
+def scatter_call(g):
+    return pl.pallas_call(
+        scatter_kernel,
+        out_shape=jax.ShapeDtypeStruct((NCH, 96, 256), F32),
+        in_specs=[pl.BlockSpec(memory_space=pl.ANY)],
+        out_specs=pl.BlockSpec(memory_space=pltpu.VMEM),
+        scratch_shapes=[pltpu.VMEM(WSHAPE, BF16)] + scatter_scratch() + [pltpu.SemaphoreType.DMA],
+        compiler_params=pltpu.CompilerParams(collective_id=1, has_side_effects=True, vmem_limit_bytes=60 << 20),
+    )(g)
+
+
+def to_chunks(blocks):
+    b, r, c = blocks.shape
+    cut = blocks.reshape(b, r, 3, c // 3).transpose(0, 2, 1, 3)
+    return jnp.concatenate([cut[0], cut[1:].transpose(1, 0, 2, 3).reshape(6, r, c // 3)])
+
+
+def from_chunks(chunks):
+    r, c = chunks.shape[1:]
+    rest = chunks[3:].reshape(3, 2, r, c).transpose(1, 0, 2, 3)
+    return jnp.concatenate([chunks[None, :3], rest]).transpose(0, 2, 1, 3).reshape(3, r, 3 * c)
+
+
+def ring_gather(shards):
+    w = gather_call(to_chunks(shards))
+    w = w.reshape(NCH, 4, 768, 256)
+    return jnp.stack([from_chunks(w[:, t]) for t in range(4)], axis=1)
+
+
+def ring_scatter(blocks):
+    g = jnp.stack([to_chunks(blocks[:, t]) for t in range(4)], axis=1)
+    return from_chunks(scatter_call(g.reshape(WSHAPE)))
 
 
 def unpack(vectors, d, ff):
@@ -174,11 +451,13 @@
         target_vectors,
     ):
         patches = block_patches[lax.axis_index("tensor")]
-        blocks = gather_blocks(pack_shards(qkv, out, up, down), dp, tensor)
+        ringed = dp == 8 and tensor == 4
+        shards = pack_shards(qkv, out, up, down)
+        blocks = ring_gather(shards) if ringed else gather_blocks(shards, dp, tensor)
         output, grad_tokens, grads, sums = local_layer(
             tokens, cotangent, patches, blocks, vectors
         )
-        grads = scatter_blocks(grads, dp, tensor).astype(F32)
+        grads = ring_scatter(grads) if ringed else scatter_blocks(grads, dp, tensor).astype(F32)
         sums = lax.psum(sums, BOTH)
         w = qkv.shape[2]
         rate = momentum[0]

time: 552 us -> 603 us (1.092)
  waiting for transfers between devices: 191 us -> 0 us
  Pallas kernels: 0 us -> 183 us
  local copies, waits for them, and re-layouts: 64.2 us -> 117 us
  other arithmetic: 56.6 us -> 86.4 us
  between operations: 16.5 us -> 3.2 us
    pallas_call x0 -> x2, Pallas kernels: none -> 183 us  [the longest x1 94 us: gather_call(): pl.pallas_call(gather_kernel, out_shape=jax.ShapeDtypeStruct(WSHAPE, BF16...]
    all_gather x1 -> x0, waiting for transfers between devices: 100 us -> none  [gather_blocks(): every = lax.all_gather(shards, BOTH, axis=0)]
    reduce_scatter x1 -> x0, waiting for transfers between devices: 90.7 us -> none  [scatter_blocks(): return lax.psum_scatter(pieces, BOTH, scatter_dimension=0, tiled=True)[0]]
    another operation x2 -> x7, other arithmetic: 1.9 us -> 26.9 us  [the longest x5 13.4 us: ring_scatter(): g = jnp.stack([to_chunks(blocks[:, t]) for t in range(4)], axis=1)]
    another operation x0 -> x9, local copies, waits for them, and re-layouts: none -> 22.2 us  [the longest x4 21.9 us: to_chunks(): cut = blocks.reshape(b, r, 3, c // 3).transpose(0, 2, 1, 3)]
    reshape x0 -> x5, local copies, waits for them, and re-layouts: none -> 15.7 us  [from_chunks(): rest = chunks[3:].reshape(3, 2, r, c).transpose(1, 0, 2, 3)]
    broadcast_in_dim x0 -> x7, local copies, waits for them, and re-layouts: none -> 14.2 us  [from_chunks(): chunks[None, :3]]
    concatenate x0 -> x6, other arithmetic: none -> 13.7 us  [the longest x4 12.8 us: from_chunks(): jnp.concatenate([chunks[None, :3], rest]).transpose(0, 2, 1, 3)]
  transfers between devices with their start and end apart: 2 -> 0, of which waited for: 2 -> 0; matrix products, arithmetic and copies ran while one was open for 7% -> 0% of each run, Pallas kernels for 0% -> 0%
where the time goes in v2:
time: 603 us; the launch traced here: 598 us
  Pallas kernels  183 us (30%)
  matrix products  169 us (28%)
  local copies, waits for them, and re-layouts  117 us (19%)
  other arithmetic  86.4 us (14%)
  blocking collectives  40.1 us (7%)
    pallas_call x1, Pallas kernels, gather_call(): pl.pallas_call(gather_kernel, out_shape=jax.ShapeDtypeStruct(WSHAPE, BF16...  94 us
    pallas_call x1, Pallas kernels, scatter_call(): pl.pallas_call(scatter_kernel, out_shape=jax.ShapeDtypeStruct((NCH, 96, 2...  88.9 us
    psum x1, blocking collectives, body(): sums = lax.psum(sums, BOTH)  40.1 us
    convert_element_type x1, other arithmetic, local_layer(): grad_scores = (soft * (grad_soft - jnp.sum(soft * grad_soft, axis=-1, kee...  27.9 us
    dot_general x1, matrix products, local_layer(): jnp.einsum('qhd,khd->hqk', grad_att, value, preferred_element_type=F32)  25.2 us
    another operation x4, local copies, waits for them, and re-layouts, to_chunks(): cut = blocks.reshape(b, r, 3, c // 3).transpose(0, 2, 1, 3)  21.9 us
    sub x1, matrix products, local_layer(): raised = jnp.exp(scores - jnp.max(scores, axis=-1, keepdims=True))  18.8 us
    dot_general x1, matrix products, local_layer(): jnp.einsum('hqk,khd->qhd', soft_low, value, preferred_element_type=F32)  15.9 us

profile of v2, /device:TPU:0, one launch (start us, length us, event | category | flops | bytes accessed | tf_op | source)
XLA Modules:
  0.0 598.2 jit_solution(9442134486762044387)
XLA Ops:
  18.9 94.0 %shard_map.229 = bf16[9,2,2,4,2,96,256]{6,5,4,3,2,1,0:T(8,128)(2,1)} custom-call(bf16[9,96,256]{2,1,0:T(8,128)(2,1)} %pad_maximum_fusion.10.own), custom_call_target="tpu_custom_call" | custom-call | tf_op jit(solution)/shard_map/pallas_call | solution.py:245
  112.9 4.3 slice_bitcast_fusion.22
  117.2 7.0 %fusion.74 = (bf16[6,1,768,256]{3,2,1,0:T(8,128)(2,1)}, bf16[6,1,768,256]{3,2,1,0:T(8,128)(2,1)S(1)}, bf16[6,1,768,256]{3,2,1,0:T(8,128)(2,1)}, bf16[6,1,768,256]{3,2,1,0:T(8,128)(2,1)}) fusion(bf16[9,4,768,256]{3,2,1,0:T(8,128)(2,1)} %bitcast.239), kind=kLoop, calls=%fused_computation.166 | loop fusion | bytes 18874368 | tf_op jit(solution)/shard_map/slice | solution.py:274
  124.2 4.3 copy.70
  145.9 4.3 copy.74
  150.2 4.1 pad_maximum_fusion.6
  154.3 4.3 copy.72
  180.5 4.6 copy.78
  185.1 18.8 %fusion.79 = (f32[12,784]{1,0:T(8,128)S(1)}, f32[12,784,784]{1,2,0:T(8,128)}) fusion(pred[784,784]{0,1:T(8,128)(4,1)S(1)} %copy-done.28, bf16[784,12,64]{0,2,1:T(8,128)(2,1)} %bitcast.272, f32[784,12,64]{0,2,1:T(8,128)S(1)} %bitcast.240, f32[12,64]{1,0:T(8,128)S(1)} %add.135), kind=kOutput, calls=%fused_computation.171 | convolution fusion | flops 974820096 | bytes 33771520 | tf_op jit(solution)/shard_map/sub | solution.py:361
  204.0 15.9 %fusion.46 = bf16[12,64,784]{2,1,0:T(8,128)(2,1)} fusion(f32[784,12,64]{0,2,1:T(8,128)} %bitcast.277, f32[12,64]{1,0:T(8,128)S(1)} %copy-done.51, f32[12,784,784]{1,2,0:T(8,128)} %get-tuple-element.80, f32[12,784]{1,0:T(8,128)S(1)} %get-tuple-element.79), kind=kOutput, calls=%fused_computation.98 | convolution fusion | flops 960669696 | bytes 33156864 | tf_op jit(solution)/shard_map/hqk,khd->qhd/dot_general | solution.py:364
  223.4 8.6 %multiply_convert_fusion.1 = (bf16[784,4,768]{2,0,1:T(8,128)(2,1)}, f32[784,4,768]{2,0,1:T(8,128)S(1)}) fusion(f32[4,768]{1,0:T(4,128)S(1)} %copy-done.50, bf16[3,4,768,768]{2,3,1,0:T(8,128)(2,1)} %copy-done, f32[784,768]{1,0:T(8,128)S(1)} %get-tuple-element.82, f32[768]{0:T(1024)S(1)} %copy-done.54, f32[768]{0:T(1024)S(1)} %copy-done.45, ...), kind=kOutput, calls=%fused_computation.21 | convolution fusion | flops 3716837376 | bytes 21602432 | tf_op jit(solution)/shard_map/rd,tdf->rtf/dot_general | solution.py:370
  232.0 10.0 %convert_reduce_fusion = (f32[4,768]{1,0:T(4,128)S(1)}, bf16[784,4,768]{2,0,1:T(8,128)(2,1)}) fusion(f32[784,4,768]{2,0,1:T(8,128)S(1)} %get-tuple-element.84, f32[4,768]{1,0:T(4,128)S(1)} %copy-done.50, bf16[784,768]{1,0:T(8,128)(2,1)S(1)} %copy-done.25, bf16[3,4,768,768]{2,3,1,0:T(8,128)(2,1)} %copy-done), kind=kOutput, calls=%fused_computation.20 | convolution fusion | flops 3730682880 | bytes 20398080 | tf_op jit(solution)/shard_map/rd,tdf->rtf/dot_general | solution.py:378
  242.6 8.8 %fusion.43 = bf16[784,768]{1,0:T(8,128)(2,1)} fusion(f32[784,768]{1,0:T(8,128)S(1)} %copy-done.16, bf16[784,4,768]{2,0,1:T(8,128)(2,1)} %get-tuple-element.83, bf16[3,4,768,768]{2,3,1,0:T(8,128)(2,1)} %copy-done, f32[768]{0:T(1024)S(1)} %copy-done.55), kind=kOutput, calls=%fused_computation.87 | convolution fusion | flops 3701182464 | bytes 13151232 | tf_op jit(solution)/shard_map/rtf,tdf->rd/dot_general | solution.py:375
  251.5 8.2 %fusion.41 = (f32[768]{0:T(1024)}, f32[784]{0:T(1024)S(1)}, f32[784]{0:T(1024)S(1)}, f32[768]{0:T(1024)}, f32[784,768,1]{1,0,2:T(8,128)S(1)}) fusion(f32[784,768]{1,0:T(8,128)S(1)} %copy-done.16, f32[784]{0:T(1024)S(1)} %add_rsqrt_fusion, f32[784]{0:T(1024)S(1)} %broadcast_multiply_fusion.4, f32[768]{0:T(1024)S(1)} %copy-done.45, ...), kind=kOutput, calls=%fused_computation.84 | convolution fusion | flops 3704792064 | bytes 14374144 | tf_op jit(solution)/shard_map/rtf,tdf->rd/dot_general | solution.py:382
  259.6 7.2 %convert_bitcast_fusion.1 = bf16[1,4,768,768]{2,3,1,0:T(8,128)(2,1)} fusion(bf16[784,4,768]{2,0,1:T(8,128)(2,1)S(1)} %copy-done.60, f32[784,768]{1,0:T(8,128)S(1)} %copy-done.16, f32[768]{0:T(1024)S(1)} %copy-done.54, f32[768]{0:T(1024)S(1)} %copy-done.45, f32[784]{0:T(1024)S(1)} %add_rsqrt_fusion, f32[784]{0:T(1024)S(1)} %broadcast_multiply_fusion.4), kind=kOutput, calls=%fused_computation.31 | convolution fusion | flops 3704745984 | bytes 11956352 | tf_op jit(solution)/shard_map/rd,rtf->tdf/dot_general | solution.py:381
  266.9 7.3 %convert_bitcast_fusion = bf16[1,4,768,768]{2,3,1,0:T(8,128)(2,1)} fusion(bf16[784,4,768]{2,0,1:T(8,128)(2,1)S(1)} %bitcast.298, bf16[784,768]{1,0:T(8,128)(2,1)S(1)} %copy-done.26), kind=kOutput, calls=%fused_computation.30 | convolution fusion | flops 3701735424 | bytes 10739712 | tf_op jit(solution)/shard_map/rd,rtf->tdf/dot_general | solution.py:380
  281.1 14.5 %convert_reduce_fusion.3 = (f32[12,64]{1,0:T(8,128)S(1)}, bf16[12,64,784]{2,1,0:T(8,128)(2,1)}) fusion(bf16[784,12,64]{0,2,1:T(8,128)(2,1)S(1)} %bitcast.283, f32[12,784,784]{1,2,0:T(8,128)} %get-tuple-element.80, f32[12,784]{1,0:T(8,128)S(1)} %get-tuple-element.79), kind=kOutput, calls=%fused_computation.63 | convolution fusion | flops 960668928 | bytes 31952640 | tf_op jit(solution)/shard_map/hqk,qhd->khd/dot_general | solution.py:389
  298.5 25.2 %multiply_reduce_fusion = (f32[12,784]{1,0:T(8,128)S(1)}, f32[12,784,784]{1,2,0:T(8,128)}) fusion(f32[12,784,784]{1,2,0:T(8,128)} %get-tuple-element.80, f32[12,784]{1,0:T(8,128)S(1)} %get-tuple-element.79, bf16[784,12,64]{0,2,1:T(8,128)(2,1)} %bitcast.284, f32[784,12,64]{0,2,1:T(8,128)S(1)} %bitcast.278, f32[12,64]{1,0:T(8,128)S(1)} %copy-done.51), kind=kOutput, calls=%fused_computation.2 | convolution fusion | flops 967434048 | bytes 62697984 | tf_op jit(solution)/shard_map/qhd,khd->hqk/dot_general | solution.py:390
  323.7 27.9 %multiply_convert_fusion = bf16[12,784,784]{1,2,0:T(8,128)(2,1)} fusion(f32[12,784,784]{1,2,0:T(8,128)} %get-tuple-element.87, f32[12,784]{1,0:T(8,128)S(1)} %get-tuple-element.86, f32[12,784,784]{1,2,0:T(8,128)} %get-tuple-element.80, f32[12,784]{1,0:T(8,128)S(1)} %get-tuple-element.79), kind=kLoop, calls=%fused_computation.1 | loop fusion | flops 29503488 | bytes 73833984 | tf_op jit(solution)/shard_map/convert_element_type | solution.py:393
  351.6 10.1 %multiply_convert_fusion.2 = bf16[12,64,784]{2,1,0:T(8,128)(2,1)} fusion(bf16[12,784,784]{1,2,0:T(8,128)(2,1)} %multiply_convert_fusion, f32[784,12,64]{0,2,1:T(8,128)S(1)} %bitcast.241, f32[12,64]{1,0:T(8,128)S(1)} %copy-done.37), kind=kOutput, calls=%fused_computation.65 | convolution fusion | flops 946520064 | bytes 18367488 | tf_op jit(solution)/shard_map/hqk,qhd->khd/dot_general | solution.py:397
  361.7 10.2 %convert_reduce_fusion.4 = (f32[12,64]{1,0:T(8,128)S(1)}, bf16[12,64,784]{2,1,0:T(8,128)(2,1)}) fusion(bf16[784,12,64]{0,2,1:T(8,128)(2,1)S(1)} %bitcast.273, bf16[12,784,784]{1,2,0:T(8,128)(2,1)} %multiply_convert_fusion), kind=kOutput, calls=%fused_computation.64 | convolution fusion | flops 946519296 | bytes 17163264 | tf_op jit(solution)/shard_map/hqk,khd->qhd/dot_general | solution.py:395
  376.5 9.1 %fusion.38 = (f32[768]{0:T(1024)S(1)}, f32[784]{0:T(1024)}, f32[784]{0:T(1024)S(1)}, f32[768]{0:T(1024)S(1)}, f32[784,768,1]{1,0,2:T(8,128)}) fusion(bf16[784,768]{1,0:T(8,128)(2,1)S(1)} %copy-done.12, f32[784]{0:T(1024)S(1)} %copy-done.47, f32[784]{0:T(1024)S(1)} %copy-done.41, f32[768]{0:T(1024)S(1)} %copy-done.44, bf16[4,768,768]{1,2,0:T(8,128)(2,1)} %copy-done.17, ...), kind=kOutput, calls=%fused_computation.76 | convolution fusion | flops 2791388160 | bytes 11588864 | tf_op jit(solution)/shard_map/rtc,tdc->rd/dot_general | solution.py:403
  385.5 4.9 convert_bitcast_fusion.2
  390.5 11.3 %pad_maximum_fusion.1 = bf16[3,4,768,768]{2,3,1,0:T(8,128)(2,1)} fusion(bf16[1,4,768,768]{2,3,1,0:T(8,128)(2,1)} %convert_bitcast_fusion, bf16[1,4,768,768]{2,3,1,0:T(8,128)(2,1)} %convert_bitcast_fusion.1, bf16[1,4,768,192]{2,3,1,0:T(8,128)(2,1)S(1)} %copy-done.27, bf16[1,4,768,576]{2,3,1,0:T(8,128)(2,1)S(1)} %convert_bitcast_fusion.2), kind=kLoop, calls=%fused_computation.12 | loop fusion | flops 56623104 | bytes 28311552 | tf_op jit(solution)/shard_map/stack | solution.py:409
  401.9 40.1 %psum.7 = f32[9216]{0:T(1024)} all-reduce(f32[9216]{0:T(1024)S(1)} %constant_dynamic-update-slice_fusion), channel_id=1, replica_groups=mesh['dp'=8,'tensor'=4] {'dp','tensor'}, use_global_device_ids=true, to_apply=%region_20.21 | all-reduce | flops 9216 | bytes 73728 | tf_op jit(solution)/shard_map/psum | solution.py:461
  442.0 9.1 %fusion.73 = (bf16[3,1,768,768]{2,3,1,0:T(8,128)(2,1)}, bf16[3,1,768,768]{2,3,1,0:T(8,128)(2,1)}, bf16[3,1,768,768]{2,3,1,0:T(8,128)(2,1)}, bf16[3,1,768,768]{2,3,1,0:T(8,128)(2,1)S(1)}) fusion(bf16[3,4,768,768]{2,3,1,0:T(8,128)(2,1)} %pad_maximum_fusion.1), kind=kLoop, calls=%fused_computation.165 | loop fusion | bytes 28311552 | tf_op jit(solution)/shard_map/slice | solution.py:285
  451.1 6.1 %copy.92 = bf16[3,768,3,256]{3,1,2,0:T(8,128)(2,1)} copy(bf16[3,768,3,256]{1,3,2,0:T(8,128)(2,1)} %bitcast.253) | data formatting | bytes 7077888 | tf_op jit(solution)/shard_map/reshape;squeeze | solution.py:268
  457.2 6.0 %copy.98 = bf16[3,768,3,256]{3,1,2,0:T(8,128)(2,1)} copy(bf16[3,768,3,256]{1,3,2,0:T(8,128)(2,1)} %bitcast.251) | data formatting | bytes 7077888 | tf_op jit(solution)/shard_map/reshape;squeeze | solution.py:268
  463.9 4.2 fusion.37
  474.3 6.1 %copy.96 = bf16[3,768,3,256]{3,1,2,0:T(8,128)(2,1)} copy(bf16[3,768,3,256]{1,3,2,0:T(8,128)(2,1)} %bitcast.243) | data formatting | bytes 7077888 | tf_op jit(solution)/shard_map/reshape;squeeze | solution.py:268
  496.9 6.7 %pad_maximum_fusion.2 = bf16[9,4,768,256]{3,2,1,0:T(8,128)(2,1)} fusion(bf16[9,1,768,256]{3,2,1,0:T(8,128)(2,1)S(1)} %copy-done.3, bf16[9,1,768,256]{3,2,1,0:T(8,128)(2,1)S(1)} %copy-done.8, bf16[9,1,768,256]{3,2,1,0:T(8,128)(2,1)S(1)} %maximum_bitcast_fusion.1, bf16[9,1,768,256]{3,2,1,0:T(8,128)(2,1)S(1)} %copy-done.5), kind=kLoop, calls=%fused_computation.13 | loop fusion | flops 21233664 | bytes 28311552 | tf_op jit(solution)/shard_map/stack | solution.py:285
  503.6 88.9 %shard_map.230 = f32[9,96,256]{2,1,0:T(8,128)} custom-call(bf16[9,2,2,4,2,96,256]{6,5,4,3,2,1,0:T(8,128)(2,1)} %bitcast.237), custom_call_target="tpu_custom_call" | custom-call | tf_op jit(solution)/shard_map/pallas_call | solution.py:256
  (233 shorter events, 103.3 us)
Async XLA Ops:
  0.6 13.5 %copy-start.31 = (bf16[768,96]{0,1:T(8,128)(2,1)S(1)}, bf16[768,96]{0,1:T(8,128)(2,1)}, u32[]{:S(2)}) copy-start(bf16[768,96]{0,1:T(8,128)(2,1)} %param.20) | copy-start | bytes 442372
  0.7 13.6 %copy-start.30 = (bf16[96,768]{1,0:T(8,128)(2,1)S(1)}, bf16[96,768]{1,0:T(8,128)(2,1)}, u32[]{:S(2)}) copy-start(bf16[96,768]{1,0:T(8,128)(2,1)} %param.19) | copy-start | bytes 442372
  0.7 12.3 %copy-start.35 = (bf16[192,96]{1,0:T(8,128)(2,1)S(1)}, bf16[192,96]{1,0:T(8,128)(2,1)}, u32[]{:S(2)}) copy-start(bf16[192,96]{1,0:T(8,128)(2,1)} %param.18) | copy-start | bytes 110596
  0.7 12.9 %copy-start.29 = (bf16[3,96,192]{2,1,0:T(8,128)(2,1)S(1)}, bf16[3,96,192]{2,1,0:T(8,128)(2,1)}, u32[]{:S(2)}) copy-start(bf16[3,96,192]{2,1,0:T(8,128)(2,1)} %param.17) | copy-start | bytes 331780
  0.7 12.2 %copy-start.38 = (f32[192,96]{1,0:T(8,128)S(1)}, f32[192,96]{1,0:T(8,128)}, u32[]{:S(2)}) copy-start(f32[192,96]{1,0:T(8,128)} %param.24) | copy-start | bytes 221188
  5.6 159.7 %copy-start.40 = (f32[784]{0:T(1024)}, f32[784]{0:T(1024)S(1)}, u32[]{:S(2)}) copy-start(f32[784]{0:T(1024)S(1)} %broadcast_multiply_fusion.5) | copy-start | bytes 9412
  10.8 154.6 %copy-start.43 = (f32[768]{0:T(1024)}, f32[768]{0:T(1024)S(1)}, u32[]{:S(2)}) copy-start(f32[768]{0:T(1024)S(1)} %get-tuple-element.78) | copy-start | bytes 9220
  10.8 174.3 %copy-start.36 = (f32[12,64]{1,0:T(8,128)}, f32[12,64]{1,0:T(8,128)S(1)}, u32[]{:S(2)}) copy-start(f32[12,64]{1,0:T(8,128)S(1)} %add.135) | copy-start | bytes 9220
  185.1 18.8 %copy-start.51 = (f32[12,64]{1,0:T(8,128)S(1)}, f32[12,64]{1,0:T(8,128)}, u32[]{:S(2)}) copy-start(f32[12,64]{1,0:T(8,128)} %add.131) | copy-start | bytes 9220
  204.0 15.9 %copy-start.11 = (bf16[784,768]{1,0:T(8,128)(2,1)S(1)}, bf16[784,768]{1,0:T(8,128)(2,1)}, u32[]{:S(2)}) copy-start(bf16[784,768]{1,0:T(8,128)(2,1)} %param.14) | copy-start | bytes 3612676
  204.0 15.9 %copy-start.56 = (f32[768]{0:T(1024)S(1)}, f32[768]{0:T(1024)}, u32[]{:S(2)}) copy-start(f32[768]{0:T(1024)} %get-tuple-element.74) | copy-start | bytes 9220
  222.9 9.1 %copy-start.15 = (f32[784,768]{1,0:T(8,128)}, f32[784,768]{1,0:T(8,128)S(1)}, u32[]{:S(2)}) copy-start(f32[784,768]{1,0:T(8,128)S(1)} %get-tuple-element.82) | copy-start | bytes 7225348
  223.4 8.6 %copy-start.25 = (bf16[784,768]{1,0:T(8,128)(2,1)S(1)}, bf16[784,768]{1,0:T(8,128)(2,1)}, u32[]{:S(2)}) copy-start(bf16[784,768]{1,0:T(8,128)(2,1)} %param.15) | copy-start | bytes 3612676
  232.0 10.6 %copy-start.16 = (f32[784,768]{1,0:T(8,128)S(1)}, f32[784,768]{1,0:T(8,128)}, u32[]{:S(2)}) copy-start(f32[784,768]{1,0:T(8,128)} %copy-done.15) | copy-start | bytes 7225348
  232.0 10.6 %copy-start.55 = (f32[768]{0:T(1024)S(1)}, f32[768]{0:T(1024)}, u32[]{:S(2)}) copy-start(f32[768]{0:T(1024)} %get-tuple-element.71) | copy-start | bytes 9220
  242.6 8.9 %copy-start.60 = (bf16[784,4,768]{2,0,1:T(8,128)(2,1)S(1)}, bf16[784,4,768]{2,0,1:T(8,128)(2,1)}, u32[]{:S(2)}) copy-start(bf16[784,4,768]{2,0,1:T(8,128)(2,1)} %get-tuple-element.94) | copy-start | bytes 14450692
  242.6 24.3 %slice-start.2 = ((s8[4816896]{0:T(1024)(128)(4,1)}), s8[4194304]{0:T(1024)(128)(4,1)S(1)}, s32[]{:S(2)}) async-start(s8[4816896]{0:T(1024)(128)(4,1)} %bitcast.297), calls=%async_computation.2 | async-start | bytes 8388608
  251.4 15.4 %slice-start.3 = ((s8[4816896]{0:T(1024)(128)(4,1)}), s8[622592]{0:T(1024)(128)(4,1)S(1)}, s32[]{:S(2)}) async-start(s8[4816896]{0:T(1024)(128)(4,1)} %bitcast.297), calls=%async_computation.3 | async-start | bytes 1245184
  259.6 7.3 %copy-start.26 = (bf16[784,768]{1,0:T(8,128)(2,1)S(1)}, bf16[784,768]{1,0:T(8,128)(2,1)}, u32[]{:S(2)}) copy-start(bf16[784,768]{1,0:T(8,128)(2,1)} %param.15) | copy-start | bytes 3612676
  323.7 27.9 %copy-start.2 = (f32[784,4,192]{0,2,1:T(8,128)S(1)}, f32[784,4,192]{0,2,1:T(8,128)}, u32[]{:S(2)}) copy-start(f32[784,4,192]{0,2,1:T(8,128)} %copy-done.1) | copy-start | bytes 7225348
  323.7 27.9 %copy-start.37 = (f32[12,64]{1,0:T(8,128)S(1)}, f32[12,64]{1,0:T(8,128)}, u32[]{:S(2)}) copy-start(f32[12,64]{1,0:T(8,128)} %copy-done.36) | copy-start | bytes 9220
  351.6 10.1 %copy-start.18 = (bf16[784,4,192]{0,2,1:T(8,128)(2,1)S(1)}, bf16[784,4,192]{0,2,1:T(8,128)(2,1)}, u32[]{:S(2)}) copy-start(bf16[784,4,192]{0,2,1:T(8,128)(2,1)} %copy.80) | copy-start | bytes 3612676
  361.7 10.2 %copy-start.13 = (bf16[12,64,784]{2,1,0:T(8,128)(2,1)S(1)}, bf16[12,64,784]{2,1,0:T(8,128)(2,1)}, u32[]{:S(2)}) copy-start(bf16[12,64,784]{2,1,0:T(8,128)(2,1)} %multiply_convert_fusion.2) | copy-start | bytes 3612676
  376.4 9.1 %copy-start.22 = (bf16[784,4,192]{2,0,1:T(8,128)(2,1)S(1)}, bf16[784,4,192]{2,0,1:T(8,128)(2,1)}, u32[]{:S(2)}) copy-start(bf16[784,4,192]{2,0,1:T(8,128)(2,1)} %copy.90) | copy-start | bytes 3612676
  376.4 9.1 %copy-start.23 = (bf16[784,4,192]{2,0,1:T(8,128)(2,1)S(1)}, bf16[784,4,192]{2,0,1:T(8,128)(2,1)}, u32[]{:S(2)}) copy-start(bf16[784,4,192]{2,0,1:T(8,128)(2,1)} %copy.89) | copy-start | bytes 3612676
  376.4 9.1 %copy-start.53 = (f32[768]{0:T(1024)S(1)}, f32[768]{0:T(1024)}, u32[]{:S(2)}) copy-start(f32[768]{0:T(1024)} %get-tuple-element.77) | copy-start | bytes 9220
  390.5 11.3 %copy-start.42 = (f32[9216]{0:T(1024)S(1)}, f32[9216]{0:T(1024)}, u32[]{:S(2)}) copy-start(f32[9216]{0:T(1024)} %custom-call) | copy-start | bytes 110596
  390.5 11.3 %copy-start.58 = (f32[768]{0:T(1024)S(1)}, f32[768]{0:T(1024)}, u32[]{:S(2)}) copy-start(f32[768]{0:T(1024)} %get-tuple-element.36) | copy-start | bytes 9220
  390.5 11.4 %copy-start.57 = (f32[768]{0:T(1024)S(1)}, f32[768]{0:T(1024)}, u32[]{:S(2)}) copy-start(f32[768]{0:T(1024)} %get-tuple-element.42) | copy-start | bytes 9220
  390.5 11.4 %copy-start.49 = (f32[768]{0:T(1024)S(1)}, f32[768]{0:T(1024)}, u32[]{:S(2)}) copy-start(f32[768]{0:T(1024)} %get-tuple-element.44) | copy-start | bytes 9220
  390.5 11.4 %copy-start.39 = (f32[3072]{0:T(1024)S(1)}, f32[3072]{0:T(1024)}, u32[]{:S(2)}) copy-start(f32[3072]{0:T(1024)} %reshape.317) | copy-start | bytes 36868
  390.5 11.4 %copy-start.48 = (f32[768]{0:T(1024)S(1)}, f32[768]{0:T(1024)}, u32[]{:S(2)}) copy-start(f32[768]{0:T(1024)} %get-tuple-element.60) | copy-start | bytes 9220
  (33 other events, 108.4 us)

commit v3 on v2

--- a/solution.py
+++ b/solution.py
@@ -1,3 +1,6 @@
+import functools
+import math
+
 import jax
 import jax.numpy as jnp
 from jax import lax
@@ -5,8 +8,6 @@
 from jax.experimental.pallas import tpu as pltpu
 from jax.sharding import PartitionSpec as P
 
-HD = 64
-BOTH = ("dp", "tensor")
 F32 = jnp.float32
 BF16 = jnp.bfloat16
 MESH = pl.DeviceIdType.MESH
@@ -24,13 +25,15 @@
         self.xnb = (d + 1 - 2 * self.x, t)
         self.zup = (lax.rem(d + 2, 8), t)
         self.zdn = (lax.rem(d + 6, 8), t)
+        self.zfar = (lax.rem(d + 4, 8), t)
+        self.zpair = self.z + 1 - 2 * lax.rem(self.z, 2)
 
     def zrel(self, s):
         return lax.rem(self.z + 4 - s, 4)
 
     def barrier(self):
         bar = pltpu.get_barrier_semaphore()
-        near = (self.core, self.ynb, self.xnb, self.zup, self.zdn)
+        near = (self.core, self.ynb, self.xnb, self.zup, self.zdn, self.zfar)
         for dev in near:
             pl.semaphore_signal(bar, inc=1, device_id=dev, device_id_type=MESH)
         pl.semaphore_wait(bar, len(near))
@@ -124,37 +127,38 @@
         self.p, self.g, self.out, self.rc, self.rd, self.rl, self.rz = p, g, out, rc, rd, rl, rz
         self.ss, self.rs = ss, rs
 
-    def part(self, n, k):
+    def part(self, m, k):
         p, g = self.p, self.g
+        n, o = self.chunk(m), lax.rem(m, 2)
         x, y, c = p.x, p.y, p.c
         lo, hi = pl.ds(0, HALF), pl.ds(HALF, HALF)
         if k == 0:
-            return g.at[n, :, 1 - c], self.rc.at[n], p.core
+            return g.at[n, :, 1 - c], self.rc.at[o], p.core
         if k == 1:
-            return g.at[n, 1 - y, c, :, 1 - x, lo], self.rd.at[n, 0], p.ynb
+            return g.at[n, 1 - y, c, :, 1 - x, lo], self.rd.at[o, 0], p.ynb
         if k == 2:
-            return g.at[n, 1 - y, c, :, 1 - x, hi], self.rd.at[n, 1], p.xnb
+            return g.at[n, 1 - y, c, :, 1 - x, hi], self.rd.at[o, 1], p.xnb
         if k == 3:
-            return g.at[n, y, c, :, 1 - x], self.rl.at[n, 0], p.xnb
+            return g.at[n, y, c, :, 1 - x], self.rl.at[o, 0], p.xnb
         if k == 4:
-            return g.at[n, 1 - y, c, :, x], self.rl.at[n, 1], p.ynb
-        return g.at[n, y, c, p.zrel(k - 4), x], self.rz.at[n, k - 5], p.zup
-
-    def copy(self, n, k):
-        src, dst, dev = self.part(n, k)
+            return g.at[n, 1 - y, c, :, x], self.rl.at[o, 1], p.ynb
+        return g.at[n, y, c, p.zrel(k - 4), x], self.rz.at[m, k - 5], p.zup
+
+    def copy(self, m, k):
+        src, dst, dev = self.part(m, k)
         return pltpu.make_async_remote_copy(
-            src, dst, send_sem=self.ss.at[n, k], recv_sem=self.rs.at[n, k], device_id=dev, device_id_type=MESH
+            src, dst, send_sem=self.ss.at[m, k], recv_sem=self.rs.at[m, k], device_id=dev, device_id_type=MESH
         )
 
-    def start(self, n, k):
-        self.copy(n, k).start()
-
-    def arrive(self, n, k):
-        self.copy(n, k).wait_recv()
-
-    def finish(self, n):
+    def start(self, m, k):
+        self.copy(m, k).start()
+
+    def arrive(self, m, k):
+        self.copy(m, k).wait_recv()
+
+    def finish(self, m):
         for k in range(self.COPIES):
-            self.copy(n, k).wait_send()
+            self.copy(m, k).wait_send()
 
     def add(self, ref, *others):
         total = ref[...].astype(F32)
@@ -162,128 +166,473 @@
             total += o[...].astype(F32)
         ref[...] = total.astype(BF16)
 
-    def stage(self, n, s):
+    def chunk(self, m):
+        return lax.rem(m + 3, NCH)
+
+    def stage(self, m, s):
         p, g = self.p, self.g
+        n, o = self.chunk(m), lax.rem(m, 2)
         x, y, c = p.x, p.y, p.c
         lo, hi = pl.ds(0, HALF), pl.ds(HALF, HALF)
         if s == 0:
-            self.start(n, 0)
+            self.start(m, 0)
         elif s == 1:
-            self.arrive(n, 0)
-            self.add(g.at[n, 1 - y, c, :, 1 - x], self.rc.at[n, 1 - y, :, 1 - x])
-            self.start(n, 1)
-            self.start(n, 2)
-            self.add(g.at[n, y, c], self.rc.at[n, y])
-            self.add(g.at[n, 1 - y, c, :, x], self.rc.at[n, 1 - y, :, x])
+            self.arrive(m, 0)
+            self.add(g.at[n, 1 - y, c, :, 1 - x], self.rc.at[o, 1 - y, :, 1 - x])
+            self.start(m, 1)
+            self.start(m, 2)
+            self.add(g.at[n, y, c], self.rc.at[o, y])
+            self.add(g.at[n, 1 - y, c, :, x], self.rc.at[o, 1 - y, :, x])
         elif s == 2:
-            self.arrive(n, 1)
-            self.add(g.at[n, y, c, :, 1 - x, lo], self.rd.at[n, 0])
-            self.start(n, 3)
-            self.arrive(n, 2)
-            self.add(g.at[n, 1 - y, c, :, x, hi], self.rd.at[n, 1])
-            self.start(n, 4)
+            self.arrive(m, 1)
+            self.add(g.at[n, y, c, :, 1 - x, lo], self.rd.at[o, 0])
+            self.start(m, 3)
+            self.arrive(m, 2)
+            self.add(g.at[n, 1 - y, c, :, x, hi], self.rd.at[o, 1])
+            self.start(m, 4)
         elif s == 3:
-            self.arrive(n, 3)
-            self.arrive(n, 4)
-            self.add(g.at[n, y, c, :, x], self.rl.at[n, 0], self.rl.at[n, 1])
-            self.start(n, 5)
+            self.arrive(m, 3)
+            self.arrive(m, 4)
+            self.add(g.at[n, y, c, :, x], self.rl.at[o, 0], self.rl.at[o, 1])
+            self.start(m, 5)
         elif s < 6:
-            self.arrive(n, s + 1)
-            self.add(g.at[n, y, c, p.zrel(s - 2), x], self.rz.at[n, s - 4])
-            self.start(n, s + 2)
+            self.arrive(m, s + 1)
+            self.add(g.at[n, y, c, p.zrel(s - 2), x], self.rz.at[m, s - 4])
+            self.start(m, s + 2)
         else:
-            self.arrive(n, 7)
-            self.out[n] = g[n, y, c, p.z, x].astype(F32) + self.rz[n, 2].astype(F32)
+            self.arrive(m, 7)
+            self.out[n] = g[n, y, c, p.z, x].astype(F32) + self.rz[m, 2].astype(F32)
 
 
 WSHAPE = (NCH, 2, 2, 4, 2, 96, 256)
-
-
-def scatter_scratch():
-    return [
-        pltpu.VMEM((NCH, 2, 4, 2, 96, 256), BF16),
-        pltpu.VMEM((NCH, 2, 4, HALF, 256), BF16),
-        pltpu.VMEM((NCH, 2, 4, 96, 256), BF16),
-        pltpu.VMEM((NCH, 3, 96, 256), BF16),
-        pltpu.SemaphoreType.DMA((NCH, Scatter.COPIES)),
-        pltpu.SemaphoreType.DMA((NCH, Scatter.COPIES)),
-    ]
-
-
-def wave(engine, count, depth):
-    for tick in range(count + engine.STAGES - 1):
-        for s in reversed(range(engine.STAGES)):
-            n = tick - s
-            if 0 <= n < count:
-                engine.stage(n, s)
-
-
-def gather_kernel(own, w, ss, rs):
+ROWS = 784
+DM = 768
+PARTS = ((0, 400), (400, 384))
+STEP = 112
+LOG2E = math.log2(math.e)
+CS = LOG2E / 8
+BIG = 1e30
+
+
+def nt(a, b):
+    return lax.dot_general(a, b, (((1,), (1,)), ((), ())), preferred_element_type=F32)
+
+
+def tn(a, b):
+    return lax.dot_general(a, b, (((0,), (0,)), ((), ())), preferred_element_type=F32)
+
+
+def nn(a, b):
+    return jnp.dot(a, b, preferred_element_type=F32)
+
+
+def split3(a):
+    one = a.astype(BF16)
+    rest = a - one.astype(F32)
+    two = rest.astype(BF16)
+    return one, two, (rest - two.astype(F32)).astype(BF16)
+
+
+def turn(a):
+    return pltpu.roll(a.astype(F32), 64, 1)
+
+
+def standard(values):
+    centred = values - jnp.mean(values, axis=-1, keepdims=True)
+    inverse = lax.rsqrt(jnp.mean(centred * centred, axis=-1, keepdims=True) + 1e-06)
+    return centred * inverse, inverse
+
+
+def norm_pull(grad, scaled, inverse, gain):
+    g = grad * gain
+    return inverse * (
+        g - jnp.mean(g, axis=-1, keepdims=True) - scaled * jnp.mean(g * scaled, axis=-1, keepdims=True)
+    )
+
+
+def gelu_slope(v):
+    cdf = 0.5 + 0.5 * lax.erf(v * math.sqrt(0.5))
+    return v * cdf, cdf + v * (jnp.exp(-0.5 * v * v) * (1.0 / math.sqrt(2.0 * math.pi)))
+
+
+def rows_of(i):
+    return pl.ds(pl.multiple_of(i * STEP, 16), STEP)
+
+
+def fold(values):
+    return jnp.sum(values.reshape(STEP // 8, 8, values.shape[1]), axis=0)
+
+
+class Layer:
+    def __init__(self, refs):
+        self.__dict__.update(refs)
+
+    def mat(self, n, y, c):
+        return self.w[n, y, c].reshape(DM, 256)
+
+    def put(self, n, y, c, value):
+        self.w[n, y, c] = value.astype(BF16).reshape(4, 2, 96, 256)
+
+    def masks(self):
+        row = lax.broadcasted_iota(jnp.int32, (ROWS, 128), 0)
+        lane = lax.broadcasted_iota(jnp.int32, (ROWS, 128), 1)
+        p = jnp.broadcast_to(self.pat[0:1, :], (ROWS, 128))
+        image = sum(jnp.where(row >= k * p, 1, 0) for k in (1, 2, 3))
+        same = jnp.where(image == lane - 64, 1.0, 0.0)
+        slot = (lane >= 64) & (lane < 68)
+        self.mq[...] = jnp.where(slot, (same - 1.0) * BIG, 0.0).astype(BF16)
+        self.mk[...] = jnp.where(slot, same, jnp.where((lane >= 68) & (lane < 71), 1.0, 0.0)).astype(BF16)
+
+    def norm1(self):
+        def step(i, _):
+            r = rows_of(i)
+            scaled, _ = standard(self.tok[r, :].astype(F32))
+            self.n1[r, :] = (scaled * self.vec[0:1, :] + self.vec[1:2, :]).astype(BF16)
+            return 0
+
+        lax.fori_loop(0, ROWS // STEP, step, 0)
+
+    def attend(self, i):
+        j, y = lax.div(i, 2), lax.rem(i, 2)
+        lane = lax.broadcasted_iota(jnp.int32, (ROWS, 128), 1)
+        left = lane < 64
+        out_halves = []
+        for c in range(2):
+            h = i * 2 + c
+            mixed = (nn(self.n1[...], self.mat(j, y, c)) + self.bias[h]).astype(BF16)
+            self.qa[h] = jnp.where(left, mixed[:, :128], self.mq[...])
+            self.ka[h] = jnp.where(left, mixed[:, 128:], self.mk[...])
+            self.va[h] = jnp.where(left, jnp.ones((), BF16), mixed[:, :128])
+            out_halves.append(self.mat(j, y, c)[:, 128:])
+        first = lax.broadcasted_iota(jnp.int32, (DM, 128), 1) < 64
+        self.ot[j, y] = jnp.where(first, turn(out_halves[0]), out_halves[1].astype(F32)).astype(BF16)
+        for r0, n in PARTS:
+            r = pl.ds(r0, n)
+            lanes = lax.broadcasted_iota(jnp.int32, (n, 128), 1)
+            results = []
+            for c in range(2):
+                h = i * 2 + c
+                q = self.qa[h, r, :]
+                s = nt(q, self.ka[h])
+                top = jnp.max(s, axis=1, keepdims=True) * CS
+                p = jnp.exp2(s * CS - top).astype(BF16)
+                a = nn(p, self.va[h])
+                total = pltpu.roll(a, 64, 1)
+                results.append(a * (1.0 / total))
+                h1, h2, h3 = split3((top + jnp.log2(total)) * (-1.0 / CS))
+                self.qa[h, r, :] = jnp.where(
+                    lanes == 68, h1, jnp.where(lanes == 69, h2, jnp.where(lanes == 70, h3, q))
+                )
+            pair = jnp.where(lanes < 64, pltpu.roll(results[0], 64, 1), results[1])
+            self.att[j, y, r, :] = pair.astype(BF16)
+
+    def pair(self, ref, j, r=slice(None)):
+        return jnp.concatenate([ref[j, 0, r, :], ref[j, 1, r, :]], axis=1)
+
+    def project(self):
+        for r0, n in PARTS:
+            r = pl.ds(r0, n)
+            total = sum(nt(self.pair(self.att, j, r), self.pair(self.ot, j)) for j in range(3))
+            self.res[r, :] = total + (self.tok[r, :].astype(F32) + self.vec[6:7, :])
+
+        def step(i, _):
+            r = rows_of(i)
+            v = self.res[r, :]
+            scaled, _ = standard(v)
+            self.n2[r, :] = (scaled * self.vec[2:3, :] + self.vec[3:4, :]).astype(BF16)
+            self.acc[r, :] = v + self.vec[11:12, :]
+            self.gn[r, :] = jnp.zeros((STEP, DM), F32)
+            return 0
+
+        lax.fori_loop(0, ROWS // STEP, step, 0)
+
+    def feed(self, i):
+        j, y = lax.div(i, 2), lax.rem(i, 2)
+        nb, nc = 3 + 2 * j, 4 + 2 * j
+        sums = [0.0, 0.0]
+        for r0, n in PARTS:
+            r = pl.ds(r0, n)
+            for c in range(2):
+                cols = slice(c * 256, c * 256 + 256)
+                pre = nn(self.n2[r, :], self.mat(nb, y, c)) + self.bias[12 + i * 2 + c]
+                up = nn(self.cot[r, :], self.mat(nc, y, c))
+                active, slope = gelu_slope(pre)
+                grad = (up * slope).astype(BF16)
+                self.act[r, cols] = active.astype(BF16)
+                self.gp[r, cols] = grad
+                sums[c] += jnp.sum(grad.astype(F32).reshape(n // 8, 8, 256), axis=0)
+            self.acc[r, :] += nt(self.act[r, 0:256], self.mat(nc, y, 0)) + nt(
+                self.act[r, 256:512], self.mat(nc, y, 1)
+            )
+            self.gn[r, :] += nt(self.gp[r, 0:256], self.mat(nb, y, 0)) + nt(
+                self.gp[r, 256:512], self.mat(nb, y, 1)
+            )
+        for c in range(2):
+            cols = slice(c * 256, c * 256 + 256)
+            self.hs[12 + i * 2 + c] = jnp.sum(sums[c], axis=0, keepdims=True)
+            self.put(nc, y, c, tn(self.cot[...], self.act[:, cols]))
+            self.put(nb, y, c, tn(self.n2[...], self.gp[:, cols]))
+
+    def residual_back(self):
+        self.vs[...] = jnp.zeros(self.vs.shape, F32)
+
+        def step(i, _):
+            r = rows_of(i)
+            self.out[r, :] = self.acc[r, :].astype(BF16)
+            scaled, inverse = standard(self.res[r, :])
+            g = self.gn[r, :]
+            ct = self.cot[r, :].astype(F32)
+            grad = ct + norm_pull(g, scaled, inverse, self.vec[2:3, :])
+            self.res[r, :] = grad
+            self.gb[r, :] = grad.astype(BF16)
+            self.gn[r, :] = jnp.zeros((STEP, DM), F32)
+            for k, v in ((2, g * scaled), (3, g), (4, grad), (5, ct)):
+                self.vs[k] += fold(v)
+            return 0
+
+        lax.fori_loop(0, ROWS // STEP, step, 0)
+
+    def attend_back(self, i):
+        j, y = lax.div(i, 2), lax.rem(i, 2)
+        lane = lax.broadcasted_iota(jnp.int32, (ROWS, 128), 1)
+        left = lane < 64
+        low = nn(self.gb[...], self.ot[j, y]).astype(BF16)
+        wide = low.astype(F32)
+        product = wide * self.att[j, y].astype(F32)
+        for c in range(2):
+            h = i * 2 + c
+            delta = jnp.sum(jnp.where(left == (c == 0), product, 0.0), axis=1, keepdims=True)
+            d1, d2, d3 = split3(jnp.broadcast_to(-delta, (ROWS, 128)))
+            moved = pltpu.roll(wide, 64, 1).astype(BF16) if c == 0 else low
+            none = jnp.zeros((), BF16)
+            extra = jnp.where(lane == 0, d1, jnp.where(lane == 1, d2, jnp.where(lane == 2, d3, none)))
+            self.da[...] = jnp.where(left, extra, moved)
+            dv = dk = 0.0
+            for r0, n in PARTS:
+                r = pl.ds(r0, n)
+                q, d = self.qa[h, r, :], self.da[r, :]
+                p = jnp.exp2(nt(q, self.ka[h]) * CS)
+                ds = (p * nt(d, self.va[h])).astype(BF16)
+                dv += tn(p.astype(BF16), d)
+                dk += tn(ds, q)
+                self.dq[c, r, 0:128] = (nn(ds, self.ka[h]) * 0.125).astype(BF16)
+            self.dq[c, :, 0:128] = jnp.where(left, self.dq[c, :, 0:128], dv.astype(BF16))
+            self.dq[c, :, 128:256] = jnp.where(left, (dk * 0.125).astype(BF16), none)
+            sums = jnp.sum(self.dq[c].astype(F32).reshape(ROWS // 8, 8, 256), axis=0)
+            self.hs[h] = jnp.sum(sums, axis=0, keepdims=True)
+        for r0, n in PARTS:
+            r = pl.ds(r0, n)
+            self.gn[r, :] += nt(self.dq[0, r, :], self.mat(j, y, 0)) + nt(
+                self.dq[1, r, :], self.mat(j, y, 1)
+            )
+        outg = tn(self.gb[...], self.att[j, y])
+        first = lax.broadcasted_iota(jnp.int32, (DM, 128), 1) < 64
+        for c in range(2):
+            g = tn(self.n1[...], self.dq[c])
+            mine = pltpu.roll(outg, 64, 1) if c == 0 else outg
+            self.put(j, y, c, jnp.concatenate([g[:, :128], jnp.where(first, g[:, 128:], mine)], axis=1))
+
+    def token_back(self):
+        def step(i, _):
+            r = rows_of(i)
+            scaled, inverse = standard(self.tok[r, :].astype(F32))
+            g = self.gn[r, :]
+            grad = self.res[r, :] + norm_pull(g, scaled, inverse, self.vec[0:1, :])
+            self.gtok[r, :] = grad.astype(BF16)
+            self.vs[0] += fold(g * scaled)
+            self.vs[1] += fold(g)
+            return 0
+
+        lax.fori_loop(0, ROWS // STEP, step, 0)
+
+    def collect(self):
+        for h in range(24):
+            self.vsum[h : h + 1, :] = self.hs[h]
+        for k in range(6):
+            row = jnp.sum(self.vs[k], axis=0, keepdims=True)
+            for b in range(3):
+                self.vsum[24 + 3 * k + b : 25 + 3 * k + b, :] = row[:, 256 * b : 256 * b + 256]
+        self.vsum[42:48, :] = jnp.zeros((6, 256), F32)
+
+
+def layer_scratch():
+    return dict(
+        w=pltpu.VMEM(WSHAPE, BF16),
+        n1=pltpu.VMEM((ROWS, DM), BF16),
+        n2=pltpu.VMEM((ROWS, DM), BF16),
+        gb=pltpu.VMEM((ROWS, DM), BF16),
+        qa=pltpu.VMEM((12, ROWS, 128), BF16),
+        ka=pltpu.VMEM((12, ROWS, 128), BF16),
+        va=pltpu.VMEM((12, ROWS, 128), BF16),
+        att=pltpu.VMEM((3, 2, ROWS, 128), BF16),
+        ot=pltpu.VMEM((3, 2, DM, 128), BF16),
+        res=pltpu.VMEM((ROWS, DM), F32),
+        acc=pltpu.VMEM((ROWS, DM), F32),
+        gn=pltpu.VMEM((ROWS, DM), F32),
+        mq=pltpu.VMEM((ROWS, 128), BF16),
+        mk=pltpu.VMEM((ROWS, 128), BF16),
+        act=pltpu.VMEM((ROWS, 512), BF16),
+        gp=pltpu.VMEM((ROWS, 512), BF16),
+        da=pltpu.VMEM((ROWS, 128), BF16),
+        dq=pltpu.VMEM((2, ROWS, 256), BF16),
+        vs=pltpu.VMEM((6, 8, DM), F32),
+        hs=pltpu.VMEM((24, 1, 256), F32),
+    )
+
+
+NAMES_IN = ("tok", "cot", "own", "vec", "bias", "pat")
+NAMES_OUT = ("out", "gtok", "gsh", "vsum")
+
+
+def slots_of(u):
+    late = u - 7
+    early_ok = (u >= 0) & (u <= 5)
+    late_ok = (late >= 0) & (late <= 4) & (lax.rem(jnp.maximum(late, 0), 2) == 0)
+    return jnp.where(early_ok, u, 6 + lax.div(jnp.maximum(late, 0), 2)), early_ok | late_ok
+
+
+def gather_slot(gather, t):
+    for s in reversed(range(gather.STAGES)):
+        n = t - s
+        if isinstance(t, int):
+            if 0 <= n < NCH:
+                gather.stage(n, s)
+        else:
+            pl.when((n >= 0) & (n < NCH))(functools.partial(gather.stage, n, s))
+
+
+def scatter_slot(scatter, t):
+    for s in reversed(range(scatter.STAGES)):
+        m, ok = slots_of(t - s)
+        pl.when(ok)(functools.partial(scatter.stage, m, s))
+
+
+class Totals:
+    def __init__(self, p, value, vr, ss, rs):
+        self.p, self.value, self.vr, self.ss, self.rs = p, value, vr, ss, rs
+        z1 = (lax.rem(p.zpair * 2 + p.x, 8), lax.axis_index("tensor"))
+        self.devs = (p.core, p.ynb, p.xnb, z1, p.zfar)
+
+    def copy(self, k):
+        src = self.vr.at[0, k]
+        return pltpu.make_async_remote_copy(
+            src, self.vr.at[1, k], send_sem=self.ss.at[k], recv_sem=self.rs.at[k],
+            device_id=self.devs[k], device_id_type=MESH,
+        )
+
+    def start(self, k, total):
+        self.vr[0, k] = total
+        self.copy(k).start()
+
+    def end(self, k):
+        self.copy(k).wait_recv()
+        return self.vr[0, k] + self.vr[1, k]
+
+
+def mega_kernel(names, *refs):
+    r = dict(zip(names, refs))
+    layer = Layer(r)
     p = Place()
     p.barrier()
-    gather = Gather(p, own, w, ss, rs)
+    gather = Gather(p, r["own"], r["w"], r["gss"], r["grs"])
+    scatter = Scatter(p, r["w"], r["gsh"], r["rc"], r["rd"], r["rl"], r["rz"], r["sss"], r["srs"])
+    totals = Totals(p, r["vsum"], r["vr"], r["vss"], r["vrs"])
+
     for n in range(NCH):
-        w[n, p.y, p.c, p.z, p.x] = own[n]
-    wave(gather, NCH, 1)
-    for n in range(NCH):
+        r["w"][n, p.y, p.c, p.z, p.x] = r["own"][n]
+    gather_slot(gather, 0)
+    layer.masks()
+    gather_slot(gather, 1)
+    layer.norm1()
+    lax.fori_loop(2, 6, lambda t, c: (gather_slot(gather, t), c)[1], 0)
+
+    def attend(i, _):
+        pl.when(lax.rem(i, 2) == 0)(lambda: gather_slot(gather, 6 + lax.div(i, 2)))
+        layer.attend(i)
+        return 0
+
+    lax.fori_loop(0, 6, attend, 0)
+    gather_slot(gather, jnp.int32(9))
+    layer.project()
+    gather_slot(gather, jnp.int32(10))
+
+    def feed(i, _):
+        @pl.when(lax.rem(i, 2) == 0)
+        def _():
+            gather.finish(3 + i)
+            gather.finish(4 + i)
+
+        layer.feed(i)
+        gather_slot(gather, 11 + i)
+        scatter_slot(scatter, i - 1)
+        return 0
+
+    lax.fori_loop(0, 6, feed, 0)
+    layer.residual_back()
+    scatter_slot(scatter, jnp.int32(5))
+    for n in range(3):
         gather.finish(n)
 
-
-def scatter_kernel(g_in, out, g, rc, rd, rl, rz, ss, rs, ls):
-    p = Place()
-    local = pltpu.make_async_copy(g_in, g, ls)
-    local.start()
-    p.barrier()
-    local.wait()
-    engine = Scatter(p, g, out, rc, rd, rl, rz, ss, rs)
-    wave(engine, NCH, 1)
-    for n in range(NCH):
-        engine.finish(n)
-
-
-def gather_call(own):
+    def back(i, _):
+        layer.attend_back(i)
+        scatter_slot(scatter, 6 + i)
+        return 0
+
+    lax.fori_loop(0, 6, back, 0)
+    layer.token_back()
+    layer.collect()
+    value = r["vsum"][...]
+    scatter_slot(scatter, jnp.int32(12))
+    for k in range(5):
+        totals.start(k, value)
+        scatter_slot(scatter, jnp.int32(13 + k))
+        value = totals.end(k)
+    r["vsum"][...] = value
+    lax.fori_loop(0, NCH, lambda m, c: (scatter.finish(m), c)[1], 0)
+    for k in range(5):
+        totals.copy(k).wait_send()
+
+
+def mega_scratch():
+    two = 2
+    return dict(
+        layer_scratch(),
+        rc=pltpu.VMEM((two, 2, 4, 2, 96, 256), BF16),
+        rd=pltpu.VMEM((two, 2, 4, HALF, 256), BF16),
+        rl=pltpu.VMEM((two, 2, 4, 96, 256), BF16),
+        rz=pltpu.VMEM((NCH, 3, 96, 256), BF16),
+        vr=pltpu.VMEM((2, 5, 48, 256), F32),
+        gss=pltpu.SemaphoreType.DMA((NCH, Gather.COPIES)),
+        grs=pltpu.SemaphoreType.DMA((NCH, Gather.COPIES)),
+        sss=pltpu.SemaphoreType.DMA((NCH, Scatter.COPIES)),
+        srs=pltpu.SemaphoreType.DMA((NCH, Scatter.COPIES)),
+        vss=pltpu.SemaphoreType.DMA((5,)),
+        vrs=pltpu.SemaphoreType.DMA((5,)),
+    )
+
+
+def mega_call(*args):
+    scratch = mega_scratch()
+    names = NAMES_IN + NAMES_OUT + tuple(scratch)
+    vm = pl.BlockSpec(memory_space=pltpu.VMEM)
+    shape = jax.ShapeDtypeStruct
     return pl.pallas_call(
-        gather_kernel,
-        out_shape=jax.ShapeDtypeStruct(WSHAPE, BF16),
-        in_specs=[pl.BlockSpec(memory_space=pltpu.VMEM)],
-        out_specs=pl.BlockSpec(memory_space=pltpu.VMEM),
-        scratch_shapes=[pltpu.SemaphoreType.DMA((NCH, Gather.COPIES)), pltpu.SemaphoreType.DMA((NCH, Gather.COPIES))],
-        compiler_params=pltpu.CompilerParams(collective_id=0, has_side_effects=True, vmem_limit_bytes=60 << 20),
-    )(own)
-
-
-def scatter_call(g):
-    return pl.pallas_call(
-        scatter_kernel,
-        out_shape=jax.ShapeDtypeStruct((NCH, 96, 256), F32),
-        in_specs=[pl.BlockSpec(memory_space=pl.ANY)],
-        out_specs=pl.BlockSpec(memory_space=pltpu.VMEM),
-        scratch_shapes=[pltpu.VMEM(WSHAPE, BF16)] + scatter_scratch() + [pltpu.SemaphoreType.DMA],
-        compiler_params=pltpu.CompilerParams(collective_id=1, has_side_effects=True, vmem_limit_bytes=60 << 20),
-    )(g)
-
-
-def to_chunks(blocks):
-    b, r, c = blocks.shape
-    cut = blocks.reshape(b, r, 3, c // 3).transpose(0, 2, 1, 3)
-    return jnp.concatenate([cut[0], cut[1:].transpose(1, 0, 2, 3).reshape(6, r, c // 3)])
-
-
-def from_chunks(chunks):
-    r, c = chunks.shape[1:]
-    rest = chunks[3:].reshape(3, 2, r, c).transpose(1, 0, 2, 3)
-    return jnp.concatenate([chunks[None, :3], rest]).transpose(0, 2, 1, 3).reshape(3, r, 3 * c)
-
-
-def ring_gather(shards):
-    w = gather_call(to_chunks(shards))
-    w = w.reshape(NCH, 4, 768, 256)
-    return jnp.stack([from_chunks(w[:, t]) for t in range(4)], axis=1)
-
-
-def ring_scatter(blocks):
-    g = jnp.stack([to_chunks(blocks[:, t]) for t in range(4)], axis=1)
-    return from_chunks(scatter_call(g.reshape(WSHAPE)))
+        functools.partial(mega_kernel, names),
+        out_shape=(
+            shape((ROWS, DM), BF16),
+            shape((ROWS, DM), BF16),
+            shape((NCH, 96, 256), F32),
+            shape((48, 256), F32),
+        ),
+        in_specs=[vm] * len(NAMES_IN),
+        out_specs=(vm,) * len(NAMES_OUT),
+        scratch_shapes=list(scratch.values()),
+        compiler_params=pltpu.CompilerParams(collective_id=0, has_side_effects=True, vmem_limit_bytes=62 << 20),
+    )(*args)
+
+
+HD = 64
+BOTH = ("dp", "tensor")
 
 
 def unpack(vectors, d, ff):
@@ -433,7 +782,74 @@
     return output, grad_tokens, grads, sums
 
 
+def own_chunks(qkv, out, up, down):
+    r = up.shape[0]
+    four = jnp.stack([a.reshape(r, 3, HD) for a in (qkv[0], qkv[2], qkv[1], out.T)], axis=2)
+    first = four.transpose(1, 0, 2, 3).reshape(3, r, 256)
+    rest = jnp.stack([up.reshape(r, 3, 256), down.T.reshape(r, 3, 256)])
+    return jnp.concatenate([first, rest.transpose(2, 0, 1, 3).reshape(6, r, 256)])
+
+
+def own_gradients(chunks):
+    r = chunks.shape[1]
+    four = chunks[:3].reshape(3, r, 4, HD)
+    qkv = jnp.stack([four[:, :, k].transpose(1, 0, 2).reshape(r, 192) for k in (0, 2, 1)])
+    out = four[:, :, 3].transpose(0, 2, 1).reshape(192, r)
+    rest = chunks[3:].reshape(3, 2, r, 256)
+    up = rest[:, 0].transpose(1, 0, 2).reshape(r, 768)
+    down = rest[:, 1].transpose(0, 2, 1).reshape(768, r)
+    return qkv, out, up, down
+
+
+def by_head(piece):
+    return piece.reshape(4, 3, HD).transpose(1, 0, 2).reshape(12, HD)
+
+
+def bias_rows(vectors):
+    rows = vectors.reshape(12, DM)
+    heads = jnp.concatenate([by_head(rows[4]), by_head(rows[5]), jnp.zeros((12, 128), F32)], axis=1)
+    units = rows[7:11].reshape(4, 3, 256).transpose(1, 0, 2).reshape(12, 256)
+    return jnp.concatenate([heads, units]).reshape(24, 1, 256)
+
+
+def vector_gradient(sums):
+    six = sums[24:42].reshape(6, DM)
+    heads = sums[:12, :128].reshape(3, 4, 2, HD).transpose(2, 1, 0, 3).reshape(2, DM)
+    units = sums[12:24].reshape(3, 4, 256).transpose(1, 0, 2).reshape(4, DM)
+    return jnp.concatenate([six[:4], heads, six[4:5], units, six[5:6]]).reshape(-1)
+
+
+def ringed(tokens, cotangent, patches, qkv, out, up, down, vectors):
+    output, grad_tokens, grads, sums = mega_call(
+        tokens,
+        cotangent,
+        own_chunks(qkv, out, up, down),
+        vectors.reshape(12, DM),
+        bias_rows(vectors),
+        jnp.full((8, 128), patches, jnp.int32),
+    )
+    return (output, grad_tokens) + own_gradients(grads) + (vector_gradient(sums),)
+
+
+def general(dp, tensor, tokens, cotangent, patches, qkv, out, up, down, vectors):
+    blocks = gather_blocks(pack_shards(qkv, out, up, down), dp, tensor)
+    output, grad_tokens, grads, sums = local_layer(tokens, cotangent, patches, blocks, vectors)
+    grads = scatter_blocks(grads, dp, tensor).astype(F32)
+    w = qkv.shape[2]
+    return (
+        output,
+        grad_tokens,
+        jnp.stack([grads[0][:, i * w : (i + 1) * w] for i in range(3)]),
+        grads[0][:, 3 * w :].T,
+        grads[1],
+        grads[2].T,
+        lax.psum(sums, BOTH),
+    )
+
+
 def make_body(dp, tensor):
+    layer = ringed if (dp, tensor) == (8, 4) else functools.partial(general, dp, tensor)
+
     def body(
         tokens,
         cotangent,
@@ -451,28 +867,13 @@
         target_vectors,
     ):
         patches = block_patches[lax.axis_index("tensor")]
-        ringed = dp == 8 and tensor == 4
-        shards = pack_shards(qkv, out, up, down)
-        blocks = ring_gather(shards) if ringed else gather_blocks(shards, dp, tensor)
-        output, grad_tokens, grads, sums = local_layer(
-            tokens, cotangent, patches, blocks, vectors
-        )
-        grads = ring_scatter(grads) if ringed else scatter_blocks(grads, dp, tensor).astype(F32)
-        sums = lax.psum(sums, BOTH)
-        w = qkv.shape[2]
+        results = layer(tokens, cotangent, patches, qkv, out, up, down, vectors)
         rate = momentum[0]
 
         def average(target, online):
             return rate * target + (1.0 - rate) * online.astype(F32)
 
-        return (
-            output,
-            grad_tokens,
-            jnp.stack([grads[0][:, i * w : (i + 1) * w] for i in range(3)]),
-            grads[0][:, 3 * w :].T,
-            grads[1],
-            grads[2].T,
-            sums,
+        return results + (
             average(target_qkv, qkv),
             average(target_out, out),
             average(target_up, up),

time: 603 us -> 218 us (0.36)
  matrix products: 169 us -> 0 us
  local copies, waits for them, and re-layouts: 117 us -> 14.4 us
  other arithmetic: 86.4 us -> 4.79 us
  blocking collectives: 40.1 us -> 0 us
  Pallas kernels: 183 us -> 197 us
    dot_general x16 -> x0, matrix products: 149 us -> none  [the longest x1 25.2 us: local_layer(): jnp.einsum('qhd,khd->hqk', grad_att, value, preferred_element_type=F32)]
    psum x1 -> x0, blocking collectives: 40.1 us -> none  [body(): sums = lax.psum(sums, BOTH)]
    convert_element_type x3 -> x0, other arithmetic: 32.2 us -> none  [the longest x1 27.9 us: local_layer(): grad_scores = (soft * (grad_soft - jnp.sum(soft * grad_soft, axis=-1, kee...]
    slice x17 -> x12, local copies, waits for them, and re-layouts: 32.8 us -> 1.96 us  [the longest x2 1.15 us: own_gradients(): four = chunks[:3].reshape(3, r, 4, HD)]
    another operation x8 -> x1, other arithmetic: 26.9 us -> 0.02 us  [own_gradients(): jnp.stack([four[:, :, k].transpose(1, 0, 2).reshape(r, 192) for k in (0,...]
    reshape x11, local copies, waits for them, and re-layouts: 23.7 us -> 2.23 us  [the longest x1 0.63 us: ringed(): vectors.reshape(12, DM)]
    another operation x9 -> x4, local copies, waits for them, and re-layouts: 22.2 us -> 2.15 us  [the longest x2 2 us: own_chunks(): rest = jnp.stack([up.reshape(r, 3, 256), down.T.reshape(r, 3, 256)])]
    sub x1 -> x0, matrix products: 18.8 us -> none  [local_layer(): raised = jnp.exp(scores - jnp.max(scores, axis=-1, keepdims=True))]
where the time goes in v3:
time: 218 us
  Pallas kernels  197 us (90%)
  local copies, waits for them, and re-layouts  14.4 us (7%)
  other arithmetic  4.79 us (2%)
    pallas_call x1, Pallas kernels, mega_call(): pl.pallas_call(functools.partial(mega_kernel, names), out_shape=(shape((R...  197 us
    unnamed x43, local copies, waits for them, and re-layouts  5.98 us

profile of v3, /device:TPU:0, one launch (start us, length us, event | category | flops | bytes accessed | tf_op | source)
XLA Modules:
  0.0 218.0 jit_solution(12013845367418804815)
XLA Ops:
  0.7 1.0 stack_reshape.20
  1.7 1.0 stack_reshape.19
  2.7 0.3 maximum_bitcast_fusion
  3.0 0.1 copy.54
  3.1 0.1 copy.53
  3.3 0.1 copy.52
  3.5 0.1 copy.43
  3.6 0.8 pad_maximum_fusion.refs_2_
  4.4 0.6 reshape.113.refs_3_
  5.4 0.6 reshape.117.refs_4_
  6.0 0.6 dynamic_slice.3
  6.6 1.2 broadcast_in_dim.7.refs_5_
  7.8 197.3 %shard_map.229 = (bf16[784,768]{1,0:T(8,128)(2,1)}, bf16[784,768]{1,0:T(8,128)(2,1)}, f32[9,96,256]{2,1,0:T(8,128)}, f32[48,256]{1,0:T(8,128)}) custom-call(bf16[784,768]{1,0:T(8,128)(2,1)} %refs_0_.1, bf16[784,768]{1,0:T(8,128)(2,1)} %refs_1_.1, bf16[9,96,256]{2,1,0:T(8,128)(2,1)} %pad_maximum_fusion.refs_2_, f32[12,768]{1,0:T(8,128)} %reshape.113.refs_3_, ...), custom_call_target="tpu_custom_call" | custom-call | tf_op jit(solution)/shard_map/pallas_call | solution.py:619
  205.1 1.0 slice.106
  206.1 0.2 copy.47
  206.3 0.7 fusion.1
  207.0 0.9 copy.51
  208.0 0.2 copy.55
  208.2 0.8 copy.57
  209.0 0.2 copy.56
  209.2 0.8 copy.58
  210.1 0.1 reshape.124
  210.2 0.2 concatenate.15
  210.4 0.6 reshape.127
  211.7 0.8 multiply_add_fusion.2
  212.5 0.7 multiply_add_fusion.3
  213.1 0.8 multiply_add_fusion.1
  213.9 0.8 multiply_add_fusion
  214.6 0.6 multiply_add_fusion.4
  215.3 1.0 copy.66
  216.3 0.7 copy-done
  217.0 1.0 copy.67
  (58 shorter events, 0.7 us)
Async XLA Ops:
  0.6 2.4 %copy-start.3 = (bf16[3,96,192]{2,1,0:T(8,128)(2,1)S(1)}, bf16[3,96,192]{2,1,0:T(8,128)(2,1)}, u32[]{:S(2)}) copy-start(bf16[3,96,192]{2,1,0:T(8,128)(2,1)} %param.17) | copy-start | bytes 331780
  1.7 1.7 copy-start.10
  3.0 1.4 copy-start.9
  3.4 2.6 %copy-start.14 = (s32[4]{0:T(128)S(1)}, s32[4]{0:T(128)}, u32[]{:S(2)}) copy-start(s32[4]{0:T(128)} %param.16) | copy-start | bytes 52
  206.1 1.8 copy-start.2
  208.2 1.8 copy-start.12
  208.2 3.5 %copy-start.6 = (f32[3,96,192]{2,1,0:T(8,128)S(1)}, f32[3,96,192]{2,1,0:T(8,128)}, u32[]{:S(2)}) copy-start(f32[3,96,192]{2,1,0:T(8,128)} %param.23) | copy-start | bytes 663556
  209.0 3.5 %copy-start.11 = (f32[192,96]{1,0:T(8,128)S(1)}, f32[192,96]{1,0:T(8,128)}, u32[]{:S(2)}) copy-start(f32[192,96]{1,0:T(8,128)} %param.24) | copy-start | bytes 221188
  209.2 3.9 %copy-start.4 = (bf16[96,768]{1,0:T(8,128)(2,1)S(1)}, bf16[96,768]{1,0:T(8,128)(2,1)}, u32[]{:S(2)}) copy-start(bf16[96,768]{1,0:T(8,128)(2,1)} %param.19) | copy-start | bytes 442372
  209.2 3.9 %copy-start.7 = (f32[96,768]{1,0:T(8,128)S(1)}, f32[96,768]{1,0:T(8,128)}, u32[]{:S(2)}) copy-start(f32[96,768]{1,0:T(8,128)} %param.25) | copy-start | bytes 884740
  210.0 3.9 %copy-start.5 = (bf16[768,96]{0,1:T(8,128)(2,1)S(1)}, bf16[768,96]{0,1:T(8,128)(2,1)}, u32[]{:S(2)}) copy-start(bf16[768,96]{0,1:T(8,128)(2,1)} %param.20) | copy-start | bytes 442372
  210.0 3.9 %copy-start.8 = (f32[768,96]{0,1:T(8,128)S(1)}, f32[768,96]{0,1:T(8,128)}, u32[]{:S(2)}) copy-start(f32[768,96]{0,1:T(8,128)} %param.26) | copy-start | bytes 884740
  211.7 3.0 %copy-start.13 = (f32[9216]{0:T(1024)S(1)}, f32[9216]{0:T(1024)}, u32[]{:S(2)}) copy-start(f32[9216]{0:T(1024)} %param.27) | copy-start | bytes 110596
  211.7 3.6 %copy-start.1 = (bf16[784,768]{1,0:T(8,128)(2,1)S(1)}, bf16[784,768]{1,0:T(8,128)(2,1)}, u32[]{:S(2)}) copy-start(bf16[784,768]{1,0:T(8,128)(2,1)} %get-tuple-element.59) | copy-start | bytes 3612676
  215.3 1.7 copy-start

commit v4 on v3

--- a/solution.py
+++ b/solution.py
@@ -40,6 +40,9 @@
 
 
 class Gather:
+    STAGES = 7
+    COPIES = 11
+
     def __init__(self, p, own, w, ss, rs):
         self.p, self.own, self.w, self.ss, self.rs = p, own, w, ss, rs
 
@@ -50,52 +53,54 @@
 
     def part(self, n, k):
         p, w = self.p, self.w
-        x, y, c, z = p.x, p.y, p.c, p.z
+        x, y, c = p.x, p.y, p.c
         lo, hi = pl.ds(0, HALF), pl.ds(HALF, HALF)
+        line = lambda yy, cc, xx: w.at[n, yy, cc, :, xx]
         if k < 3:
-            src = self.own.at[n] if k == 0 else w.at[n, y, c, p.zrel(k), x]
-            return src, w.at[n, y, c, p.zrel(k), x], w.at[n, y, c, p.zrel(k + 1), x], p.zup
-        line = lambda yy, cc, xx: w.at[n, yy, cc, :, xx]
+            return w.at[n, y, c, p.zrel(k), x], w.at[n, y, c, p.zrel(k + 1), x], p.zup
         if k == 3:
-            return line(y, c, x), line(y, c, x), line(y, c, 1 - x), p.xnb
+            return line(y, c, x), line(y, c, 1 - x), p.xnb
         if k == 4:
-            return line(y, c, x), line(y, c, x), line(1 - y, c, x), p.ynb
+            return line(y, c, x), line(1 - y, c, x), p.ynb
         if k == 5:
-            return line(y, c, x), line(y, c, x), line(y, 1 - c, x), p.core
+            return line(y, c, x), line(y, 1 - c, x), p.core
         if k == 6:
-            s = w.at[n, y, c, :, 1 - x, lo]
-            return s, s, w.at[n, 1 - y, c, :, 1 - x, lo], p.ynb
+            return w.at[n, y, c, :, 1 - x, lo], w.at[n, 1 - y, c, :, 1 - x, lo], p.ynb
         if k == 7:
-            return line(y, c, 1 - x), line(y, c, 1 - x), line(y, 1 - c, 1 - x), p.core
+            return line(y, c, 1 - x), line(y, 1 - c, 1 - x), p.core
         if k == 8:
-            s = w.at[n, 1 - y, c, :, x, hi]
-            return s, s, w.at[n, 1 - y, c, :, 1 - x, hi], p.xnb
+            return w.at[n, 1 - y, c, :, x, hi], w.at[n, 1 - y, c, :, 1 - x, hi], p.xnb
         if k == 9:
-            return line(1 - y, c, x), line(1 - y, c, x), line(1 - y, 1 - c, x), p.core
-        return line(1 - y, c, 1 - x), line(1 - y, c, 1 - x), line(1 - y, 1 - c, 1 - x), p.core
+            return line(1 - y, c, x), line(1 - y, 1 - c, x), p.core
+        return line(1 - y, c, 1 - x), line(1 - y, 1 - c, 1 - x), p.core
 
     def start(self, n, k):
-        src, dst, _, dev = self.part(n, k)
-        self.copy(src, dst, n, k, dev).start()
+        src, _, dev = self.part(n, k)
+        self.copy(src, src, n, k, dev).start()
+
+    def pass_on(self, n, s):
+        p = self.p
+        at = self.w.at[n, p.y, p.c, p.zrel(s), p.x]
+        src = self.own.at[n] if s == 0 else at
+        if s < 3:
+            self.copy(src, at, n, s, p.zup).start()
+        for k, dev in ((3, p.xnb), (4, p.ynb), (5, p.core)):
+            self.copy(src, at, n, k, dev).start()
 
     def arrive(self, n, k):
-        _, _, mine, dev = self.part(n, k)
+        _, mine, dev = self.part(n, k)
         self.copy(mine, mine, n, k, dev).wait_recv()
 
-    def sent(self, n, k):
-        src, dst, _, dev = self.part(n, k)
-        self.copy(src, dst, n, k, dev).wait_send()
+    def finish(self, n):
+        for k in range(self.COPIES):
+            src, _, dev = self.part(n, k)
+            self.copy(src, src, n, k, dev).wait_send()
 
     def stage(self, n, s):
-        if s == 0:
-            self.start(n, 0)
-        elif s < 3:
-            self.arrive(n, s - 1)
-            self.start(n, s)
-        elif s == 3:
-            self.arrive(n, 2)
-            for k in (3, 4, 5):
-                self.start(n, k)
+        if s < 4:
+            if s > 0:
+                self.arrive(n, s - 1)
+            self.pass_on(n, s)
         elif s == 4:
             self.arrive(n, 3)
             self.start(n, 6)
@@ -111,13 +116,6 @@
             for k in (5, 7, 9, 10):
                 self.arrive(n, k)
 
-    STAGES = 7
-    COPIES = 11
-
-    def finish(self, n):
-        for k in range(self.COPIES):
-            self.sent(n, k)
-
 
 class Scatter:
     STAGES = 7
@@ -129,7 +127,7 @@
 
     def part(self, m, k):
         p, g = self.p, self.g
-        n, o = self.chunk(m), lax.rem(m, 2)
+        n, o = self.chunk(m), m
         x, y, c = p.x, p.y, p.c
         lo, hi = pl.ds(0, HALF), pl.ds(HALF, HALF)
         if k == 0:
@@ -171,7 +169,7 @@
 
     def stage(self, m, s):
         p, g = self.p, self.g
-        n, o = self.chunk(m), lax.rem(m, 2)
+        n, o = self.chunk(m), m
         x, y, c = p.x, p.y, p.c
         lo, hi = pl.ds(0, HALF), pl.ds(HALF, HALF)
         if s == 0:
@@ -263,6 +261,10 @@
     return jnp.sum(values.reshape(STEP // 8, 8, values.shape[1]), axis=0)
 
 
+def head_slot(g):
+    return (g % 3) * 4 + g // 3
+
+
 class Layer:
     def __init__(self, refs):
         self.__dict__.update(refs)
@@ -273,10 +275,30 @@
     def put(self, n, y, c, value):
         self.w[n, y, c] = value.astype(BF16).reshape(4, 2, 96, 256)
 
+    def pack(self):
+        outt = self.wout[...].astype(F32).T
+        q, k, v = (self.qkv[a].astype(F32) for a in range(3))
+        for j in range(3):
+            cols, wide = slice(64 * j, 64 * j + 64), slice(256 * j, 256 * j + 256)
+            self.own[j] = jnp.concatenate([a[:, cols] for a in (q, v, k, outt)], axis=1).astype(BF16)
+            self.own[3 + 2 * j] = self.up[:, wide]
+            self.own[4 + 2 * j] = self.down[:, wide]
+
+    def prepare(self, t):
+        for k in range(12):
+            for b in range(6):
+                self.vec[k : k + 1, 128 * b : 128 * b + 128] = self.flat[6 * k + b : 6 * k + b + 1, :]
+        none = jnp.zeros((1, 128), F32)
+        for g in range(12):
+            cols = slice(64 * g, 64 * g + 64)
+            self.bias[head_slot(g)] = jnp.concatenate([self.vec[4:5, cols], self.vec[5:6, cols], none], axis=1)
+            self.bias[12 + head_slot(g)] = self.vec[7 + g // 3 : 8 + g // 3, 256 * (g % 3) : 256 * (g % 3) + 256]
+        self.patches = self.pat[t]
+
     def masks(self):
         row = lax.broadcasted_iota(jnp.int32, (ROWS, 128), 0)
         lane = lax.broadcasted_iota(jnp.int32, (ROWS, 128), 1)
-        p = jnp.broadcast_to(self.pat[0:1, :], (ROWS, 128))
+        p = jnp.full((ROWS, 128), self.patches, jnp.int32)
         image = sum(jnp.where(row >= k * p, 1, 0) for k in (1, 2, 3))
         same = jnp.where(image == lane - 64, 1.0, 0.0)
         slot = (lane >= 64) & (lane < 68)
@@ -346,7 +368,7 @@
 
         lax.fori_loop(0, ROWS // STEP, step, 0)
 
-    def feed(self, i):
+    def feed(self, i, pause):
         j, y = lax.div(i, 2), lax.rem(i, 2)
         nb, nc = 3 + 2 * j, 4 + 2 * j
         sums = [0.0, 0.0]
@@ -367,11 +389,13 @@
             self.gn[r, :] += nt(self.gp[r, 0:256], self.mat(nb, y, 0)) + nt(
                 self.gp[r, 256:512], self.mat(nb, y, 1)
             )
+        pause(0)
         for c in range(2):
             cols = slice(c * 256, c * 256 + 256)
             self.hs[12 + i * 2 + c] = jnp.sum(sums[c], axis=0, keepdims=True)
             self.put(nc, y, c, tn(self.cot[...], self.act[:, cols]))
             self.put(nb, y, c, tn(self.n2[...], self.gp[:, cols]))
+        pause(1)
 
     def residual_back(self):
         self.vs[...] = jnp.zeros(self.vs.shape, F32)
@@ -392,7 +416,7 @@
 
         lax.fori_loop(0, ROWS // STEP, step, 0)
 
-    def attend_back(self, i):
+    def attend_back(self, i, pause):
         j, y = lax.div(i, 2), lax.rem(i, 2)
         lane = lax.broadcasted_iota(jnp.int32, (ROWS, 128), 1)
         left = lane < 64
@@ -420,6 +444,7 @@
             self.dq[c, :, 128:256] = jnp.where(left, (dk * 0.125).astype(BF16), none)
             sums = jnp.sum(self.dq[c].astype(F32).reshape(ROWS // 8, 8, 256), axis=0)
             self.hs[h] = jnp.sum(sums, axis=0, keepdims=True)
+            pause(c)
         for r0, n in PARTS:
             r = pl.ds(r0, n)
             self.gn[r, :] += nt(self.dq[0, r, :], self.mat(j, y, 0)) + nt(
@@ -431,6 +456,7 @@
             g = tn(self.n1[...], self.dq[c])
             mine = pltpu.roll(outg, 64, 1) if c == 0 else outg
             self.put(j, y, c, jnp.concatenate([g[:, :128], jnp.where(first, g[:, 128:], mine)], axis=1))
+        pause(2)
 
     def token_back(self):
         def step(i, _):
@@ -477,10 +503,13 @@
         dq=pltpu.VMEM((2, ROWS, 256), BF16),
         vs=pltpu.VMEM((6, 8, DM), F32),
         hs=pltpu.VMEM((24, 1, 256), F32),
-    )
-
-
-NAMES_IN = ("tok", "cot", "own", "vec", "bias", "pat")
+        own=pltpu.VMEM((NCH, 96, 256), BF16),
+        vec=pltpu.VMEM((12, DM), F32),
+        bias=pltpu.VMEM((24, 1, 256), F32),
+    )
+
+
+NAMES_IN = ("tok", "cot", "qkv", "wout", "up", "down", "flat", "pat")
 NAMES_OUT = ("out", "gtok", "gsh", "vsum")
 
 
@@ -492,7 +521,7 @@
 
 
 def gather_slot(gather, t):
-    for s in reversed(range(gather.STAGES)):
+    for s in range(gather.STAGES):
         n = t - s
         if isinstance(t, int):
             if 0 <= n < NCH:
@@ -502,7 +531,7 @@
 
 
 def scatter_slot(scatter, t):
-    for s in reversed(range(scatter.STAGES)):
+    for s in range(scatter.STAGES):
         m, ok = slots_of(t - s)
         pl.when(ok)(functools.partial(scatter.stage, m, s))
 
@@ -538,9 +567,11 @@
     scatter = Scatter(p, r["w"], r["gsh"], r["rc"], r["rd"], r["rl"], r["rz"], r["sss"], r["srs"])
     totals = Totals(p, r["vsum"], r["vr"], r["vss"], r["vrs"])
 
+    layer.pack()
     for n in range(NCH):
         r["w"][n, p.y, p.c, p.z, p.x] = r["own"][n]
     gather_slot(gather, 0)
+    layer.prepare(lax.axis_index("tensor"))
     layer.masks()
     gather_slot(gather, 1)
     layer.norm1()
@@ -562,7 +593,7 @@
             gather.finish(3 + i)
             gather.finish(4 + i)
 
-        layer.feed(i)
+        layer.feed(i, lambda k: None)
         gather_slot(gather, 11 + i)
         scatter_slot(scatter, i - 1)
         return 0
@@ -574,7 +605,7 @@
         gather.finish(n)
 
     def back(i, _):
-        layer.attend_back(i)
+        layer.attend_back(i, lambda k: None)
         scatter_slot(scatter, 6 + i)
         return 0
 
@@ -594,12 +625,11 @@
 
 
 def mega_scratch():
-    two = 2
     return dict(
         layer_scratch(),
-        rc=pltpu.VMEM((two, 2, 4, 2, 96, 256), BF16),
-        rd=pltpu.VMEM((two, 2, 4, HALF, 256), BF16),
-        rl=pltpu.VMEM((two, 2, 4, 96, 256), BF16),
+        rc=pltpu.VMEM((NCH, 2, 4, 2, 96, 256), BF16),
+        rd=pltpu.VMEM((NCH, 2, 4, HALF, 256), BF16),
+        rl=pltpu.VMEM((NCH, 2, 4, 96, 256), BF16),
         rz=pltpu.VMEM((NCH, 3, 96, 256), BF16),
         vr=pltpu.VMEM((2, 5, 48, 256), F32),
         gss=pltpu.SemaphoreType.DMA((NCH, Gather.COPIES)),
@@ -624,11 +654,55 @@
             shape((NCH, 96, 256), F32),
             shape((48, 256), F32),
         ),
-        in_specs=[vm] * len(NAMES_IN),
+        in_specs=[vm] * (len(NAMES_IN) - 1) + [pl.BlockSpec(memory_space=pltpu.SMEM)],
         out_specs=(vm,) * len(NAMES_OUT),
         scratch_shapes=list(scratch.values()),
         compiler_params=pltpu.CompilerParams(collective_id=0, has_side_effects=True, vmem_limit_bytes=62 << 20),
     )(*args)
+
+
+def tail_kernel(names, *refs):
+    r = dict(zip(names, refs))
+    r["out"][...] = r["out_in"][...]
+    r["gtok"][...] = r["gtok_in"][...]
+    g = r["gsh"]
+    for j in range(3):
+        cols = slice(64 * j, 64 * j + 64)
+        for a, k in enumerate((0, 128, 64)):
+            r["gqkv"][a, :, cols] = g[j, :, k : k + 64]
+        r["gup"][:, 256 * j : 256 * j + 256] = g[3 + 2 * j]
+        r["gdown"][:, 256 * j : 256 * j + 256] = g[4 + 2 * j]
+        r["gout"][cols, :] = g[j, :, 128:256].T[64:128, :]
+    v, gv = r["vsum"], r["gvec"]
+    for k, row in enumerate((0, 1, 2, 3, 6, 11)):
+        for b in range(6):
+            gv[6 * row + b : 6 * row + b + 1, :] = v[24 + 3 * k + b // 2 : 25 + 3 * k + b // 2, 128 * (b % 2) : 128 * (b % 2) + 128]
+    for half in range(2):
+        for b in range(6):
+            two = [v[h : h + 1, 64 * half : 64 * half + 64] for h in (head_slot(2 * b), head_slot(2 * b + 1))]
+            gv[24 + 6 * half + b : 25 + 6 * half + b, :] = jnp.concatenate(two, axis=1)
+    for t in range(4):
+        for b in range(6):
+            row = 12 + (b // 2) * 4 + t
+            gv[42 + 6 * t + b : 43 + 6 * t + b, :] = v[row : row + 1, 128 * (b % 2) : 128 * (b % 2) + 128]
+    rate = r["rate"][0]
+    for name in ("qkv", "wout", "up", "down", "vec"):
+        r["next_" + name][...] = rate * r["target_" + name][...] + (1.0 - rate) * r[name][...].astype(F32)
+
+
+def tail_call(results, online, targets, momentum):
+    five = ("qkv", "wout", "up", "down", "vec")
+    ins = ("out_in", "gtok_in", "gsh", "vsum") + five + tuple("target_" + a for a in five) + ("rate",)
+    outs = ("out", "gtok", "gqkv", "gout", "gup", "gdown", "gvec") + tuple("next_" + a for a in five)
+    vm = pl.BlockSpec(memory_space=pltpu.VMEM)
+    shape = jax.ShapeDtypeStruct
+    like = [shape(a.shape, F32) for a in online]
+    return pl.pallas_call(
+        functools.partial(tail_kernel, ins + outs),
+        out_shape=[shape(results[0].shape, BF16), shape(results[1].shape, BF16)] + like + like,
+        in_specs=[vm] * 14 + [pl.BlockSpec(memory_space=pltpu.SMEM)],
+        out_specs=[vm] * 12,
+    )(*results, *online, *targets, momentum)
 
 
 HD = 64
@@ -782,53 +856,18 @@
     return output, grad_tokens, grads, sums
 
 
-def own_chunks(qkv, out, up, down):
-    r = up.shape[0]
-    four = jnp.stack([a.reshape(r, 3, HD) for a in (qkv[0], qkv[2], qkv[1], out.T)], axis=2)
-    first = four.transpose(1, 0, 2, 3).reshape(3, r, 256)
-    rest = jnp.stack([up.reshape(r, 3, 256), down.T.reshape(r, 3, 256)])
-    return jnp.concatenate([first, rest.transpose(2, 0, 1, 3).reshape(6, r, 256)])
-
-
-def own_gradients(chunks):
-    r = chunks.shape[1]
-    four = chunks[:3].reshape(3, r, 4, HD)
-    qkv = jnp.stack([four[:, :, k].transpose(1, 0, 2).reshape(r, 192) for k in (0, 2, 1)])
-    out = four[:, :, 3].transpose(0, 2, 1).reshape(192, r)
-    rest = chunks[3:].reshape(3, 2, r, 256)
-    up = rest[:, 0].transpose(1, 0, 2).reshape(r, 768)
-    down = rest[:, 1].transpose(0, 2, 1).reshape(768, r)
-    return qkv, out, up, down
-
-
-def by_head(piece):
-    return piece.reshape(4, 3, HD).transpose(1, 0, 2).reshape(12, HD)
-
-
-def bias_rows(vectors):
-    rows = vectors.reshape(12, DM)
-    heads = jnp.concatenate([by_head(rows[4]), by_head(rows[5]), jnp.zeros((12, 128), F32)], axis=1)
-    units = rows[7:11].reshape(4, 3, 256).transpose(1, 0, 2).reshape(12, 256)
-    return jnp.concatenate([heads, units]).reshape(24, 1, 256)
-
-
-def vector_gradient(sums):
-    six = sums[24:42].reshape(6, DM)
-    heads = sums[:12, :128].reshape(3, 4, 2, HD).transpose(2, 1, 0, 3).reshape(2, DM)
-    units = sums[12:24].reshape(3, 4, 256).transpose(1, 0, 2).reshape(4, DM)
-    return jnp.concatenate([six[:4], heads, six[4:5], units, six[5:6]]).reshape(-1)
-
-
-def ringed(tokens, cotangent, patches, qkv, out, up, down, vectors):
-    output, grad_tokens, grads, sums = mega_call(
-        tokens,
-        cotangent,
-        own_chunks(qkv, out, up, down),
-        vectors.reshape(12, DM),
-        bias_rows(vectors),
-        jnp.full((8, 128), patches, jnp.int32),
-    )
-    return (output, grad_tokens) + own_gradients(grads) + (vector_gradient(sums),)
+def flat_views(arrays):
+    qkv, out, up, down, vectors = arrays
+    return qkv, out, up, down.T, vectors.reshape(72, 128)
+
+
+def ringed(tokens, cotangent, block_patches, online, momentum, targets):
+    online, targets = flat_views(online), flat_views(targets)
+    results = mega_call(tokens, cotangent, *online, block_patches)
+    final = tail_call(results, online, targets, momentum)
+    return tuple(final[:2]) + tuple(
+        a.T if k == 3 else a.reshape(-1) if k == 4 else a for five in (final[2:7], final[7:]) for k, a in enumerate(five)
+    )
 
 
 def general(dp, tensor, tokens, cotangent, patches, qkv, out, up, down, vectors):
@@ -848,37 +887,15 @@
 
 
 def make_body(dp, tensor):
-    layer = ringed if (dp, tensor) == (8, 4) else functools.partial(general, dp, tensor)
-
-    def body(
-        tokens,
-        cotangent,
-        block_patches,
-        qkv,
-        out,
-        up,
-        down,
-        vectors,
-        momentum,
-        target_qkv,
-        target_out,
-        target_up,
-        target_down,
-        target_vectors,
-    ):
+    def body(tokens, cotangent, block_patches, qkv, out, up, down, vectors, momentum, *targets):
+        online = (qkv, out, up, down, vectors)
+        if (dp, tensor) == (8, 4):
+            return ringed(tokens, cotangent, block_patches, online, momentum, targets)
         patches = block_patches[lax.axis_index("tensor")]
-        results = layer(tokens, cotangent, patches, qkv, out, up, down, vectors)
+        results = general(dp, tensor, tokens, cotangent, patches, *online)
         rate = momentum[0]
-
-        def average(target, online):
-            return rate * target + (1.0 - rate) * online.astype(F32)
-
-        return results + (
-            average(target_qkv, qkv),
-            average(target_out, out),
-            average(target_up, up),
-            average(target_down, down),
-            average(target_vectors, vectors),
+        return results + tuple(
+            rate * target + (1.0 - rate) * weight.astype(F32) for target, weight in zip(targets, online)
         )
 
     return body

time: 218 us -> 186 us (0.85)
  local copies, waits for them, and re-layouts: 14.4 us -> 0 us
  Pallas kernels: 197 us -> 184 us
  other arithmetic: 4.79 us -> 0 us
    pallas_call x1, Pallas kernels: 197 us -> 180 us  [mega_call(): pl.pallas_call(functools.partial(mega_kernel, names), out_shape=(shape((R...]
    unnamed x43 -> x0, local copies, waits for them, and re-layouts: 5.98 us -> none
    pallas_call x0 -> x1, Pallas kernels: none -> 4.63 us  [tail_call(): pl.pallas_call(functools.partial(tail_kernel, ins + outs), out_shape=[sha...]
    add x5 -> x0, other arithmetic: 3.55 us -> none  [average(): return rate * target + (1.0 - rate) * online.astype(F32)]
    reshape x11 -> x0, local copies, waits for them, and re-layouts: 2.23 us -> none  [the longest x1 0.63 us: ringed(): vectors.reshape(12, DM)]
where the time goes in v4:
time: 186 us
  Pallas kernels  184 us (99%)
    pallas_call x1, Pallas kernels, mega_call(): pl.pallas_call(functools.partial(mega_kernel, names), out_shape=(shape((R...  180 us
    pallas_call x1, Pallas kernels, tail_call(): pl.pallas_call(functools.partial(tail_kernel, ins + outs), out_shape=[sha...  4.63 us

profile of v4, /device:TPU:0, one launch (start us, length us, event | category | flops | bytes accessed | tf_op | source)
XLA Modules:
  0.0 185.8 jit_solution(4692927630736753645)
XLA Ops:
  1.3 179.7 %shard_map.229 = (bf16[784,768]{1,0:T(8,128)(2,1)}, bf16[784,768]{1,0:T(8,128)(2,1)}, f32[9,96,256]{2,1,0:T(8,128)}, f32[48,256]{1,0:T(8,128)}) custom-call(bf16[784,768]{1,0:T(8,128)(2,1)} %refs_0_.1, bf16[784,768]{1,0:T(8,128)(2,1)} %refs_1_.1, bf16[3,96,192]{2,1,0:T(8,128)(2,1)} %refs_4_.3, bf16[192,96]{1,0:T(8,128)(2,1)} %refs_5_.1, ...), custom_call_target="tpu_custom_call" | custom-call | tf_op jit(solution)/shard_map/pallas_call | solution.py:649
  181.0 4.6 %shard_map.230 = (bf16[784,768]{1,0:T(8,128)(2,1)}, bf16[784,768]{1,0:T(8,128)(2,1)}, f32[3,96,192]{2,1,0:T(8,128)}, f32[192,96]{1,0:T(8,128)}, f32[96,768]{1,0:...) custom-call(bf16[784,768]{1,0:T(8,128)(2,1)} %get-tuple-element.28.r, ...), custom_call_target="tpu_custom_call" | custom-call | tf_op jit(solution)/shard_map/pallas_call | solution.py:700

commit v5 on v4

--- a/solution.py
+++ b/solution.py
@@ -13,6 +13,7 @@
 MESH = pl.DeviceIdType.MESH
 NCH = 9
 HALF = 48
+SPLIT = (0, 1)
 
 
 class Place:
@@ -26,21 +27,21 @@
         self.zup = (lax.rem(d + 2, 8), t)
         self.zdn = (lax.rem(d + 6, 8), t)
         self.zfar = (lax.rem(d + 4, 8), t)
-        self.zpair = self.z + 1 - 2 * lax.rem(self.z, 2)
+        self.along = (self.zup, self.zfar, self.zdn)
+        self.diag = (d + 1 - 2 * self.x, lax.rem(t + 2, 4))
 
     def zrel(self, s):
         return lax.rem(self.z + 4 - s, 4)
 
     def barrier(self):
         bar = pltpu.get_barrier_semaphore()
-        near = (self.core, self.ynb, self.xnb, self.zup, self.zdn, self.zfar)
+        near = (self.core, self.ynb, self.xnb, self.diag, self.zup, self.zdn, self.zfar)
         for dev in near:
             pl.semaphore_signal(bar, inc=1, device_id=dev, device_id_type=MESH)
         pl.semaphore_wait(bar, len(near))
 
 
 class Gather:
-    STAGES = 7
     COPIES = 11
 
     def __init__(self, p, own, w, ss, rs):
@@ -57,7 +58,7 @@
         lo, hi = pl.ds(0, HALF), pl.ds(HALF, HALF)
         line = lambda yy, cc, xx: w.at[n, yy, cc, :, xx]
         if k < 3:
-            return w.at[n, y, c, p.zrel(k), x], w.at[n, y, c, p.zrel(k + 1), x], p.zup
+            return w.at[n, y, c, p.z, x], w.at[n, y, c, p.zrel(k + 1), x], p.along[k]
         if k == 3:
             return line(y, c, x), line(y, c, 1 - x), p.xnb
         if k == 4:
@@ -74,22 +75,22 @@
             return line(1 - y, c, x), line(1 - y, 1 - c, x), p.core
         return line(1 - y, c, 1 - x), line(1 - y, 1 - c, 1 - x), p.core
 
-    def start(self, n, k):
-        src, _, dev = self.part(n, k)
-        self.copy(src, src, n, k, dev).start()
-
-    def pass_on(self, n, s):
+    def start(self, n, *ks):
+        for k in ks:
+            src, _, dev = self.part(n, k)
+            self.copy(src, src, n, k, dev).start()
+
+    def pieces(self, n, hops):
         p = self.p
-        at = self.w.at[n, p.y, p.c, p.zrel(s), p.x]
-        src = self.own.at[n] if s == 0 else at
-        if s < 3:
-            self.copy(src, at, n, s, p.zup).start()
-        for k, dev in ((3, p.xnb), (4, p.ynb), (5, p.core)):
-            self.copy(src, at, n, k, dev).start()
-
-    def arrive(self, n, k):
-        _, mine, dev = self.part(n, k)
-        self.copy(mine, mine, n, k, dev).wait_recv()
+        for s in hops:
+            at = self.w.at[n, p.y, p.c, p.zrel(s), p.x]
+            for k, dev in ((3, p.xnb), (4, p.ynb), (5, p.core)):
+                self.copy(self.own.at[n] if s == 0 else at, at, n, k, dev).start()
+
+    def arrive(self, n, *ks):
+        for k in ks:
+            _, mine, dev = self.part(n, k)
+            self.copy(mine, mine, n, k, dev).wait_recv()
 
     def finish(self, n):
         for k in range(self.COPIES):
@@ -97,50 +98,64 @@
             self.copy(src, src, n, k, dev).wait_send()
 
     def stage(self, n, s):
-        if s < 4:
-            if s > 0:
-                self.arrive(n, s - 1)
-            self.pass_on(n, s)
+        p = self.p
+        if s == 0:
+            at = self.w.at[n, p.y, p.c, p.z, p.x]
+            for k in range(3):
+                self.copy(self.own.at[n], at, n, k, p.along[k]).start()
+            if n in SPLIT:
+                self.pieces(n, (0,))
+        elif s == 1 and n in SPLIT:
+            for k in range(3):
+                self.arrive(n, k)
+                self.pieces(n, (k + 1,))
+        elif s == 1:
+            self.arrive(n, 0, 1, 2)
+            self.start(n, 3, 4, 5)
+        elif s == 2:
+            self.arrive(n, 3)
+            self.start(n, 6, 7)
+        elif s == 3:
+            self.arrive(n, 4)
+            self.start(n, 8, 9)
         elif s == 4:
-            self.arrive(n, 3)
-            self.start(n, 6)
-            self.start(n, 7)
-            self.arrive(n, 4)
-            self.start(n, 8)
-            self.start(n, 9)
-        elif s == 5:
-            self.arrive(n, 6)
-            self.arrive(n, 8)
+            self.arrive(n, 6, 8)
             self.start(n, 10)
         else:
-            for k in (5, 7, 9, 10):
-                self.arrive(n, k)
+            self.arrive(n, 5, 7, 9, 10)
 
 
 class Scatter:
-    STAGES = 7
     COPIES = 8
 
     def __init__(self, p, g, out, rc, rd, rl, rz, ss, rs):
         self.p, self.g, self.out, self.rc, self.rd, self.rl, self.rz = p, g, out, rc, rd, rl, rz
         self.ss, self.rs = ss, rs
 
+    def chunk(self, m):
+        return (m + 3) % NCH
+
+    def at(self, m, y, c, *rest):
+        n = self.chunk(m)
+        if n > 2:
+            return self.g.at[(n, y, c) + rest]
+        return self.rc.at[(pl.ds(2 * n, 2) if isinstance(y, slice) else 2 * n + y, c) + rest]
+
     def part(self, m, k):
-        p, g = self.p, self.g
-        n, o = self.chunk(m), m
+        p, every = self.p, slice(None)
         x, y, c = p.x, p.y, p.c
         lo, hi = pl.ds(0, HALF), pl.ds(HALF, HALF)
         if k == 0:
-            return g.at[n, :, 1 - c], self.rc.at[o], p.core
+            return self.at(m, every, 1 - c), self.rc.at[m], p.core
         if k == 1:
-            return g.at[n, 1 - y, c, :, 1 - x, lo], self.rd.at[o, 0], p.ynb
+            return self.at(m, 1 - y, c, every, 1 - x, lo), self.rd.at[m, 0], p.ynb
         if k == 2:
-            return g.at[n, 1 - y, c, :, 1 - x, hi], self.rd.at[o, 1], p.xnb
+            return self.at(m, 1 - y, c, every, 1 - x, hi), self.rd.at[m, 1], p.xnb
         if k == 3:
-            return g.at[n, y, c, :, 1 - x], self.rl.at[o, 0], p.xnb
+            return self.at(m, y, c, every, 1 - x), self.rl.at[m, 0], p.xnb
         if k == 4:
-            return g.at[n, 1 - y, c, :, x], self.rl.at[o, 1], p.ynb
-        return g.at[n, y, c, p.zrel(k - 4), x], self.rz.at[m, k - 5], p.zup
+            return self.at(m, 1 - y, c, every, x), self.rl.at[m, 1], p.ynb
+        return self.at(m, y, c, p.zrel(8 - k), x), self.rz.at[m, k - 5], p.along[k - 5]
 
     def copy(self, m, k):
         src, dst, dev = self.part(m, k)
@@ -148,58 +163,54 @@
             src, dst, send_sem=self.ss.at[m, k], recv_sem=self.rs.at[m, k], device_id=dev, device_id_type=MESH
         )
 
-    def start(self, m, k):
-        self.copy(m, k).start()
-
-    def arrive(self, m, k):
-        self.copy(m, k).wait_recv()
+    def start(self, m, *ks):
+        for k in ks:
+            self.copy(m, k).start()
+
+    def arrive(self, m, *ks):
+        for k in ks:
+            self.copy(m, k).wait_recv()
 
     def finish(self, m):
         for k in range(self.COPIES):
             self.copy(m, k).wait_send()
 
     def add(self, ref, *others):
-        total = ref[...].astype(F32)
-        for o in others:
-            total += o[...].astype(F32)
-        ref[...] = total.astype(BF16)
-
-    def chunk(self, m):
-        return lax.rem(m + 3, NCH)
+        if len(others) == 1:
+            ref[...] += others[0][...]
+        else:
+            ref[...] = sum((o[...].astype(F32) for o in others), ref[...].astype(F32)).astype(BF16)
 
     def stage(self, m, s):
-        p, g = self.p, self.g
-        n, o = self.chunk(m), m
+        p, every = self.p, slice(None)
         x, y, c = p.x, p.y, p.c
         lo, hi = pl.ds(0, HALF), pl.ds(HALF, HALF)
         if s == 0:
             self.start(m, 0)
         elif s == 1:
             self.arrive(m, 0)
-            self.add(g.at[n, 1 - y, c, :, 1 - x], self.rc.at[o, 1 - y, :, 1 - x])
-            self.start(m, 1)
-            self.start(m, 2)
-            self.add(g.at[n, y, c], self.rc.at[o, y])
-            self.add(g.at[n, 1 - y, c, :, x], self.rc.at[o, 1 - y, :, x])
+            self.add(self.at(m, 1 - y, c, every, 1 - x), self.rc.at[m, 1 - y, :, 1 - x])
+            self.start(m, 1, 2)
+            self.add(self.at(m, y, c), self.rc.at[m, y])
+            self.add(self.at(m, 1 - y, c, every, x), self.rc.at[m, 1 - y, :, x])
         elif s == 2:
             self.arrive(m, 1)
-            self.add(g.at[n, y, c, :, 1 - x, lo], self.rd.at[o, 0])
+            self.add(self.at(m, y, c, every, 1 - x, lo), self.rd.at[m, 0])
             self.start(m, 3)
+        elif s == 3:
             self.arrive(m, 2)
-            self.add(g.at[n, 1 - y, c, :, x, hi], self.rd.at[o, 1])
+            self.add(self.at(m, 1 - y, c, every, x, hi), self.rd.at[m, 1])
             self.start(m, 4)
-        elif s == 3:
-            self.arrive(m, 3)
-            self.arrive(m, 4)
-            self.add(g.at[n, y, c, :, x], self.rl.at[o, 0], self.rl.at[o, 1])
-            self.start(m, 5)
-        elif s < 6:
-            self.arrive(m, s + 1)
-            self.add(g.at[n, y, c, p.zrel(s - 2), x], self.rz.at[m, s - 4])
-            self.start(m, s + 2)
+        elif s == 4:
+            self.arrive(m, 3, 4)
+            self.add(self.at(m, y, c, every, x), self.rl.at[m, 0], self.rl.at[m, 1])
+            self.start(m, 5, 6, 7)
         else:
-            self.arrive(m, 7)
-            self.out[n] = g[n, y, c, p.z, x].astype(F32) + self.rz[m, 2].astype(F32)
+            self.arrive(m, 5, 6, 7)
+            total = self.at(m, y, c, p.z, x)[...].astype(F32)
+            for k in range(3):
+                total += self.rz[m, k].astype(F32)
+            self.out[self.chunk(m)] = total
 
 
 WSHAPE = (NCH, 2, 2, 4, 2, 96, 256)
@@ -275,14 +286,17 @@
     def put(self, n, y, c, value):
         self.w[n, y, c] = value.astype(BF16).reshape(4, 2, 96, 256)
 
-    def pack(self):
+    def pack(self, which):
         outt = self.wout[...].astype(F32).T
         q, k, v = (self.qkv[a].astype(F32) for a in range(3))
-        for j in range(3):
-            cols, wide = slice(64 * j, 64 * j + 64), slice(256 * j, 256 * j + 256)
+        for j in which:
+            cols = slice(64 * j, 64 * j + 64)
             self.own[j] = jnp.concatenate([a[:, cols] for a in (q, v, k, outt)], axis=1).astype(BF16)
-            self.own[3 + 2 * j] = self.up[:, wide]
-            self.own[4 + 2 * j] = self.down[:, wide]
+            if j > 0:
+                for i in (0, j) if j == 1 else (j,):
+                    wide = slice(256 * i, 256 * i + 256)
+                    self.own[3 + 2 * i] = self.up[:, wide]
+                    self.own[4 + 2 * i] = self.down[:, wide]
 
     def prepare(self, t):
         for k in range(12):
@@ -305,14 +319,14 @@
         self.mq[...] = jnp.where(slot, (same - 1.0) * BIG, 0.0).astype(BF16)
         self.mk[...] = jnp.where(slot, same, jnp.where((lane >= 68) & (lane < 71), 1.0, 0.0)).astype(BF16)
 
-    def norm1(self):
+    def norm1(self, half):
         def step(i, _):
             r = rows_of(i)
             scaled, _ = standard(self.tok[r, :].astype(F32))
             self.n1[r, :] = (scaled * self.vec[0:1, :] + self.vec[1:2, :]).astype(BF16)
             return 0
 
-        lax.fori_loop(0, ROWS // STEP, step, 0)
+        lax.fori_loop(4 * half, 4 + 3 * half, step, 0)
 
     def attend(self, i):
         j, y = lax.div(i, 2), lax.rem(i, 2)
@@ -372,7 +386,7 @@
         j, y = lax.div(i, 2), lax.rem(i, 2)
         nb, nc = 3 + 2 * j, 4 + 2 * j
         sums = [0.0, 0.0]
-        for r0, n in PARTS:
+        for half, (r0, n) in enumerate(PARTS):
             r = pl.ds(r0, n)
             for c in range(2):
                 cols = slice(c * 256, c * 256 + 256)
@@ -389,13 +403,13 @@
             self.gn[r, :] += nt(self.gp[r, 0:256], self.mat(nb, y, 0)) + nt(
                 self.gp[r, 256:512], self.mat(nb, y, 1)
             )
-        pause(0)
+            pause(half)
         for c in range(2):
             cols = slice(c * 256, c * 256 + 256)
             self.hs[12 + i * 2 + c] = jnp.sum(sums[c], axis=0, keepdims=True)
             self.put(nc, y, c, tn(self.cot[...], self.act[:, cols]))
             self.put(nb, y, c, tn(self.n2[...], self.gp[:, cols]))
-        pause(1)
+        pause(2)
 
     def residual_back(self):
         self.vs[...] = jnp.zeros(self.vs.shape, F32)
@@ -430,35 +444,41 @@
             moved = pltpu.roll(wide, 64, 1).astype(BF16) if c == 0 else low
             none = jnp.zeros((), BF16)
             extra = jnp.where(lane == 0, d1, jnp.where(lane == 1, d2, jnp.where(lane == 2, d3, none)))
-            self.da[...] = jnp.where(left, extra, moved)
+            self.act[:, 0:128] = jnp.where(left, extra, moved)
             dv = dk = 0.0
             for r0, n in PARTS:
                 r = pl.ds(r0, n)
-                q, d = self.qa[h, r, :], self.da[r, :]
+                q, d = self.qa[h, r, :], self.act[r, 0:128]
                 p = jnp.exp2(nt(q, self.ka[h]) * CS)
                 ds = (p * nt(d, self.va[h])).astype(BF16)
                 dv += tn(p.astype(BF16), d)
                 dk += tn(ds, q)
-                self.dq[c, r, 0:128] = (nn(ds, self.ka[h]) * 0.125).astype(BF16)
-            self.dq[c, :, 0:128] = jnp.where(left, self.dq[c, :, 0:128], dv.astype(BF16))
-            self.dq[c, :, 128:256] = jnp.where(left, (dk * 0.125).astype(BF16), none)
-            sums = jnp.sum(self.dq[c].astype(F32).reshape(ROWS // 8, 8, 256), axis=0)
+                self.acc[r, 0:128] = nn(ds, self.ka[h])
+            self.qa[h] = jnp.where(left, self.acc[:, 0:128] * 0.125, dv).astype(BF16)
+            self.ka[h] = jnp.where(left, (dk * 0.125).astype(BF16), none)
+            sums = jnp.sum(self.mixed_grad(h).astype(F32).reshape(ROWS // 8, 8, 256), axis=0)
             self.hs[h] = jnp.sum(sums, axis=0, keepdims=True)
             pause(c)
-        for r0, n in PARTS:
-            r = pl.ds(r0, n)
-            self.gn[r, :] += nt(self.dq[0, r, :], self.mat(j, y, 0)) + nt(
-                self.dq[1, r, :], self.mat(j, y, 1)
-            )
         outg = tn(self.gb[...], self.att[j, y])
         first = lax.broadcasted_iota(jnp.int32, (DM, 128), 1) < 64
         for c in range(2):
-            g = tn(self.n1[...], self.dq[c])
+            g = tn(self.n1[...], self.mixed_grad(i * 2 + c))
             mine = pltpu.roll(outg, 64, 1) if c == 0 else outg
-            self.put(j, y, c, jnp.concatenate([g[:, :128], jnp.where(first, g[:, 128:], mine)], axis=1))
+            whole = jnp.concatenate([g[:, :128], jnp.where(first, g[:, 128:], mine)], axis=1)
+            self.rc[i, c] = whole.astype(BF16).reshape(4, 2, 96, 256)
         pause(2)
 
-    def token_back(self):
+    def mixed_grad(self, h, r=slice(None)):
+        return jnp.concatenate([self.qa[h, r, :], self.ka[h, r, :]], axis=1)
+
+    def mixed_back(self, j):
+        for r0, n in PARTS:
+            r = pl.ds(r0, n)
+            self.gn[r, :] += sum(
+                nt(self.mixed_grad(4 * j + 2 * y + c, r), self.mat(j, y, c)) for y in range(2) for c in range(2)
+            )
+
+    def token_back(self, half):
         def step(i, _):
             r = rows_of(i)
             scaled, inverse = standard(self.tok[r, :].astype(F32))
@@ -469,7 +489,7 @@
             self.vs[1] += fold(g)
             return 0
 
-        lax.fori_loop(0, ROWS // STEP, step, 0)
+        lax.fori_loop(4 * half, 4 + 3 * half, step, 0)
 
     def collect(self):
         for h in range(24):
@@ -499,8 +519,6 @@
         mk=pltpu.VMEM((ROWS, 128), BF16),
         act=pltpu.VMEM((ROWS, 512), BF16),
         gp=pltpu.VMEM((ROWS, 512), BF16),
-        da=pltpu.VMEM((ROWS, 128), BF16),
-        dq=pltpu.VMEM((2, ROWS, 256), BF16),
         vs=pltpu.VMEM((6, 8, DM), F32),
         hs=pltpu.VMEM((24, 1, 256), F32),
         own=pltpu.VMEM((NCH, 96, 256), BF16),
@@ -513,49 +531,98 @@
 NAMES_OUT = ("out", "gtok", "gsh", "vsum")
 
 
-def slots_of(u):
-    late = u - 7
-    early_ok = (u >= 0) & (u <= 5)
-    late_ok = (late >= 0) & (late <= 4) & (lax.rem(jnp.maximum(late, 0), 2) == 0)
-    return jnp.where(early_ok, u, 6 + lax.div(jnp.maximum(late, 0), 2)), early_ok | late_ok
-
-
-def gather_slot(gather, t):
-    for s in range(gather.STAGES):
-        n = t - s
-        if isinstance(t, int):
-            if 0 <= n < NCH:
-                gather.stage(n, s)
-        else:
-            pl.when((n >= 0) & (n < NCH))(functools.partial(gather.stage, n, s))
-
-
-def scatter_slot(scatter, t):
-    for s in range(scatter.STAGES):
-        m, ok = slots_of(t - s)
-        pl.when(ok)(functools.partial(scatter.stage, m, s))
+PLAN = {
+    "s0": ((0, 0, 0),),
+    "s1": ((0, 1, 0),),
+    "s2": ((0, 2, 0), (0, 3, 0),),
+    "s3": ((0, 4, 0), (0, 5, 0), (0, 0, 1), (0, 1, 1), (0, 0, 2), (0, 0, 3), (0, 2, 1), (0, 1, 2), (0, 1, 3), (0, 0, 4), (0, 3, 1), (0, 0, 5),),
+    ("a", 0, 0): ((0, 2, 2), (0, 2, 3), (0, 4, 1),),
+    ("a", 1, 0): ((0, 1, 4), (0, 5, 1), (0, 1, 5),),
+    ("a", 2, 0): ((0, 2, 4), (0, 3, 2), (0, 3, 3), (0, 6, 0),),
+    ("a", 3, 0): ((0, 2, 5), (0, 7, 0),),
+    ("a", 4, 0): ((0, 4, 2), (0, 4, 3), (0, 6, 1),),
+    ("a", 5, 0): ((0, 3, 4), (0, 5, 2), (0, 5, 3),),
+    "p": ((0, 3, 5), (0, 4, 4), (0, 7, 1), (0, 8, 0), (0, 4, 5),),
+    ("f", 0, 0): ((0, 6, 2), (0, 6, 3),),
+    ("f", 0, 1): ((0, 5, 4),),
+    ("f", 0, 2): ((0, 5, 5),),
+    ("f", 1, 0): ((0, 8, 1),),
+    ("f", 1, 1): ((0, 7, 2), (0, 7, 3),),
+    ("f", 1, 2): ((0, 6, 4), (1, 0, 0), (1, 1, 0), (0, 6, 5),),
+    ("f", 2, 0): ((1, 0, 1),),
+    ("f", 2, 1): ((0, 8, 2), (0, 8, 3), (1, 1, 1),),
+    ("f", 2, 2): ((0, 7, 4),),
+    ("f", 3, 0): ((0, 7, 5), (1, 0, 2), (1, 0, 3),),
+    ("f", 3, 1): ((0, 8, 4),),
+    ("f", 3, 2): ((0, 8, 5), (1, 1, 2), (1, 1, 3), (1, 2, 0), (1, 3, 0),),
+    ("f", 4, 1): ((1, 2, 1),),
+    ("f", 4, 2): ((1, 0, 4), (1, 3, 1),),
+    ("f", 5, 1): ((1, 1, 4),),
+    ("f", 5, 2): ((1, 2, 2), (1, 2, 3), (1, 4, 0), (1, 5, 0),),
+    "q": ((1, 0, 5), (1, 3, 2), (1, 3, 3), (1, 4, 1), (1, 5, 1),),
+    ("b", 0, 0): ((1, 1, 5), (1, 2, 4),),
+    ("b", 0, 2): ((1, 3, 4),),
+    ("b", 1, 0): ((1, 2, 5), (1, 4, 2), (1, 4, 3),),
+    ("b", 1, 1): ((1, 5, 2), (1, 5, 3),),
+    ("b", 1, 2): ((1, 3, 5), (1, 6, 0),),
+    ("b", 2, 0): ((1, 4, 4), (1, 6, 1),),
+    ("b", 2, 2): ((1, 5, 4),),
+    ("b", 3, 0): ((1, 4, 5), (1, 6, 2), (1, 6, 3),),
+    ("b", 3, 2): ((1, 5, 5), (1, 7, 0),),
+    ("b", 4, 0): ((1, 6, 4), (1, 7, 1),),
+    ("b", 4, 2): ((1, 7, 2), (1, 7, 3),),
+    ("b", 5, 0): ((1, 6, 5),),
+    ("b", 5, 2): ((1, 8, 0), (1, 7, 4),),
+    ("u", 1): ((1, 8, 1),),
+    ("t", 1): ((1, 7, 5), (1, 8, 2), (1, 8, 3),),
+    "end": ((2, 0, 0), (2, 0, 1), (1, 8, 4), (2, 0, 2), (1, 8, 5), (2, 0, 3),),
+}
 
 
 class Totals:
     def __init__(self, p, value, vr, ss, rs):
         self.p, self.value, self.vr, self.ss, self.rs = p, value, vr, ss, rs
-        z1 = (lax.rem(p.zpair * 2 + p.x, 8), lax.axis_index("tensor"))
-        self.devs = (p.core, p.ynb, p.xnb, z1, p.zfar)
-
-    def copy(self, k):
-        src = self.vr.at[0, k]
+        self.mine = (1 + 2 * p.y + p.x, 5 + p.z)
+        self.to = (p.core, p.xnb, p.ynb, p.diag) + p.along
+        x, y = p.x, p.y
+        self.there = (0, 1 + 2 * y + 1 - x, 1 + 2 * (1 - y) + x, 1 + 2 * (1 - y) + 1 - x) + tuple(
+            5 + p.zrel(s) for s in (1, 2, 3)
+        )
+
+    def copy(self, k, src, dst):
         return pltpu.make_async_remote_copy(
-            src, self.vr.at[1, k], send_sem=self.ss.at[k], recv_sem=self.rs.at[k],
-            device_id=self.devs[k], device_id_type=MESH,
+            src, dst, send_sem=self.ss.at[k], recv_sem=self.rs.at[k], device_id=self.to[k], device_id_type=MESH
         )
 
-    def start(self, k, total):
-        self.vr[0, k] = total
-        self.copy(k).start()
-
-    def end(self, k):
-        self.copy(k).wait_recv()
-        return self.vr[0, k] + self.vr[1, k]
+    def arrive(self, *ks):
+        for k in ks:
+            slot = self.vr.at[self.there[k]]
+            self.copy(k, slot, slot).wait_recv()
+
+    def send(self, *ks):
+        slot = self.vr.at[self.mine[0] if ks[0] < 4 else self.mine[1]]
+        for k in ks:
+            self.copy(k, slot, slot).start()
+
+    def finish(self, _):
+        for k in range(1, 7):
+            self.copy(k, self.vr.at[0], self.vr.at[0]).wait_send()
+
+    def stage(self, _, s):
+        if s == 0:
+            self.copy(0, self.value, self.vr.at[0]).start()
+        elif s == 1:
+            self.arrive(0)
+            self.vr[self.mine[0]] = self.value[...] + self.vr[0]
+            self.send(1, 2, 3)
+        elif s == 2:
+            self.arrive(1, 2, 3)
+            self.vr[self.mine[1]] = (self.vr[1] + self.vr[2]) + (self.vr[3] + self.vr[4])
+            self.send(4, 5, 6)
+        else:
+            self.arrive(4, 5, 6)
+            self.copy(0, self.value, self.value).wait_send()
+            self.value[...] = (self.vr[5] + self.vr[6]) + (self.vr[7] + self.vr[8])
 
 
 def mega_kernel(names, *refs):
@@ -567,61 +634,66 @@
     scatter = Scatter(p, r["w"], r["gsh"], r["rc"], r["rd"], r["rl"], r["rz"], r["sss"], r["srs"])
     totals = Totals(p, r["vsum"], r["vr"], r["vss"], r["vrs"])
 
-    layer.pack()
+    engines = (gather, scatter, totals)
+
+    def at(site):
+        for e, n, s in PLAN.get(site, ()):
+            engines[e].stage(n, s)
+
+    def within(kind, i, k=0):
+        for turn in range(6):
+            if (kind, turn, k) in PLAN:
+                pl.when(i == turn)(functools.partial(at, (kind, turn, k)))
+
+    def loop(count, body):
+        lax.fori_loop(0, count, lambda i, c: (body(i), c)[1], 0)
+
+    layer.pack((0,))
+    at("s0")
+    layer.pack((1, 2))
     for n in range(NCH):
         r["w"][n, p.y, p.c, p.z, p.x] = r["own"][n]
-    gather_slot(gather, 0)
     layer.prepare(lax.axis_index("tensor"))
     layer.masks()
-    gather_slot(gather, 1)
-    layer.norm1()
-    lax.fori_loop(2, 6, lambda t, c: (gather_slot(gather, t), c)[1], 0)
-
-    def attend(i, _):
-        pl.when(lax.rem(i, 2) == 0)(lambda: gather_slot(gather, 6 + lax.div(i, 2)))
+    at("s1")
+    layer.norm1(0)
+    at("s2")
+    layer.norm1(1)
+    at("s3")
+
+    def attend(i):
         layer.attend(i)
-        return 0
-
-    lax.fori_loop(0, 6, attend, 0)
-    gather_slot(gather, jnp.int32(9))
+        within("a", i)
+
+    loop(6, attend)
     layer.project()
-    gather_slot(gather, jnp.int32(10))
-
-    def feed(i, _):
+    at("p")
+
+    def feed(i):
         @pl.when(lax.rem(i, 2) == 0)
         def _():
             gather.finish(3 + i)
             gather.finish(4 + i)
 
-        layer.feed(i, lambda k: None)
-        gather_slot(gather, 11 + i)
-        scatter_slot(scatter, i - 1)
-        return 0
-
-    lax.fori_loop(0, 6, feed, 0)
+        layer.feed(i, functools.partial(within, "f", i))
+
+    loop(6, feed)
     layer.residual_back()
-    scatter_slot(scatter, jnp.int32(5))
+    at("q")
+    loop(6, lambda i: layer.attend_back(i, functools.partial(within, "b", i)))
+    for j in range(3):
+        layer.mixed_back(j)
+        at(("u", j))
+    for half in range(2):
+        layer.token_back(half)
+        at(("t", half))
+    layer.collect()
+    at("end")
     for n in range(3):
         gather.finish(n)
-
-    def back(i, _):
-        layer.attend_back(i, lambda k: None)
-        scatter_slot(scatter, 6 + i)
-        return 0
-
-    lax.fori_loop(0, 6, back, 0)
-    layer.token_back()
-    layer.collect()
-    value = r["vsum"][...]
-    scatter_slot(scatter, jnp.int32(12))
-    for k in range(5):
-        totals.start(k, value)
-        scatter_slot(scatter, jnp.int32(13 + k))
-        value = totals.end(k)
-    r["vsum"][...] = value
-    lax.fori_loop(0, NCH, lambda m, c: (scatter.finish(m), c)[1], 0)
-    for k in range(5):
-        totals.copy(k).wait_send()
+    for m in range(NCH):
+        scatter.finish(m)
+    totals.finish(0)
 
 
 def mega_scratch():
@@ -631,13 +703,13 @@
         rd=pltpu.VMEM((NCH, 2, 4, HALF, 256), BF16),
         rl=pltpu.VMEM((NCH, 2, 4, 96, 256), BF16),
         rz=pltpu.VMEM((NCH, 3, 96, 256), BF16),
-        vr=pltpu.VMEM((2, 5, 48, 256), F32),
+        vr=pltpu.VMEM((9, 48, 256), F32),
         gss=pltpu.SemaphoreType.DMA((NCH, Gather.COPIES)),
         grs=pltpu.SemaphoreType.DMA((NCH, Gather.COPIES)),
         sss=pltpu.SemaphoreType.DMA((NCH, Scatter.COPIES)),
         srs=pltpu.SemaphoreType.DMA((NCH, Scatter.COPIES)),
-        vss=pltpu.SemaphoreType.DMA((5,)),
-        vrs=pltpu.SemaphoreType.DMA((5,)),
+        vss=pltpu.SemaphoreType.DMA((7,)),
+        vrs=pltpu.SemaphoreType.DMA((7,)),
     )
 
 

time: 186 us -> 175 us (0.941)
  Pallas kernels: 184 us -> 173 us
    pallas_call x1, Pallas kernels: 180 us -> 169 us  [mega_call(): pl.pallas_call(functools.partial(mega_kernel, names), out_shape=(shape((R...]
where the time goes in v5:
time: 175 us
  Pallas kernels  173 us (99%)
    pallas_call x1, Pallas kernels, mega_call(): pl.pallas_call(functools.partial(mega_kernel, names), out_shape=(shape((R...  169 us
    pallas_call x1, Pallas kernels, tail_call(): pl.pallas_call(functools.partial(tail_kernel, ins + outs), out_shape=[sha...  4.63 us

profile of v5, /device:TPU:0, one launch (start us, length us, event | category | flops | bytes accessed | tf_op | source)
XLA Modules:
  0.0 174.7 jit_solution(6568137086649227910)
XLA Ops:
  1.3 168.6 %shard_map.229 = (bf16[784,768]{1,0:T(8,128)(2,1)}, bf16[784,768]{1,0:T(8,128)(2,1)}, f32[9,96,256]{2,1,0:T(8,128)}, f32[48,256]{1,0:T(8,128)}) custom-call(bf16[784,768]{1,0:T(8,128)(2,1)} %refs_0_.1, bf16[784,768]{1,0:T(8,128)(2,1)} %refs_1_.1, bf16[3,96,192]{2,1,0:T(8,128)(2,1)} %refs_4_.3, bf16[192,96]{1,0:T(8,128)(2,1)} %refs_5_.1, ...), custom_call_target="tpu_custom_call" | custom-call | tf_op jit(solution)/shard_map/pallas_call | solution.py:721
  169.9 4.6 %shard_map.230 = (bf16[784,768]{1,0:T(8,128)(2,1)}, bf16[784,768]{1,0:T(8,128)(2,1)}, f32[3,96,192]{2,1,0:T(8,128)}, f32[192,96]{1,0:T(8,128)}, f32[96,768]{1,0:...) custom-call(bf16[784,768]{1,0:T(8,128)(2,1)} %get-tuple-element.28.r, ...), custom_call_target="tpu_custom_call" | custom-call | tf_op jit(solution)/shard_map/pallas_call | solution.py:772

commit v6 on v5

--- a/solution.py
+++ b/solution.py
@@ -42,7 +42,7 @@
 
 
 class Gather:
-    COPIES = 11
+    COPIES = 13
 
     def __init__(self, p, own, w, ss, rs):
         self.p, self.own, self.w, self.ss, self.rs = p, own, w, ss, rs
@@ -59,10 +59,12 @@
         line = lambda yy, cc, xx: w.at[n, yy, cc, :, xx]
         if k < 3:
             return w.at[n, y, c, p.z, x], w.at[n, y, c, p.zrel(k + 1), x], p.along[k]
-        if k == 3:
-            return line(y, c, x), line(y, c, 1 - x), p.xnb
-        if k == 4:
-            return line(y, c, x), line(1 - y, c, x), p.ynb
+        if k in (3, 11):
+            rows = lo if k == 3 else hi
+            return w.at[n, y, c, :, x, rows], w.at[n, y, c, :, 1 - x, rows], p.xnb
+        if k in (4, 12):
+            rows = hi if k == 4 else lo
+            return w.at[n, y, c, :, x, rows], w.at[n, 1 - y, c, :, x, rows], p.ynb
         if k == 5:
             return line(y, c, x), line(y, 1 - c, x), p.core
         if k == 6:
@@ -82,10 +84,11 @@
 
     def pieces(self, n, hops):
         p = self.p
+        lo, hi, both = pl.ds(0, HALF), pl.ds(HALF, HALF), pl.ds(0, 2 * HALF)
         for s in hops:
-            at = self.w.at[n, p.y, p.c, p.zrel(s), p.x]
-            for k, dev in ((3, p.xnb), (4, p.ynb), (5, p.core)):
-                self.copy(self.own.at[n] if s == 0 else at, at, n, k, dev).start()
+            for k, rows, dev in ((3, lo, p.xnb), (4, hi, p.ynb), (11, hi, p.xnb), (12, lo, p.ynb), (5, both, p.core)):
+                at = self.w.at[n, p.y, p.c, p.zrel(s), p.x, rows]
+                self.copy(self.own.at[n, rows] if s == 0 else at, at, n, k, dev).start()
 
     def arrive(self, n, *ks):
         for k in ks:
@@ -111,14 +114,17 @@
                 self.pieces(n, (k + 1,))
         elif s == 1:
             self.arrive(n, 0, 1, 2)
-            self.start(n, 3, 4, 5)
+            self.start(n, 3, 4, 11, 12, 5)
         elif s == 2:
             self.arrive(n, 3)
-            self.start(n, 6, 7)
+            self.start(n, 6)
         elif s == 3:
             self.arrive(n, 4)
-            self.start(n, 8, 9)
+            self.start(n, 8)
         elif s == 4:
+            self.arrive(n, 11, 12)
+            self.start(n, 7, 9)
+        elif s == 5:
             self.arrive(n, 6, 8)
             self.start(n, 10)
         else:
@@ -126,7 +132,7 @@
 
 
 class Scatter:
-    COPIES = 8
+    COPIES = 10
 
     def __init__(self, p, g, out, rc, rd, rl, rz, ss, rs):
         self.p, self.g, self.out, self.rc, self.rd, self.rl, self.rz = p, g, out, rc, rd, rl, rz
@@ -151,10 +157,12 @@
             return self.at(m, 1 - y, c, every, 1 - x, lo), self.rd.at[m, 0], p.ynb
         if k == 2:
             return self.at(m, 1 - y, c, every, 1 - x, hi), self.rd.at[m, 1], p.xnb
-        if k == 3:
-            return self.at(m, y, c, every, 1 - x), self.rl.at[m, 0], p.xnb
-        if k == 4:
-            return self.at(m, 1 - y, c, every, x), self.rl.at[m, 1], p.ynb
+        if k in (3, 8):
+            rows = lo if k == 3 else hi
+            return self.at(m, y, c, every, 1 - x, rows), self.rl.at[m, 0, :, rows], p.xnb
+        if k in (4, 9):
+            rows = hi if k == 4 else lo
+            return self.at(m, 1 - y, c, every, x, rows), self.rl.at[m, 1, :, rows], p.ynb
         return self.at(m, y, c, p.zrel(8 - k), x), self.rz.at[m, k - 5], p.along[k - 5]
 
     def copy(self, m, k):
@@ -193,6 +201,7 @@
             self.start(m, 1, 2)
             self.add(self.at(m, y, c), self.rc.at[m, y])
             self.add(self.at(m, 1 - y, c, every, x), self.rc.at[m, 1 - y, :, x])
+            self.start(m, 8, 9)
         elif s == 2:
             self.arrive(m, 1)
             self.add(self.at(m, y, c, every, 1 - x, lo), self.rd.at[m, 0])
@@ -202,7 +211,7 @@
             self.add(self.at(m, 1 - y, c, every, x, hi), self.rd.at[m, 1])
             self.start(m, 4)
         elif s == 4:
-            self.arrive(m, 3, 4)
+            self.arrive(m, 3, 4, 8, 9)
             self.add(self.at(m, y, c, every, x), self.rl.at[m, 0], self.rl.at[m, 1])
             self.start(m, 5, 6, 7)
         else:
@@ -434,7 +443,13 @@
         j, y = lax.div(i, 2), lax.rem(i, 2)
         lane = lax.broadcasted_iota(jnp.int32, (ROWS, 128), 1)
         left = lane < 64
-        low = nn(self.gb[...], self.ot[j, y]).astype(BF16)
+
+        @pl.when(y == 0)
+        def _():
+            self.act[:, 256:512] = nn(self.gb[...], self.pair(self.ot, j)).astype(BF16)
+            self.acc[0:DM, 128:384] = tn(self.gb[...], self.pair(self.att, j))
+
+        low = self.act[:, pl.ds(pl.multiple_of(256 + 128 * y, 128), 128)]
         wide = low.astype(F32)
         product = wide * self.att[j, y].astype(F32)
         for c in range(2):
@@ -459,7 +474,7 @@
             sums = jnp.sum(self.mixed_grad(h).astype(F32).reshape(ROWS // 8, 8, 256), axis=0)
             self.hs[h] = jnp.sum(sums, axis=0, keepdims=True)
             pause(c)
-        outg = tn(self.gb[...], self.att[j, y])
+        outg = self.acc[0:DM, pl.ds(pl.multiple_of(128 + 128 * y, 128), 128)]
         first = lax.broadcasted_iota(jnp.int32, (DM, 128), 1) < 64
         for c in range(2):
             g = tn(self.n1[...], self.mixed_grad(i * 2 + c))
@@ -471,12 +486,12 @@
     def mixed_grad(self, h, r=slice(None)):
         return jnp.concatenate([self.qa[h, r, :], self.ka[h, r, :]], axis=1)
 
-    def mixed_back(self, j):
-        for r0, n in PARTS:
-            r = pl.ds(r0, n)
-            self.gn[r, :] += sum(
-                nt(self.mixed_grad(4 * j + 2 * y + c, r), self.mat(j, y, c)) for y in range(2) for c in range(2)
-            )
+    def mixed_back(self, j, half):
+        r0, n = PARTS[half]
+        r = pl.ds(r0, n)
+        self.gn[r, :] += sum(
+            nt(self.mixed_grad(4 * j + 2 * y + c, r), self.mat(j, y, c)) for y in range(2) for c in range(2)
+        )
 
     def token_back(self, half):
         def step(i, _):
@@ -491,19 +506,29 @@
 
         lax.fori_loop(4 * half, 4 + 3 * half, step, 0)
 
-    def collect(self):
-        for h in range(24):
-            self.vsum[h : h + 1, :] = self.hs[h]
-        for k in range(6):
+    def collect(self, group):
+        for h in range(12):
+            if group == 0:
+                self.vsum[h : h + 1, :] = self.hs[12 + h]
+            if group == 1:
+                self.vsum[24 + h : 25 + h, :] = self.hs[h]
+        for k, at in {0: ((2, 12), (3, 15), (4, 18), (5, 21)), 1: (), 2: ((0, 40), (1, 43))}[group]:
             row = jnp.sum(self.vs[k], axis=0, keepdims=True)
             for b in range(3):
-                self.vsum[24 + 3 * k + b : 25 + 3 * k + b, :] = row[:, 256 * b : 256 * b + 256]
-        self.vsum[42:48, :] = jnp.zeros((6, 256), F32)
+                self.vsum[at + b : at + b + 1, :] = row[:, 256 * b : 256 * b + 256]
+        if group:
+            lo, hi = ((36, 40), (46, 48))[group - 1]
+            self.vsum[lo:hi, :] = jnp.zeros((hi - lo, 256), F32)
 
 
 def layer_scratch():
     return dict(
         w=pltpu.VMEM(WSHAPE, BF16),
+        tok=pltpu.VMEM((ROWS, DM), BF16),
+        cot=pltpu.VMEM((ROWS, DM), BF16),
+        out=pltpu.VMEM((ROWS, DM), BF16),
+        gtok=pltpu.VMEM((ROWS, DM), BF16),
+        io=pltpu.SemaphoreType.DMA((5,)),
         n1=pltpu.VMEM((ROWS, DM), BF16),
         n2=pltpu.VMEM((ROWS, DM), BF16),
         gb=pltpu.VMEM((ROWS, DM), BF16),
@@ -527,59 +552,65 @@
     )
 
 
-NAMES_IN = ("tok", "cot", "qkv", "wout", "up", "down", "flat", "pat")
-NAMES_OUT = ("out", "gtok", "gsh", "vsum")
+NAMES_IN = ("tok_in", "cot_in", "qkv", "wout", "up", "down", "flat", "pat")
+NAMES_OUT = ("out_to", "gtok_to", "gsh", "vsum")
 
 
 PLAN = {
     "s0": ((0, 0, 0),),
-    "s1": ((0, 1, 0),),
-    "s2": ((0, 2, 0), (0, 3, 0),),
-    "s3": ((0, 4, 0), (0, 5, 0), (0, 0, 1), (0, 1, 1), (0, 0, 2), (0, 0, 3), (0, 2, 1), (0, 1, 2), (0, 1, 3), (0, 0, 4), (0, 3, 1), (0, 0, 5),),
-    ("a", 0, 0): ((0, 2, 2), (0, 2, 3), (0, 4, 1),),
-    ("a", 1, 0): ((0, 1, 4), (0, 5, 1), (0, 1, 5),),
-    ("a", 2, 0): ((0, 2, 4), (0, 3, 2), (0, 3, 3), (0, 6, 0),),
-    ("a", 3, 0): ((0, 2, 5), (0, 7, 0),),
-    ("a", 4, 0): ((0, 4, 2), (0, 4, 3), (0, 6, 1),),
-    ("a", 5, 0): ((0, 3, 4), (0, 5, 2), (0, 5, 3),),
-    "p": ((0, 3, 5), (0, 4, 4), (0, 7, 1), (0, 8, 0), (0, 4, 5),),
-    ("f", 0, 0): ((0, 6, 2), (0, 6, 3),),
-    ("f", 0, 1): ((0, 5, 4),),
-    ("f", 0, 2): ((0, 5, 5),),
-    ("f", 1, 0): ((0, 8, 1),),
+    "s2": ((0, 1, 0), (0, 2, 0),),
+    "s3": ((0, 3, 0), (0, 4, 0), (0, 0, 1), (0, 1, 1), (0, 0, 2), (0, 0, 3), (0, 0, 4), (0, 2, 1), (0, 1, 2), (0, 1, 3), (0, 1, 4), (0, 0, 5), (0, 3, 1), (0, 0, 6),),
+    ("a", 0, 0): ((0, 2, 2), (0, 2, 3), (0, 2, 4), (0, 4, 1), (0, 5, 0),),
+    ("a", 1, 0): ((0, 1, 5), (0, 3, 2), (0, 3, 3), (0, 1, 6),),
+    ("a", 2, 0): ((0, 2, 5), (0, 3, 4), (0, 5, 1), (0, 6, 0),),
+    ("a", 3, 0): ((0, 2, 6), (0, 4, 2), (0, 4, 3), (0, 7, 0),),
+    ("a", 4, 0): ((0, 3, 5), (0, 4, 4), (0, 6, 1),),
+    ("a", 5, 0): ((0, 3, 6), (0, 5, 2), (0, 5, 3), (0, 5, 4),),
+    "p": ((0, 4, 5), (0, 6, 2), (0, 6, 3), (0, 7, 1), (0, 8, 0), (0, 4, 6),),
+    ("f", 0, 0): ((0, 6, 4),),
+    ("f", 0, 1): ((0, 5, 5),),
+    ("f", 0, 2): ((0, 5, 6), (0, 6, 5),),
+    ("f", 1, 0): ((0, 6, 6), (0, 8, 1),),
     ("f", 1, 1): ((0, 7, 2), (0, 7, 3),),
-    ("f", 1, 2): ((0, 6, 4), (1, 0, 0), (1, 1, 0), (0, 6, 5),),
-    ("f", 2, 0): ((1, 0, 1),),
-    ("f", 2, 1): ((0, 8, 2), (0, 8, 3), (1, 1, 1),),
-    ("f", 2, 2): ((0, 7, 4),),
-    ("f", 3, 0): ((0, 7, 5), (1, 0, 2), (1, 0, 3),),
-    ("f", 3, 1): ((0, 8, 4),),
-    ("f", 3, 2): ((0, 8, 5), (1, 1, 2), (1, 1, 3), (1, 2, 0), (1, 3, 0),),
+    ("f", 1, 2): ((0, 7, 4), (1, 0, 0), (1, 1, 0),),
+    ("f", 2, 0): ((0, 8, 2), (0, 8, 3),),
+    ("f", 2, 2): ((0, 8, 4),),
+    ("f", 3, 0): ((0, 7, 5),),
+    ("f", 3, 1): ((0, 7, 6), (0, 8, 5),),
+    ("f", 3, 2): ((0, 8, 6), (1, 0, 1), (1, 1, 1), (1, 2, 0), (1, 3, 0),),
     ("f", 4, 1): ((1, 2, 1),),
-    ("f", 4, 2): ((1, 0, 4), (1, 3, 1),),
-    ("f", 5, 1): ((1, 1, 4),),
-    ("f", 5, 2): ((1, 2, 2), (1, 2, 3), (1, 4, 0), (1, 5, 0),),
-    "q": ((1, 0, 5), (1, 3, 2), (1, 3, 3), (1, 4, 1), (1, 5, 1),),
-    ("b", 0, 0): ((1, 1, 5), (1, 2, 4),),
-    ("b", 0, 2): ((1, 3, 4),),
-    ("b", 1, 0): ((1, 2, 5), (1, 4, 2), (1, 4, 3),),
-    ("b", 1, 1): ((1, 5, 2), (1, 5, 3),),
-    ("b", 1, 2): ((1, 3, 5), (1, 6, 0),),
-    ("b", 2, 0): ((1, 4, 4), (1, 6, 1),),
-    ("b", 2, 2): ((1, 5, 4),),
-    ("b", 3, 0): ((1, 4, 5), (1, 6, 2), (1, 6, 3),),
-    ("b", 3, 2): ((1, 5, 5), (1, 7, 0),),
-    ("b", 4, 0): ((1, 6, 4), (1, 7, 1),),
-    ("b", 4, 2): ((1, 7, 2), (1, 7, 3),),
-    ("b", 5, 0): ((1, 6, 5),),
-    ("b", 5, 2): ((1, 8, 0), (1, 7, 4),),
-    ("u", 1): ((1, 8, 1),),
+    ("f", 4, 2): ((1, 0, 2), (1, 0, 3), (1, 3, 1),),
+    ("f", 5, 1): ((1, 1, 2), (1, 1, 3),),
+    ("f", 5, 2): ((1, 4, 0), (1, 5, 0),),
+    "q": ((2, 0, 0), (1, 2, 2), (1, 2, 3), (1, 4, 1), (1, 5, 1),),
+    ("b", 0, 0): ((2, 0, 1), (1, 0, 4),),
+    ("b", 0, 1): ((1, 3, 2), (1, 3, 3),),
+    ("b", 1, 0): ((1, 1, 4),),
+    ("b", 1, 1): ((1, 0, 5), (1, 2, 4),),
+    ("b", 1, 2): ((1, 4, 2), (1, 4, 3), (1, 6, 0),),
+    ("b", 2, 0): ((1, 6, 1), (1, 1, 5),),
+    ("b", 2, 1): ((1, 5, 2), (1, 5, 3),),
+    ("b", 2, 2): ((2, 0, 2), (1, 2, 5),),
+    ("b", 3, 0): ((1, 3, 4),),
+    ("b", 3, 1): ((1, 4, 4), (2, 0, 3),),
+    ("b", 3, 2): ((1, 6, 2), (1, 6, 3), (1, 7, 0),),
+    ("b", 4, 0): ((1, 7, 1), (1, 3, 5),),
+    ("b", 4, 1): ((1, 5, 4),),
+    ("b", 4, 2): ((1, 4, 5), (1, 6, 4),),
+    ("b", 5, 0): ((1, 7, 2), (1, 7, 3),),
+    ("b", 5, 2): ((1, 5, 5), (1, 8, 0),),
+    ("u", 0): ((2, 1, 0),),
+    ("u", 1): ((1, 7, 4),),
+    ("u", 3): ((2, 1, 1), (1, 6, 5), (1, 8, 1),),
+    ("t", 0): ((2, 1, 2),),
     ("t", 1): ((1, 7, 5), (1, 8, 2), (1, 8, 3),),
-    "end": ((2, 0, 0), (2, 0, 1), (1, 8, 4), (2, 0, 2), (1, 8, 5), (2, 0, 3),),
+    "end": ((2, 2, 0), (2, 2, 1), (2, 1, 3), (1, 8, 4), (2, 2, 2), (1, 8, 5), (2, 2, 3),),
 }
 
 
 class Totals:
+    ROWS = (pl.ds(0, 24), pl.ds(24, 16), pl.ds(40, 8))
+
     def __init__(self, p, value, vr, ss, rs):
         self.p, self.value, self.vr, self.ss, self.rs = p, value, vr, ss, rs
         self.mine = (1 + 2 * p.y + p.x, 5 + p.z)
@@ -589,45 +620,63 @@
             5 + p.zrel(s) for s in (1, 2, 3)
         )
 
-    def copy(self, k, src, dst):
+    def copy(self, g, k, src, dst):
         return pltpu.make_async_remote_copy(
-            src, dst, send_sem=self.ss.at[k], recv_sem=self.rs.at[k], device_id=self.to[k], device_id_type=MESH
+            src, dst, send_sem=self.ss.at[g, k], recv_sem=self.rs.at[g, k], device_id=self.to[k], device_id_type=MESH
         )
 
-    def arrive(self, *ks):
+    def arrive(self, g, *ks):
         for k in ks:
-            slot = self.vr.at[self.there[k]]
-            self.copy(k, slot, slot).wait_recv()
-
-    def send(self, *ks):
-        slot = self.vr.at[self.mine[0] if ks[0] < 4 else self.mine[1]]
+            slot = self.vr.at[self.there[k], self.ROWS[g]]
+            self.copy(g, k, slot, slot).wait_recv()
+
+    def send(self, g, *ks):
+        slot = self.vr.at[self.mine[0] if ks[0] < 4 else self.mine[1], self.ROWS[g]]
         for k in ks:
-            self.copy(k, slot, slot).start()
-
-    def finish(self, _):
+            self.copy(g, k, slot, slot).start()
+
+    def finish(self, g):
+        slot = self.vr.at[0, self.ROWS[g]]
         for k in range(1, 7):
-            self.copy(k, self.vr.at[0], self.vr.at[0]).wait_send()
-
-    def stage(self, _, s):
+            self.copy(g, k, slot, slot).wait_send()
+
+    def stage(self, g, s):
+        rows, value = self.ROWS[g], self.value.at[self.ROWS[g]]
+        part = [self.vr.at[k, rows] for k in range(9)]
         if s == 0:
-            self.copy(0, self.value, self.vr.at[0]).start()
+            self.copy(g, 0, value, part[0]).start()
         elif s == 1:
-            self.arrive(0)
-            self.vr[self.mine[0]] = self.value[...] + self.vr[0]
-            self.send(1, 2, 3)
+            self.arrive(g, 0)
+            self.vr[self.mine[0], rows] = value[...] + part[0][...]
+            self.send(g, 1, 2, 3)
         elif s == 2:
-            self.arrive(1, 2, 3)
-            self.vr[self.mine[1]] = (self.vr[1] + self.vr[2]) + (self.vr[3] + self.vr[4])
-            self.send(4, 5, 6)
+            self.arrive(g, 1, 2, 3)
+            self.vr[self.mine[1], rows] = (part[1][...] + part[2][...]) + (part[3][...] + part[4][...])
+            self.send(g, 4, 5, 6)
         else:
-            self.arrive(4, 5, 6)
-            self.copy(0, self.value, self.value).wait_send()
-            self.value[...] = (self.vr[5] + self.vr[6]) + (self.vr[7] + self.vr[8])
+            self.arrive(g, 4, 5, 6)
+            self.copy(g, 0, value, value).wait_send()
+            value[...] = (part[5][...] + part[6][...]) + (part[7][...] + part[8][...])
 
 
 def mega_kernel(names, *refs):
     r = dict(zip(names, refs))
     layer = Layer(r)
+    cut = STEP * 4
+    moves = [
+        pltpu.make_async_copy(a, b, r["io"].at[k])
+        for k, (a, b) in enumerate(
+            (
+                (r["tok_in"], r["tok"]),
+                (r["cot_in"], r["cot"]),
+                (r["out"], r["out_to"]),
+                (r["gtok"].at[0:cut], r["gtok_to"].at[0:cut]),
+                (r["gtok"].at[cut:ROWS], r["gtok_to"].at[cut:ROWS]),
+            )
+        )
+    ]
+    moves[0].start()
+    moves[1].start()
     p = Place()
     p.barrier()
     gather = Gather(p, r["own"], r["w"], r["gss"], r["grs"])
@@ -656,6 +705,7 @@
     layer.prepare(lax.axis_index("tensor"))
     layer.masks()
     at("s1")
+    moves[0].wait()
     layer.norm1(0)
     at("s2")
     layer.norm1(1)
@@ -666,6 +716,7 @@
         within("a", i)
 
     loop(6, attend)
+    moves[1].wait()
     layer.project()
     at("p")
 
@@ -679,21 +730,28 @@
 
     loop(6, feed)
     layer.residual_back()
+    moves[2].start()
+    layer.collect(0)
     at("q")
     loop(6, lambda i: layer.attend_back(i, functools.partial(within, "b", i)))
-    for j in range(3):
-        layer.mixed_back(j)
-        at(("u", j))
+    layer.collect(1)
+    for k in range(6):
+        layer.mixed_back(k // 2, k % 2)
+        at(("u", k))
     for half in range(2):
         layer.token_back(half)
+        moves[3 + half].start()
         at(("t", half))
-    layer.collect()
+    layer.collect(2)
     at("end")
+    for move in moves[2:]:
+        move.wait()
     for n in range(3):
         gather.finish(n)
     for m in range(NCH):
         scatter.finish(m)
-    totals.finish(0)
+    for g in range(3):
+        totals.finish(g)
 
 
 def mega_scratch():
@@ -708,8 +766,8 @@
         grs=pltpu.SemaphoreType.DMA((NCH, Gather.COPIES)),
         sss=pltpu.SemaphoreType.DMA((NCH, Scatter.COPIES)),
         srs=pltpu.SemaphoreType.DMA((NCH, Scatter.COPIES)),
-        vss=pltpu.SemaphoreType.DMA((7,)),
-        vrs=pltpu.SemaphoreType.DMA((7,)),
+        vss=pltpu.SemaphoreType.DMA((3, 7)),
+        vrs=pltpu.SemaphoreType.DMA((3, 7)),
     )
 
 
@@ -726,8 +784,8 @@
             shape((NCH, 96, 256), F32),
             shape((48, 256), F32),
         ),
-        in_specs=[vm] * (len(NAMES_IN) - 1) + [pl.BlockSpec(memory_space=pltpu.SMEM)],
-        out_specs=(vm,) * len(NAMES_OUT),
+        in_specs=[pl.BlockSpec(memory_space=pl.ANY)] * 2 + [vm] * (len(NAMES_IN) - 3) + [pl.BlockSpec(memory_space=pltpu.SMEM)],
+        out_specs=(pl.BlockSpec(memory_space=pl.ANY),) * 2 + (vm,) * 2,
         scratch_shapes=list(scratch.values()),
         compiler_params=pltpu.CompilerParams(collective_id=0, has_side_effects=True, vmem_limit_bytes=62 << 20),
     )(*args)
@@ -746,16 +804,17 @@
         r["gdown"][:, 256 * j : 256 * j + 256] = g[4 + 2 * j]
         r["gout"][cols, :] = g[j, :, 128:256].T[64:128, :]
     v, gv = r["vsum"], r["gvec"]
-    for k, row in enumerate((0, 1, 2, 3, 6, 11)):
+    for row, at in ((0, 40), (1, 43), (2, 12), (3, 15), (6, 18), (11, 21)):
         for b in range(6):
-            gv[6 * row + b : 6 * row + b + 1, :] = v[24 + 3 * k + b // 2 : 25 + 3 * k + b // 2, 128 * (b % 2) : 128 * (b % 2) + 128]
+            k = at + b // 2
+            gv[6 * row + b : 6 * row + b + 1, :] = v[k : k + 1, 128 * (b % 2) : 128 * (b % 2) + 128]
     for half in range(2):
         for b in range(6):
-            two = [v[h : h + 1, 64 * half : 64 * half + 64] for h in (head_slot(2 * b), head_slot(2 * b + 1))]
+            two = [v[24 + h : 25 + h, 64 * half : 64 * half + 64] for h in (head_slot(2 * b), head_slot(2 * b + 1))]
             gv[24 + 6 * half + b : 25 + 6 * half + b, :] = jnp.concatenate(two, axis=1)
     for t in range(4):
         for b in range(6):
-            row = 12 + (b // 2) * 4 + t
+            row = (b // 2) * 4 + t
             gv[42 + 6 * t + b : 43 + 6 * t + b, :] = v[row : row + 1, 128 * (b % 2) : 128 * (b % 2) + 128]
     rate = r["rate"][0]
     for name in ("qkv", "wout", "up", "down", "vec"):

time: 175 us -> 166 us (0.949)
  Pallas kernels: 173 us -> 165 us
    pallas_call x1, Pallas kernels: 169 us -> 160 us  [mega_call(): pl.pallas_call(functools.partial(mega_kernel, names), out_shape=(shape((R...]
where the time goes in v6:
time: 166 us
  Pallas kernels  165 us (99%)
    pallas_call x1, Pallas kernels, mega_call(): pl.pallas_call(functools.partial(mega_kernel, names), out_shape=(shape((R...  160 us
    pallas_call x1, Pallas kernels, tail_call(): pl.pallas_call(functools.partial(tail_kernel, ins + outs), out_shape=[sha...  4.63 us

profile of v6, /device:TPU:0, one launch (start us, length us, event | category | flops | bytes accessed | tf_op | source)
XLA Modules:
  0.0 166.3 jit_solution(6787254747202231417)
XLA Ops:
  1.3 160.2 %shard_map.229 = (bf16[784,768]{1,0:T(8,128)(2,1)}, bf16[784,768]{1,0:T(8,128)(2,1)}, f32[9,96,256]{2,1,0:T(8,128)}, f32[48,256]{1,0:T(8,128)}) custom-call(bf16[784,768]{1,0:T(8,128)(2,1)} %refs_0_.1, bf16[784,768]{1,0:T(8,128)(2,1)} %refs_1_.1, bf16[3,96,192]{2,1,0:T(8,128)(2,1)} %refs_4_.3, bf16[192,96]{1,0:T(8,128)(2,1)} %refs_5_.1, ...), custom_call_target="tpu_custom_call" | custom-call | tf_op jit(solution)/shard_map/pallas_call | solution.py:779
  161.5 4.6 %shard_map.230 = (bf16[784,768]{1,0:T(8,128)(2,1)}, bf16[784,768]{1,0:T(8,128)(2,1)}, f32[3,96,192]{2,1,0:T(8,128)}, f32[192,96]{1,0:T(8,128)}, f32[96,768]{1,0:...) custom-call(bf16[784,768]{1,0:T(8,128)(2,1)} %get-tuple-element.28.r, ...), custom_call_target="tpu_custom_call" | custom-call | tf_op jit(solution)/shard_map/pallas_call | solution.py:831
